TPU v7x, 32 devices: a whole 2x2x4 slice. The times are simulated.
32 devices in a mesh: fsdp: 8 (over z, x), sub: 4 (over y, core).
Axes of the slice: x: 2, y: 2, z: 4, core: 2. Of those that a mesh axis runs over, the one named last changes fastest.
Arguments:
- rows: bfloat16 [4096, 960], P(('fsdp', 'sub')), may hold values from -6 to 6
- cotangent: bfloat16 [4096, 960], P(('fsdp', 'sub')), may hold values from -6 to 6
- lengths: int32 [64], P(('fsdp', 'sub')), may hold values from 1 to 64, as said below
- gains: bfloat16 [1920], P('fsdp'), may hold values from 0.5 to 1.5
- attn_weight: bfloat16 [2457600], P(('fsdp', 'sub')), as said below
- gate_weight: bfloat16 [2457600], P(('fsdp', 'sub')), may hold values from -0.1875 to 0.1875
- up_weight: bfloat16 [2457600], P(('fsdp', 'sub')), may hold values from -0.1875 to 0.1875
- down_weight: bfloat16 [2457600], P(('fsdp', 'sub')), may hold values from -0.125 to 0.125
Outputs:
- output: bfloat16 [4096, 960], P(('fsdp', 'sub'))
- input_grad: float32 [4096, 960], P(('fsdp', 'sub'))
- attn_grad: float32 [2457600], P(('fsdp', 'sub'))
- gate_grad: float32 [2457600], P(('fsdp', 'sub'))
- up_grad: float32 [2457600], P(('fsdp', 'sub'))
- down_grad: float32 [2457600], P(('fsdp', 'sub'))
- gain_grad: float32 [1920], P('fsdp')
Inputs may be any that keep to these rules, and one draw needn't show every extreme that they name: `lengths`: sequences of one device lie in its first slots in order; the rest are empty. Some sequence has exactly 64 tokens. `attn_weight`: its columns from 1600 on (the output projection's) have a larger scale than the others.
All inputs are finite; a program needn't handle non-finite values.
Results may differ from a plain program's by a relative error of at most 0.012.
Values may be sent and summed in bfloat16 or wider, within the bound.
No kernel may reach another device: no remote copies, remote signals or barrier semaphores. Data moves between devices by JAX's collectives and lax.ppermute only.
A program may use at most 256 MiB of HBM per device.

v0:
```python
import jax
import jax.numpy as jnp
from jax import lax
from jax.sharding import PartitionSpec as P

D = 960
KV = 5
HD = 64
FF = 2560
GROUP = 3


EPS = 1e-05
THETA = 100000.0
NEG = -1e30
piece_width = 64


def rope_tables(position, width):
    half = jnp.arange(width // 2, dtype=jnp.float32)
    inverse = jnp.exp(-(2.0 * half / width) * jnp.log(jnp.float32(THETA)))
    angle = position.astype(jnp.float32)[:, None] * inverse[None, :]
    cosine = jnp.concatenate([jnp.cos(angle), jnp.cos(angle)], axis=1)
    sine = jnp.concatenate([jnp.sin(angle), jnp.sin(angle)], axis=1)
    return (cosine, sine)


def rotate(values, cosine, sine):
    half = values.shape[-1] // 2
    turned = jnp.concatenate([-values[..., half:], values[..., :half]], axis=-1)
    return values * cosine + turned * sine


def unrotate(grads, cosine, sine):
    half = grads.shape[-1] // 2
    scaled = grads * sine
    return grads * cosine + jnp.concatenate([scaled[..., half:], -scaled[..., :half]], axis=-1)


def norm_forward(values):
    scale = lax.rsqrt(jnp.mean(values * values, axis=1, keepdims=True) + EPS)
    return (values * scale, scale)


def norm_backward(grad_in, normed, scale, gain):
    gain_term = jnp.sum(grad_in * normed, axis=0)
    inner = grad_in * gain[None, :]
    back = scale * (inner - normed * jnp.mean(inner * normed, axis=1, keepdims=True))
    return (back, gain_term)


def layout(block_lengths, count):
    slots = jnp.arange(count, dtype=jnp.int32)
    first = block_lengths[0]
    second = block_lengths[1]
    segment = (slots >= first).astype(jnp.int32) + (slots >= first + second).astype(jnp.int32)
    position = (
        slots - first * (segment >= 1).astype(jnp.int32) - second * (segment >= 2).astype(jnp.int32)
    )
    live = (segment < 2).astype(jnp.float32)[:, None]
    allowed = (segment[:, None] == segment[None, :]) & (slots[None, :] <= slots[:, None])
    return (position, live, allowed)


def masked_scores(queries, keys, allowed):
    scores = jnp.einsum(
        "qkgd,jkd->kgqj", queries, keys, preferred_element_type=jnp.float32
    ) * HD ** (-0.5)
    return jnp.where(allowed[None, None], scores, NEG)


def attend(projected, cosine, sine, allowed, count):
    kv_width = KV * HD
    queries = rotate(
        projected[:, :D].reshape(count, KV, GROUP, HD),
        cosine[:, None, None, :],
        sine[:, None, None, :],
    ).astype(jnp.bfloat16)
    keys = rotate(
        projected[:, D : D + kv_width].reshape(count, KV, HD), cosine[:, None, :], sine[:, None, :]
    ).astype(jnp.bfloat16)
    values = projected[:, D + kv_width :].reshape(count, KV, HD).astype(jnp.bfloat16)
    scores = masked_scores(queries, keys, allowed)
    top = jnp.max(scores, axis=-1, keepdims=True)
    expo = jnp.exp(scores - top)
    total = jnp.sum(expo, axis=-1, keepdims=True)
    logsum = top + jnp.log(total)
    weights = (expo / total).astype(jnp.bfloat16)
    attended = (
        jnp.einsum("kgqj,jkd->qkgd", weights, values, preferred_element_type=jnp.float32)
        .reshape(count, D)
        .astype(jnp.bfloat16)
    )
    return (queries, keys, values, logsum, attended)


def attend_back(grad_att, queries, keys, values, logsum, allowed, cosine, sine, count):
    kv_width = KV * HD
    probs = jnp.exp(masked_scores(queries, keys, allowed) - logsum)
    probs_b = probs.astype(jnp.bfloat16)
    value_grad = jnp.einsum("kgqj,qkgd->jkd", probs_b, grad_att, preferred_element_type=jnp.float32)
    prob_grad = jnp.einsum("qkgd,jkd->kgqj", grad_att, values, preferred_element_type=jnp.float32)
    delta = jnp.sum(probs * prob_grad, axis=-1, keepdims=True)
    score_grad = (probs * (prob_grad - delta) * HD ** (-0.5)).astype(jnp.bfloat16)
    query_grad = jnp.einsum("kgqj,jkd->qkgd", score_grad, keys, preferred_element_type=jnp.float32)
    key_grad = jnp.einsum("kgqj,qkgd->jkd", score_grad, queries, preferred_element_type=jnp.float32)
    query_grad = unrotate(query_grad, cosine[:, None, None, :], sine[:, None, None, :])
    key_grad = unrotate(key_grad, cosine[:, None, :], sine[:, None, :])
    return jnp.concatenate(
        [
            query_grad.reshape(count, D),
            key_grad.reshape(count, kv_width),
            value_grad.reshape(count, kv_width),
        ],
        axis=1,
    ).astype(jnp.bfloat16)


def collect(attn_flat, gate_flat, up_flat, down_flat):
    whole = (
        lax.all_gather(attn_flat, ("fsdp", "sub"), axis=0, tiled=True),
        lax.all_gather(gate_flat, ("fsdp", "sub"), axis=0, tiled=True),
        lax.all_gather(up_flat, ("fsdp", "sub"), axis=0, tiled=True),
        lax.all_gather(down_flat, ("fsdp", "sub"), axis=0, tiled=True),
    )
    return tuple((piece.reshape(D, FF) for piece in whole))


def flat_terms(pair_lists, count):
    results = []
    for pairs in pair_lists:
        blocks = [
            jnp.dot(left.T, right, preferred_element_type=jnp.float32) for left, right in pairs
        ]
        joined = blocks[0] if len(blocks) == 1 else jnp.concatenate(blocks, axis=1)
        results.append(joined.reshape(-1).reshape(count, piece_width))
    return jnp.concatenate(results, axis=1)


def split_owned(owned):
    return tuple(
        (
            owned[:, index * piece_width : (index + 1) * piece_width].reshape(-1)
            for index in range(4)
        )
    )


def spread(pair_lists):
    share = D * FF // (piece_width * lax.axis_size("fsdp") * lax.axis_size("sub"))
    owned = lax.psum_scatter(
        flat_terms(pair_lists, share * lax.axis_size(("fsdp", "sub"))),
        ("fsdp", "sub"),
        scatter_dimension=0,
        tiled=True,
    )
    return split_owned(owned)


def flat_path(
    rows32,
    cotangent,
    live,
    allowed,
    cosine,
    sine,
    gain_attn,
    gain_mlp,
    normed1,
    scale1,
    input1,
    flats,
):
    count = rows32.shape[0]
    q_width = D + 2 * KV * HD
    attn_mat, gate_mat, up_mat, down_mat = collect(flats[0], flats[1], flats[2], flats[3])
    projected = jnp.dot(input1, attn_mat[:, :q_width], preferred_element_type=jnp.float32)
    queries, keys, values, logsum, attended = attend(projected, cosine, sine, allowed, count)
    hidden1 = rows32 + jnp.dot(
        attended, attn_mat[:, q_width:].T, preferred_element_type=jnp.float32
    )
    normed2, scale2 = norm_forward(hidden1)
    input2 = (normed2 * gain_mlp[None, :]).astype(jnp.bfloat16)
    gate = jnp.dot(input2, gate_mat, preferred_element_type=jnp.float32)
    up = jnp.dot(input2, up_mat, preferred_element_type=jnp.float32)
    sigma = jax.nn.sigmoid(gate)
    active = gate * sigma
    hidden = (active * up).astype(jnp.bfloat16)
    result = hidden1 + jnp.dot(hidden, down_mat.T, preferred_element_type=jnp.float32)
    output = (live * result).astype(jnp.bfloat16)
    attn_back, gate_back, up_back, down_back = collect(flats[0], flats[1], flats[2], flats[3])
    grad_out = live * cotangent.astype(jnp.float32)
    grad_outb = grad_out.astype(jnp.bfloat16)
    grad_hidden = jnp.dot(grad_outb, down_back, preferred_element_type=jnp.float32)
    grad_gate = (grad_hidden * up * sigma * (1.0 + gate * (1.0 - sigma))).astype(jnp.bfloat16)
    grad_up = (grad_hidden * active).astype(jnp.bfloat16)
    grad_in2 = jnp.dot(grad_gate, gate_back.T, preferred_element_type=jnp.float32) + jnp.dot(
        grad_up, up_back.T, preferred_element_type=jnp.float32
    )
    back2, gain2_term = norm_backward(grad_in2, normed2, scale2, gain_mlp)
    grad_h1 = grad_out + back2
    grad_h1b = grad_h1.astype(jnp.bfloat16)
    grad_att = (
        jnp.dot(grad_h1b, attn_back[:, q_width:], preferred_element_type=jnp.float32)
        .astype(jnp.bfloat16)
        .reshape(count, KV, GROUP, HD)
    )
    proj_grad = attend_back(grad_att, queries, keys, values, logsum, allowed, cosine, sine, count)
    grad_in1 = jnp.dot(proj_grad, attn_back[:, :q_width].T, preferred_element_type=jnp.float32)
    back1, gain1_term = norm_backward(grad_in1, normed1, scale1, gain_attn)
    input_grad = grad_h1 + back1
    pair_lists = (
        ((input1, proj_grad), (grad_h1b, attended)),
        ((input2, grad_gate),),
        ((input2, grad_up),),
        ((grad_outb, hidden),),
    )
    owned = spread(pair_lists)
    return (output, input_grad, owned, gain1_term, gain2_term)


def body(rows, cotangent, lengths, gains, attn_weight, gate_weight, up_weight, down_weight):
    count = rows.shape[0]
    position, live, allowed = layout(lengths, count)
    cosine, sine = rope_tables(position, HD)
    full_gains = lax.all_gather(gains, "fsdp", axis=0, tiled=True).astype(jnp.float32)
    gain_attn = full_gains[:D]
    gain_mlp = full_gains[D:]
    rows32 = rows.astype(jnp.float32)
    normed1, scale1 = norm_forward(rows32)
    input1 = (normed1 * gain_attn[None, :]).astype(jnp.bfloat16)
    flats = (attn_weight, gate_weight, up_weight, down_weight)
    output, input_grad, owned, gain1_term, gain2_term = flat_path(
        rows32,
        cotangent,
        live,
        allowed,
        cosine,
        sine,
        gain_attn,
        gain_mlp,
        normed1,
        scale1,
        input1,
        flats,
    )
    gain_total = lax.psum(jnp.concatenate([gain1_term, gain2_term]), ("fsdp", "sub"))
    share = gains.shape[0]
    gain_grad = lax.dynamic_slice_in_dim(gain_total, lax.axis_index("fsdp") * share, share)
    return (output, input_grad, owned[0], owned[1], owned[2], owned[3], gain_grad)


def solution(mesh):
    in_specs = (
        P(("fsdp", "sub"), None),
        P(("fsdp", "sub"), None),
        P(("fsdp", "sub")),
        P("fsdp"),
        P(("fsdp", "sub")),
        P(("fsdp", "sub")),
        P(("fsdp", "sub")),
        P(("fsdp", "sub")),
    )
    out_specs = (
        P(("fsdp", "sub"), None),
        P(("fsdp", "sub"), None),
        P(("fsdp", "sub")),
        P(("fsdp", "sub")),
        P(("fsdp", "sub")),
        P(("fsdp", "sub")),
        P("fsdp"),
    )
    return jax.shard_map(body, mesh=mesh, in_specs=in_specs, out_specs=out_specs, check_vma=False)
```

profile of v0, /device:TPU:0, one launch (start us, length us, event | category | flops | bytes accessed | tf_op | source)
XLA Modules:
  0.0 811.4 jit_solution(17668553833936328837)
XLA Ops:
  15.4 23.2 %all-reduce = bf16[1920]{0:T(1024)(128)(2,1)S(1)} all-reduce(bf16[1920]{0:T(1024)(128)(2,1)S(1)} %dynamic-update-slice), channel_id=1, replica_groups=mesh['fsdp'=8,'sub'=4] {'fsdp'}, use_global_device_ids=true, to_apply=%add | all-reduce | flops 1920 | bytes 7680
  42.1 35.9 %all-gather.5.cloned.1.call-done = bf16[2457600]{0:T(1024)(128)(2,1)} async-done(((bf16[76800]{0:T(1024)(128)(2,1)}), bf16[2457600]{0:T(1024)(128)(2,1)}) %all-gather.5.cloned.1.call-update) | async-done | bytes 4915216 | tf_op jit(solution)/shard_map/all_gather | solution.py:121
  78.0 10.0 %reshape.188 = bf16[960,2560]{1,0:T(8,128)(2,1)} reshape(bf16[2457600]{0:T(1024)(128)(2,1)} %all-gather.5.cloned.1.call-done) | data formatting | bytes 9830400 | tf_op jit(solution)/shard_map/reshape | solution.py:126
  87.9 3.5 fusion.3
  91.5 52.4 %all-gather.7.cloned.1.call-done = bf16[2457600]{0:T(1024)(128)(2,1)} async-done(((bf16[76800]{0:T(1024)(128)(2,1)}), bf16[2457600]{0:T(1024)(128)(2,1)}) %all-gather.7.cloned.1.call-update) | async-done | bytes 4915216 | tf_op jit(solution)/shard_map/all_gather | solution.py:122
  144.0 10.0 %reshape.191 = bf16[960,2560]{1,0:T(8,128)(2,1)} reshape(bf16[2457600]{0:T(1024)(128)(2,1)} %all-gather.7.cloned.1.call-done) | data formatting | bytes 9830400 | tf_op jit(solution)/shard_map/reshape | solution.py:126
  154.0 56.1 %all-gather.9.cloned.1.call-done = bf16[2457600]{0:T(1024)(128)(2,1)} async-done(((bf16[76800]{0:T(1024)(128)(2,1)}), bf16[2457600]{0:T(1024)(128)(2,1)}) %all-gather.9.cloned.1.call-update) | async-done | bytes 4915216 | tf_op jit(solution)/shard_map/all_gather | solution.py:123
  210.0 10.0 %reshape.192 = bf16[960,2560]{1,0:T(8,128)(2,1)} reshape(bf16[2457600]{0:T(1024)(128)(2,1)} %all-gather.9.cloned.1.call-done) | data formatting | bytes 9830400 | tf_op jit(solution)/shard_map/reshape | solution.py:126
  221.1 2.8 multiply_reduce_fusion.3
  228.6 47.3 %all-gather.11.cloned.1.call-done = bf16[2457600]{0:T(1024)(128)(2,1)} async-done(((bf16[76800]{0:T(1024)(128)(2,1)}), bf16[2457600]{0:T(1024)(128)(2,1)}) %all-gather.11.cloned.1.call-update) | async-done | bytes 4915216 | tf_op jit(solution)/shard_map/all_gather | solution.py:124
  275.9 10.1 %reshape.193 = bf16[960,2560]{1,0:T(8,128)(2,1)} reshape(bf16[2457600]{0:T(1024)(128)(2,1)} %all-gather.11.cloned.1.call-done) | data formatting | bytes 9830400 | tf_op jit(solution)/shard_map/reshape | solution.py:126
  285.9 4.7 multiply_convert_fusion
  292.2 4.0 multiply_reduce_fusion.1
  296.5 3.4 fusion.20
  301.6 2.8 broadcast_multiply_fusion.1
  304.4 2.9 broadcast_multiply_fusion
  307.3 3.5 fusion.63
  310.9 5.2 fusion.95
  316.1 5.1 fusion.94
  321.3 5.1 fusion.55
  326.4 15.1 %reshape_reshape.13 = f32[38400,64]{1,0:T(8,128)} reshape(f32[960,2560]{1,0:T(8,128)} %fusion.94) | data formatting | bytes 19660800 | tf_op jit(solution)/shard_map/reshape;reshape | solution.py:136
  341.5 15.0 %reshape_reshape.14 = f32[38400,64]{1,0:T(8,128)} reshape(f32[960,2560]{1,0:T(8,128)} %fusion.95) | data formatting | bytes 19660800 | tf_op jit(solution)/shard_map/reshape;reshape | solution.py:136
  356.5 15.3 %reshape_reshape.15 = f32[38400,64]{1,0:T(8,128)} reshape(f32[960,2560]{1,0:T(8,128)} %fusion.55) | data formatting | bytes 19660800 | tf_op jit(solution)/shard_map/reshape;reshape | solution.py:136
  372.8 3.7 fusion.59
  376.4 9.6 %pad_maximum_fusion.1 = f32[960,2560]{1,0:T(8,128)} fusion(f32[960,960]{1,0:T(8,128)} %fusion.63, f32[960,1600]{1,0:T(8,128)} %fusion.59), kind=kLoop, calls=%fused_computation.2 | loop fusion | flops 2457600 | bytes 19660800 | tf_op jit(solution)/shard_map/concatenate | solution.py:135
  386.0 15.0 %reshape_reshape.12 = f32[38400,64]{1,0:T(8,128)} reshape(f32[960,2560]{1,0:T(8,128)} %pad_maximum_fusion.1) | data formatting | bytes 19660800 | tf_op jit(solution)/shard_map/reshape;reshape | solution.py:136
  401.0 38.5 %pad_maximum_fusion = f32[38400,256]{1,0:T(8,128)} fusion(f32[38400,64]{1,0:T(8,128)} %reshape_reshape.15, f32[38400,64]{1,0:T(8,128)} %reshape_reshape.14, f32[38400,64]{1,0:T(8,128)} %reshape_reshape.13, f32[38400,64]{1,0:T(8,128)} %reshape_reshape.12), kind=kLoop, calls=%fused_computation.1 | loop fusion | flops 29491200 | bytes 78643200 | tf_op jit(solution)/shard_map/concatenate | solution.py:137
  439.6 3.0 fusion.42
  442.6 39.6 %psum.7 = f32[1920]{0:T(1024)S(1)} all-reduce(f32[1920]{0:T(1024)S(1)} %pad_maximum_fusion.7), channel_id=1, replica_groups=mesh['fsdp'=8,'sub'=4] {'fsdp','sub'}, use_global_device_ids=true, to_apply=%region_10.11 | all-reduce | flops 1920 | bytes 15360 | tf_op jit(solution)/shard_map/psum | solution.py:247
  483.9 5.3 fusion.23
  489.2 310.2 %reduce-scatter.2.cloned.1.call-done = f32[1200,256]{1,0:T(8,128)} async-done(((f32[38400,256]{1,0:T(8,128)}), f32[1200,256]{1,0:T(8,128)}) %reduce-scatter.2.cloned.1.call-update) | async-done | bytes 1228816 | tf_op jit(solution)/shard_map/reduce_scatter | solution.py:151
  799.3 2.0 fusion.81
  (105 shorter events, 25.0 us)
Async XLA Ops:
  7.2 70.8 %all-gather.5.cloned.1.call-start = ((), (), s32[]{:S(2)}) async-start(), calls=%async_computation.1 | async-start | bytes 5068800 | tf_op jit(solution)/shard_map/all_gather | solution.py:121
  7.9 136.1 %all-gather.7.cloned.1.call-start = ((), (), s32[]{:S(2)}) async-start(), calls=%async_computation.2 | async-start | bytes 5068800 | tf_op jit(solution)/shard_map/all_gather | solution.py:122
  8.6 201.4 %all-gather.9.cloned.1.call-start = ((), (), s32[]{:S(2)}) async-start(), calls=%async_computation.3 | async-start | bytes 5068800 | tf_op jit(solution)/shard_map/all_gather | solution.py:123
  9.4 266.5 %all-gather.11.cloned.1.call-start = ((), (), s32[]{:S(2)}) async-start(), calls=%async_computation.4 | async-start | bytes 5068800 | tf_op jit(solution)/shard_map/all_gather | solution.py:124
  10.0 789.4 %reduce-scatter.2.cloned.1.call-start = ((), (), s32[]{:S(2)}) async-start(), calls=%async_computation.5 | async-start | bytes 40550400 | tf_op jit(solution)/shard_map/reduce_scatter | solution.py:151
  40.8 179.3 %copy-start.11 = (f32[128,64]{0,1:T(8,128)}, f32[128,64]{0,1:T(8,128)S(1)}, u32[]{:S(2)}) copy-start(f32[128,64]{0,1:T(8,128)S(1)} %get-tuple-element.45) | copy-start | bytes 98308
  41.9 46.0 %copy-start.16 = (f32[128]{0:T(128)}, f32[128]{0:T(128)S(1)}, u32[]{:S(2)}) copy-start(f32[128]{0:T(128)S(1)} %add_rsqrt_fusion.1) | copy-start | bytes 1540
  42.1 45.9 %copy-start.1 = (bf16[128,960]{0,1:T(8,128)(2,1)S(1)}, bf16[128,960]{0,1:T(8,128)(2,1)}, u32[]{:S(2)}) copy-start(bf16[128,960]{0,1:T(8,128)(2,1)} %param.8) | copy-start | bytes 737284
  220.2 0.9 copy-start.8
  220.5 4.1 copy-start
  220.7 5.9 slice-start
  221.1 3.4 copy-start.13
  221.1 5.6 slice-start.1
  223.8 4.7 copy-start.18
  275.9 14.8 %slice-start.2 = ((s8[4915200]{0:T(1024)(128)(4,1)}), s8[720896]{0:T(1024)(128)(4,1)S(1)}, s32[]{:S(2)}) async-start(s8[4915200]{0:T(1024)(128)(4,1)} %bitcast.69), calls=%async_computation.8 | async-start | bytes 1441792
  285.9 4.8 slice-start.3
  290.7 5.5 copy-start.2
  290.7 5.5 copy-start.4
  290.7 1.5 copy-start.19
  292.2 4.1 copy-start.6
  292.2 9.0 %copy-start.15 = (f32[5,3,128]{2,1,0:T(4,128)S(1)}, f32[5,3,128]{2,1,0:T(4,128)}, u32[]{:S(2)}) copy-start(f32[5,3,128]{2,1,0:T(4,128)} %log_add_fusion) | copy-start | bytes 23044
  296.2 5.4 copy-start.12
  307.3 3.5 copy-start.5
  310.9 5.2 copy-start.3
  316.0 5.1 copy-start.14
  316.1 5.1 copy-start.10
  316.1 5.2 copy-start.7
  356.5 16.2 %copy-start.9 = (f32[128,5,3,64]{0,3,2,1:T(8,128)S(1)}, f32[128,5,3,64]{0,3,2,1:T(8,128)}, u32[]{:S(2)}) copy-start(f32[128,5,3,64]{0,3,2,1:T(8,128)} %get-tuple-element.42) | copy-start | bytes 1474564
  356.5 16.3 %copy-start.17 = (f32[128]{0:T(128)S(1)}, f32[128]{0:T(128)}, u32[]{:S(2)}) copy-start(f32[128]{0:T(128)} %copy-done.16) | copy-start | bytes 1540
Sparse Core Ops, SparseCore 0:
  10.8 67.0 all-gather.4
  80.8 63.1 all-gather.6
  146.8 63.1 all-gather.8
  212.7 63.1 all-gather.10
  439.7 359.6 reduce-scatter.1
where the time goes:
time: 814 us; the launch traced here: 811 us
  waiting for transfers between devices  504 us (62%)
  local copies, waits for them, and re-layouts  110 us (14%)
  blocking collectives  62.9 us (8%)
  matrix products  62.8 us (8%)
  other arithmetic  54.8 us (7%)
  between operations  16.2 us (2%)
    reduce_scatter x1, waiting for transfers between devices, spread(): lax.psum_scatter(flat_terms(pair_lists, share * lax.axis_size(('fsdp', 's...  310 us
    another operation x4, local copies, waits for them, and re-layouts, flat_terms(): results.append(joined.reshape(-1).reshape(count, piece_width))  60.3 us
    all_gather x1, waiting for transfers between devices, collect(): lax.all_gather(up_flat, ('fsdp', 'sub'), axis=0, tiled=True)  56.1 us
    all_gather x1, waiting for transfers between devices, collect(): lax.all_gather(gate_flat, ('fsdp', 'sub'), axis=0, tiled=True)  52.4 us
    all_gather x1, waiting for transfers between devices, collect(): lax.all_gather(down_flat, ('fsdp', 'sub'), axis=0, tiled=True)  47.3 us
    reshape x4, local copies, waits for them, and re-layouts, collect(): return tuple((piece.reshape(D, FF) for piece in whole))  39.9 us
    psum x1, blocking collectives, body(): lax.psum(jnp.concatenate([gain1_term, gain2_term]), ('fsdp', 'sub'))  39.6 us
    concatenate x1, other arithmetic, flat_terms(): return jnp.concatenate(results, axis=1)  38.5 us
  transfers between devices with their start and end apart: 5, of which 5 were waited for; matrix products, arithmetic and copies ran while one was open for 7% of the time, Pallas kernels for 0%

commit v1 on v0

--- a/solution.py
+++ b/solution.py
@@ -1,6 +1,8 @@
 import jax
 import jax.numpy as jnp
 from jax import lax
+from jax.experimental import pallas as pl
+from jax.experimental.pallas import tpu as pltpu
 from jax.sharding import PartitionSpec as P
 
 D = 960
@@ -219,7 +221,7 @@
     return (output, input_grad, owned, gain1_term, gain2_term)
 
 
-def body(rows, cotangent, lengths, gains, attn_weight, gate_weight, up_weight, down_weight):
+def plain_body(rows, cotangent, lengths, gains, attn_weight, gate_weight, up_weight, down_weight):
     count = rows.shape[0]
     position, live, allowed = layout(lengths, count)
     cosine, sine = rope_tables(position, HD)
@@ -250,7 +252,456 @@
     return (output, input_grad, owned[0], owned[1], owned[2], owned[3], gain_grad)
 
 
+BF = jnp.bfloat16
+F32 = jnp.float32
+
+
+def swap(value, axis, bit):
+    return lax.ppermute(value, axis, [(i, i ^ bit) for i in range(lax.axis_size(axis))])
+
+
+def after(value, *done):
+    return lax.optimization_barrier((value, *done))[0]
+
+
+def add2(kept, came):
+    return (kept.astype(F32) + came.astype(F32)).astype(BF)
+
+
+def pick(value, index, axis):
+    return lax.dynamic_index_in_dim(value, index, axis, keepdims=False)
+
+
+def put2(own, came, bit, axis):
+    first = bit == 0
+    return jnp.stack([jnp.where(first, own, came), jnp.where(first, came, own)], axis=axis)
+
+
+def mm(a, b):
+    return jnp.dot(a, b, preferred_element_type=F32)
+
+
+def mm_t(a, b):
+    return lax.dot_general(a, b, (((1,), (1,)), ((), ())), preferred_element_type=F32)
+
+
+def term(a, b):
+    return lax.dot_general(a, b, (((0,), (0,)), ((), ())), preferred_element_type=F32).astype(BF)
+
+
+def dot_f(a, b):
+    return lax.dot_general(a, b, (((1,), (0,)), ((), ())), preferred_element_type=F32)
+
+
+def dot_t(a, b):
+    return lax.dot_general(a, b, (((1,), (1,)), ((), ())), preferred_element_type=F32)
+
+
+def dot_0(a, b):
+    return lax.dot_general(a, b, (((0,), (0,)), ((), ())), preferred_element_type=F32)
+
+
+def norm_rows(values):
+    mean = jnp.sum(values * values, axis=1, keepdims=True) * (1.0 / D)
+    scale = lax.rsqrt(mean + EPS)
+    return values * scale, scale
+
+
+def norm_rows_back(grad_in, normed, scale, gain):
+    gain_term = jnp.sum(grad_in * normed, axis=0, keepdims=True)
+    inner = grad_in * gain
+    mean = jnp.sum(inner * normed, axis=1, keepdims=True) * (1.0 / D)
+    return scale * (inner - normed * mean), gain_term
+
+
+def first_half(shape):
+    return lax.broadcasted_iota(jnp.int32, shape, 1) % HD < HD // 2
+
+
+def gain_masks(owner, my_fsdp, n_fsdp, own, share):
+    wide = owner.shape[1]
+    per = share // own
+    place = lax.broadcasted_iota(jnp.int32, (n_fsdp, wide), 0) ^ my_fsdp
+    group = owner // per
+    return place == group, place == group + n_fsdp // 2
+
+
+def slot_matrix(owner, inner, own, share):
+    per = share // own
+    slot = jnp.where(inner < own, owner % per * own + inner, -1)
+    return (lax.broadcasted_iota(jnp.int32, (share, owner.shape[1]), 0) == slot).astype(F32).astype(BF)
+
+
+def make_forward(n_fsdp, own, padded, share):
+    kv_width = KV * HD
+
+    def kernel(
+        place_ref, rows_ref, pieces_ref, owner_ref, inner_ref, cos_ref, sin_ref, seg_ref,
+        attn_q_ref, attn_o_ref,
+        input1_ref, qk_ref, v_ref, logsum_ref, att_ref, hidden1_ref, input2_ref, gains_ref,
+    ):
+        owner = owner_ref[...]
+        first, second = gain_masks(owner, place_ref[0], n_fsdp, own, share)
+        spots = dot_f(pieces_ref[...], slot_matrix(owner, inner_ref[...], own, share))
+        gain1 = jnp.sum(jnp.where(first, spots, 0.0), axis=0, keepdims=True)
+        gain2 = jnp.sum(jnp.where(second, spots, 0.0), axis=0, keepdims=True)
+        gains_ref[0:1, :] = gain1
+        gains_ref[1:2, :] = gain2
+        rows = rows_ref[...]
+        normed, _ = norm_rows(rows)
+        input1 = (normed * gain1).astype(BF)
+        input1_ref[...] = input1
+        projected = dot_f(input1, attn_q_ref[...])
+        cosine = cos_ref[...]
+        sine = sin_ref[...]
+        low = first_half(cosine.shape)
+        for i in range(projected.shape[1] // 128):
+            part = projected[:, 128 * i : 128 * (i + 1)]
+            turned = jnp.where(low, -pltpu.roll(part, 96, 1), pltpu.roll(part, 32, 1))
+            qk_ref[:, 128 * i : 128 * (i + 1)] = (part * cosine + turned * sine).astype(BF)
+        values = dot_f(input1, attn_o_ref[:, :384]).astype(BF)
+        v_ref[...] = values
+        allowed = seg_ref[...] > 0.0
+        att_ref[:, :384] = jnp.zeros((rows.shape[0], 384), BF)
+        for k in range(KV):
+            keys = qk_ref[:, D + HD * k : D + HD * (k + 1)]
+            value = values[:, HD * k : HD * (k + 1)]
+            for g in range(GROUP):
+                h = GROUP * k + g
+                queries = qk_ref[:, HD * h : HD * (h + 1)]
+                scores = jnp.where(allowed, dot_t(queries, keys) * HD ** (-0.5), NEG)
+                top = jnp.max(scores, axis=1, keepdims=True)
+                expo = jnp.exp(scores - top)
+                total = jnp.sum(expo, axis=1, keepdims=True)
+                logsum_ref[:, h : h + 1] = top + jnp.log(total)
+                weights = (expo / total).astype(BF)
+                att_ref[:, kv_width + HD * h : kv_width + HD * (h + 1)] = dot_f(weights, value).astype(BF)
+        hidden1 = rows + dot_t(att_ref[...], attn_o_ref[...])
+        hidden1_ref[...] = hidden1
+        normed2, _ = norm_rows(hidden1)
+        input2_ref[...] = (normed2 * gain2).astype(BF)
+
+    return kernel
+
+
+def make_backward(n_fsdp, own, padded, share):
+    kv_width = KV * HD
+
+    def kernel(
+        place_ref, grad_a_ref, grad_b_ref, grad_out_ref, hidden1_ref, rows_ref, gains_ref, owner_ref, inner_ref,
+        spots_ref, cos_ref, sin_ref, seg_ref, input1_ref, qk_ref, v_ref, logsum_ref, att_ref,
+        attn_q_ref, attn_o_ref,
+        q_term_ref, o_term_ref, input_grad_ref,
+        left_ref, right_ref, turn_ref,
+    ):
+        count = rows_ref.shape[0]
+        wide = rows_ref.shape[1]
+        gain1 = gains_ref[0:1, :]
+        gain2 = gains_ref[1:2, :]
+        grad_in2 = grad_a_ref[...].astype(F32) + grad_b_ref[...].astype(F32)
+        normed2, scale2 = norm_rows(hidden1_ref[...])
+        back2, gain2_term = norm_rows_back(grad_in2, normed2, scale2, gain2)
+        grad_h1 = grad_out_ref[...].astype(F32) + back2
+        grad_h1b = grad_h1.astype(BF)
+        left_ref[:count, :] = input1_ref[...]
+        left_ref[count:, :] = grad_h1b
+        right_ref[:count, :] = jnp.zeros((count, right_ref.shape[1]), BF)
+        right_ref[count:, :] = att_ref[...]
+        grad_att = dot_f(grad_h1b, attn_o_ref[...]).astype(BF)
+        allowed = seg_ref[...] > 0.0
+        for k in range(KV):
+            keys = qk_ref[:, D + HD * k : D + HD * (k + 1)]
+            value = v_ref[:, HD * k : HD * (k + 1)]
+            value_grad = jnp.zeros((count, HD), F32)
+            key_grad = jnp.zeros((count, HD), F32)
+            for g in range(GROUP):
+                h = GROUP * k + g
+                queries = qk_ref[:, HD * h : HD * (h + 1)]
+                grad = grad_att[:, kv_width + HD * h : kv_width + HD * (h + 1)]
+                scores = jnp.where(allowed, dot_t(queries, keys) * HD ** (-0.5), NEG)
+                probs = jnp.exp(scores - logsum_ref[:, h : h + 1])
+                value_grad = value_grad + dot_0(probs.astype(BF), grad)
+                prob_grad = dot_t(grad, value)
+                delta = jnp.sum(probs * prob_grad, axis=1, keepdims=True)
+                score_grad = (probs * (prob_grad - delta) * HD ** (-0.5)).astype(BF)
+                turn_ref[:, HD * h : HD * (h + 1)] = dot_f(score_grad, keys)
+                key_grad = key_grad + dot_0(score_grad, queries)
+            turn_ref[:, D + HD * k : D + HD * (k + 1)] = key_grad
+            right_ref[:count, HD * k : HD * (k + 1)] = value_grad.astype(BF)
+        cosine = cos_ref[...]
+        sine = sin_ref[...]
+        low = first_half(cosine.shape)
+        pieces = []
+        for i in range(turn_ref.shape[1] // 128):
+            part = turn_ref[:, 128 * i : 128 * (i + 1)]
+            scaled = part * sine
+            turned = jnp.where(low, pltpu.roll(scaled, 96, 1), -pltpu.roll(scaled, 32, 1))
+            pieces.append((part * cosine + turned).astype(BF))
+        proj_grad = jnp.concatenate(pieces, axis=1)
+        o_term_ref[...] = dot_0(left_ref[...], right_ref[...]).astype(BF)
+        owner = owner_ref[...]
+        inner = inner_ref[...]
+        grad_in1 = dot_t(proj_grad, attn_q_ref[...]) * jnp.where(inner < own, 1.0, 0.0) + dot_t(
+            right_ref[:count, :], attn_o_ref[...]
+        )
+        normed1, scale1 = norm_rows(rows_ref[...])
+        back1, gain1_term = norm_rows_back(grad_in1, normed1, scale1, gain1)
+        input_grad_ref[...] = grad_h1 + back1
+        first, second = gain_masks(owner, place_ref[0], n_fsdp, own, share)
+        both = jnp.where(first, gain1_term, 0.0) + jnp.where(second, gain2_term, 0.0)
+        gain_rows = dot_t(both.astype(BF), slot_matrix(owner, inner, own, share)).astype(BF)
+        q_term = dot_0(input1_ref[...], proj_grad)
+        q_term_ref[...] = q_term.astype(BF)
+        q_term_ref[:, :share] = (q_term[:, :share] + dot_f(spots_ref[...], gain_rows)).astype(BF)
+
+    return kernel
+
+
+VMEM = pl.BlockSpec(memory_space=pltpu.VMEM)
+SMEM = pl.BlockSpec(memory_space=pltpu.SMEM)
+
+
+def run_kernel(kernel, outs, args, scratch=(), name=None):
+    return pl.pallas_call(
+        kernel,
+        out_shape=[jax.ShapeDtypeStruct(shape, kind) for shape, kind in outs],
+        in_specs=[SMEM] + [VMEM] * (len(args) - 1),
+        out_specs=[VMEM] * len(outs),
+        scratch_shapes=scratch,
+        compiler_params=pltpu.CompilerParams(vmem_limit_bytes=56 << 20),
+        cost_estimate=pl.CostEstimate(flops=1000, transcendentals=0, bytes_accessed=1000),
+        name=name,
+    )(*args)
+
+
+def body(rows, cotangent, lengths, gains, attn_weight, gate_weight, up_weight, down_weight):
+    count = rows.shape[0]
+    n_fsdp = lax.axis_size("fsdp")
+    n_sub = lax.axis_size("sub")
+    n_all = n_fsdp * n_sub
+    n_far = n_fsdp // 2
+    own = D // n_all
+    padded = -(-(own + 1) // 16) * 16
+    wide = n_all * padded
+    half_ff = FF // 2
+    quarter = FF // 4
+    share = gains.shape[0]
+    kv_width = KV * HD
+    my_fsdp = lax.axis_index("fsdp")
+    my_sub = lax.axis_index("sub")
+    my_y = my_sub // 2
+    my_c = my_sub % 2
+
+    column = jnp.arange(wide, dtype=jnp.int32)
+    place = column // padded
+    inner = column % padded
+    rel = (place // n_sub) % n_far * 2 + place // (n_sub * n_far)
+    real = inner < own
+    source = jnp.where(real, ((rel ^ my_fsdp) * n_sub + place % n_sub) * own + inner, -1)
+    spread_mat = (jnp.arange(D, dtype=jnp.int32)[:, None] == source[None, :]).astype(BF)
+
+    def padded_block(flat):
+        return jnp.pad(flat.reshape(own, FF), ((0, padded - own), (0, 0)))
+
+    def far_gather(block):
+        return jnp.stack([block] + [swap(block, "fsdp", 2 * k) for k in range(1, n_far)], axis=0)
+
+    def columns(value, index, width):
+        return lax.dynamic_slice_in_dim(value, index * width, width, axis=value.ndim - 1)
+
+    position, live, allowed = layout(lengths, count)
+    cosine, sine = rope_tables(position, HD)
+    cosine = jnp.concatenate([cosine, cosine], axis=1)
+    sine = jnp.concatenate([sine, sine], axis=1)
+    seg = allowed.astype(F32)
+    rows32 = mm(rows, spread_mat)
+    grad_outb = (live * mm(cotangent, spread_mat)).astype(BF)
+
+    def group_tokens(value):
+        value = jnp.stack([value, swap(value, "sub", 2)])
+        return jnp.stack([value, swap(value, "sub", 1)]).reshape(4 * count, wide)
+
+    def group_half(value):
+        value = value.astype(BF).reshape(2, 2 * count, wide)
+        value = add2(value[0], swap(value[1], "sub", 1)).reshape(2, count, wide)
+        return value[0], swap(value[1], "sub", 2)
+
+    attn_block = padded_block(attn_weight)
+    attn_block = attn_block.at[own, :share].set(gains)
+    attn_far = far_gather(attn_block)
+    mlp_block = jnp.stack([padded_block(w) for w in (gate_weight, up_weight, down_weight)])
+    came = swap(columns(mlp_block, 1 - my_y, half_ff), "sub", 2)
+    mlp_block = put2(columns(mlp_block, my_y, half_ff), came, my_y, 1)
+    came = swap(columns(mlp_block, 1 - my_c, quarter), "sub", 1)
+    mlp_block = put2(columns(mlp_block, my_c, quarter), came, my_c, 2)
+    mlp_block = mlp_block.reshape(3, n_sub * padded, quarter)
+    cot_all = group_tokens(grad_outb)
+    attn_far, mlp_block, cot_all = lax.optimization_barrier((attn_far, mlp_block, cot_all))
+
+    half0 = attn_far[:, :, :half_ff]
+    half1 = attn_far[:, :, half_ff:]
+    gate_up = [mlp_block[:2]]
+    half0 = jnp.stack([half0, swap(half0, "fsdp", 1)])
+    half1 = put2(half1, swap(half1, "sub", 2), my_y, 1)
+    gate_up.append(swap(mlp_block[:2], "fsdp", 2))
+    half0, half1, gate_up = lax.optimization_barrier((half0, half1, gate_up))
+
+    gate_up = gate_up + [swap(gate_up[0], "fsdp", 2 * k) for k in range(2, 3)]
+    half0 = put2(half0, swap(half0, "sub", 2), my_y, 2)
+    half1 = jnp.stack([half1, swap(half1, "fsdp", 1)])
+    half0, half1, gate_up, down_w = lax.optimization_barrier((half0, half1, gate_up, mlp_block[2:]))
+
+    attn_q = put2(half0, swap(half0, "sub", 1), my_c, 3).reshape(wide, half_ff)
+    attn_o = put2(half1, swap(half1, "sub", 1), my_c, 3).reshape(wide, half_ff)
+    gate_up = gate_up + [swap(gate_up[0], "fsdp", 2 * k) for k in range(3, n_far)]
+    attn_q, attn_o, down_w = lax.optimization_barrier((attn_q, attn_o, down_w))
+    gate_up = jnp.stack(gate_up)
+    gate_up_came = swap(gate_up, "fsdp", 1)
+    down_w = far_gather(down_w)
+
+    by_fsdp = [(f % 2) * n_far * n_sub + (f // 2) * n_sub for f in range(n_fsdp)]
+    pieces = attn_q.reshape(n_all, padded, half_ff)
+    pieces = jnp.stack([pieces[p, own, :share] for p in by_fsdp])
+    my_place = my_fsdp.reshape(1)
+    owner = (((rel ^ my_fsdp) * n_sub + place % n_sub))[None, :]
+    tables = (owner, inner[None, :])
+    angles = (cosine, sine, seg)
+    sizes = (n_fsdp, own, padded, share)
+    tall = (count, wide)
+    forward = run_kernel(
+        make_forward(*sizes),
+        [
+            (tall, BF),
+            ((count, half_ff), BF),
+            ((count, 384), BF),
+            ((count, KV * GROUP), F32),
+            ((count, half_ff), BF),
+            (tall, F32),
+            (tall, BF),
+            ((2, wide), F32),
+        ],
+        (my_place, rows32, pieces, *tables, *angles, attn_q, attn_o),
+        name="attn_forward",
+    )
+    input1, qk, values, logsum, attended, hidden1, input2, gains_p = forward
+    in2_all = group_tokens(input2)
+    gate_up_came = after(gate_up_came, input2)
+    gate_w = jnp.stack([gate_up[:, 0], gate_up_came[:, 0]]).reshape(wide, quarter)
+    up_w = jnp.stack([gate_up[:, 1], gate_up_came[:, 1]]).reshape(wide, quarter)
+    down_w = after(down_w, gate_up_came)
+    down_came = swap(down_w, "fsdp", 1)
+    gate = mm(in2_all, gate_w)
+    up = mm(in2_all, up_w)
+    sigma = jax.nn.sigmoid(gate)
+    active = gate * sigma
+    hidden = (active * up).astype(BF)
+    down_came = after(down_came, hidden)
+    down_w = jnp.stack([down_w, down_came]).reshape(wide, quarter)
+    down_term = term(cot_all, hidden)
+    grad_hidden = mm(cot_all, down_w)
+    grad_gate = (grad_hidden * up * sigma * (1.0 + gate * (1.0 - sigma))).astype(BF)
+    grad_up = (grad_hidden * active).astype(BF)
+    grad_in2 = group_half(mm_t(grad_gate, gate_w) + mm_t(grad_up, up_w))
+    gate_term = term(in2_all, grad_gate)
+    up_term = term(in2_all, grad_up)
+    result = group_half(after(mm_t(hidden, down_w), *grad_in2))
+    of_place = [(p // n_sub) % n_far * 2 + p // (n_sub * n_far) for p in range(n_all)]
+    at_spot = jnp.where(inner == own, jnp.array(of_place)[place], -1)
+    spots = (at_spot[:, None] == jnp.arange(n_fsdp)[None, :]).astype(BF)
+    q_term, o_term, input_grad = run_kernel(
+        make_backward(*sizes),
+        [((wide, half_ff), BF), ((wide, half_ff), BF), (tall, F32)],
+        (
+            my_place, *grad_in2, grad_outb, hidden1, rows32, gains_p, *tables, spots, *angles,
+            input1, qk, values, logsum, attended, attn_q, attn_o,
+        ),
+        scratch=[
+            pltpu.VMEM((2 * count, wide), BF),
+            pltpu.VMEM((2 * count, half_ff), BF),
+            pltpu.VMEM((count, half_ff), F32),
+        ],
+        name="attn_backward",
+    )
+    result = hidden1 + result[0].astype(F32) + result[1].astype(F32)
+    output = mm_t((live * result).astype(BF), spread_mat).astype(BF)
+    input_grad = lax.dot_general(
+        input_grad,
+        spread_mat.astype(F32),
+        (((1,), (1,)), ((), ())),
+        precision=lax.Precision.HIGHEST,
+    )
+
+    def far_sum(held, axis, *done):
+        parts = [lax.index_in_dim(held, 0, axis, keepdims=False)]
+        for k in range(1, n_far):
+            parts.append(swap(lax.index_in_dim(held, k, axis, keepdims=False), "fsdp", 2 * k))
+        parts = after(parts, *done)
+        total = parts[0].astype(F32)
+        for part in parts[1:]:
+            total = total + part.astype(F32)
+        return total.astype(BF)
+
+    def sub_return(held):
+        came = swap(pick(held, 1 - my_c, 2), "sub", 1)
+        mine = pick(held, my_c, 2)
+        first = my_c == 0
+        held = jnp.concatenate(
+            [jnp.where(first, mine, came), jnp.where(first, came, mine)], axis=-1
+        )
+        came = swap(pick(held, 1 - my_y, 1), "sub", 2)
+        mine = pick(held, my_y, 1)
+        first = my_y == 0
+        return jnp.concatenate(
+            [jnp.where(first, mine, came), jnp.where(first, came, mine)], axis=-1
+        )
+
+    def mlp_sum(terms, near_done, far_done):
+        k = len(terms)
+        held = jnp.stack(terms).reshape(k, 2, n_far, n_sub * padded, quarter)
+        held = add2(held[:, 0], after(swap(held[:, 1], "fsdp", 1), *near_done))
+        held = far_sum(held, 1, *far_done).reshape(k, 2, 2, padded, quarter)
+        return sub_return(held)
+
+    def core_sum(held):
+        held = held.reshape(2, n_far, 2, 2, padded, half_ff)
+        return add2(pick(held, my_c, 3), swap(pick(held, 1 - my_c, 3), "sub", 1))
+
+    def x_sum(held):
+        return add2(held[0], swap(held[1], "fsdp", 1))
+
+    def y_sum(held, axis):
+        return add2(pick(held, my_y, axis), swap(pick(held, 1 - my_y, axis), "sub", 2))
+
+    o_held = x_sum(core_sum(o_term))
+    q_held = y_sum(core_sum(q_term), 2)
+    down_own = mlp_sum([down_term], grad_in2, [q_term])
+    gate_up_own = mlp_sum([gate_term, up_term], [q_term], [o_held, q_held])
+    o_own = far_sum(y_sum(o_held, 1), 0)
+    q_own = far_sum(x_sum(q_held), 0)
+    gain_grad = q_own[own, :share].astype(F32)
+    attn_own = jnp.concatenate([q_own, o_own], axis=1)
+
+    def flat(mine):
+        return mine[:own].astype(F32).reshape(-1)
+
+    return (
+        output,
+        input_grad,
+        flat(attn_own),
+        flat(gate_up_own[0]),
+        flat(gate_up_own[1]),
+        flat(down_own[0]),
+        gain_grad,
+    )
+
+
 def solution(mesh):
+    n_fsdp, n_sub = mesh.shape["fsdp"], mesh.shape["sub"]
+    n_all = n_fsdp * n_sub
+    by_rows = (
+        n_fsdp == 8 and
+        D % n_all == 0 and n_fsdp & (n_fsdp - 1) == 0 and n_fsdp > 1 and n_sub == 4 and D // n_fsdp % (D // n_all) == 0
+    )
     in_specs = (
         P(("fsdp", "sub"), None),
         P(("fsdp", "sub"), None),
@@ -270,4 +721,4 @@
         P(("fsdp", "sub")),
         P("fsdp"),
     )
-    return jax.shard_map(body, mesh=mesh, in_specs=in_specs, out_specs=out_specs, check_vma=False)
+    return jax.shard_map(body if by_rows else plain_body, mesh=mesh, in_specs=in_specs, out_specs=out_specs, check_vma=False)

time: 814 us -> 252 us (0.31)
  waiting for transfers between devices: 504 us -> 98.2 us
  local copies, waits for them, and re-layouts: 110 us -> 21 us
  starting transfers between devices: 0.19 us -> 64.7 us
  blocking collectives: 62.9 us -> 0 us
  matrix products: 62.8 us -> 17 us
  other arithmetic: 54.8 us -> 24.9 us
  Pallas kernels: 0 us -> 22.2 us
  between operations: 16.2 us -> 2.87 us
    reduce_scatter x1 -> x0, waiting for transfers between devices: 310 us -> none  [spread(): lax.psum_scatter(flat_terms(pair_lists, share * lax.axis_size(('fsdp', 's...]
    all_gather x4 -> x0, waiting for transfers between devices: 192 us -> none  [the longest x1 56.1 us: collect(): lax.all_gather(up_flat, ('fsdp', 'sub'), axis=0, tiled=True)]
    ppermute x0 -> x51, waiting for transfers between devices: none -> 98.2 us  [swap(): lax.ppermute(value, axis, [(i, i ^ bit) for i in range(lax.axis_size(axis...]
    ppermute x0 -> x51, starting transfers between devices: none -> 64.7 us  [swap(): lax.ppermute(value, axis, [(i, i ^ bit) for i in range(lax.axis_size(axis...]
    another operation x4 -> x10, local copies, waits for them, and re-layouts: 60.3 us -> 4.43 us  [the longest x1 1.4 us: body(): jnp.stack([gate_up[:, 0], gate_up_came[:, 0]]).reshape(wide, quarter)]
    concatenate x4 -> x1, other arithmetic: 48.2 us -> 1.83 us  [body(): cosine = jnp.concatenate([cosine, cosine], axis=1)]
    dot_general x21 -> x13, matrix products: 62.8 us -> 17 us  [the longest x5 6.68 us: mm(): return jnp.dot(a, b, preferred_element_type=F32)]
    psum x1 -> x0, blocking collectives: 39.6 us -> none  [body(): lax.psum(jnp.concatenate([gain1_term, gain2_term]), ('fsdp', 'sub'))]
  transfers between devices with their start and end apart: 5 -> 51, of which waited for: 5 -> 22; matrix products, arithmetic and copies ran while one was open for 7% -> 22% of each run, Pallas kernels for 0% -> 9%
where the time goes in v1:
time: 252 us; the launch traced here: 251 us
  waiting for transfers between devices  98.2 us (39%)
  starting transfers between devices  64.7 us (26%)
  other arithmetic  24.9 us (10%)
  Pallas kernels  22.2 us (9%)
  local copies, waits for them, and re-layouts  21 us (8%)
  matrix products  17 us (7%)
  between operations  2.87 us (1%)
    ppermute x51, waiting for transfers between devices, swap(): lax.ppermute(value, axis, [(i, i ^ bit) for i in range(lax.axis_size(axis...  98.2 us
    ppermute x51, starting transfers between devices, swap(): lax.ppermute(value, axis, [(i, i ^ bit) for i in range(lax.axis_size(axis...  64.7 us
    pallas_call x2, Pallas kernels, run_kernel(): pl.pallas_call(kernel, out_shape=[jax.ShapeDtypeStruct(shape, kind) for s...  22.2 us
    convert_element_type x10, other arithmetic, add2(): return (kept.astype(F32) + came.astype(F32)).astype(BF)  7.25 us
    dot_general x5, matrix products, mm(): return jnp.dot(a, b, preferred_element_type=F32)  6.68 us
    another operation x12, other arithmetic, put2(): jnp.stack([jnp.where(first, own, came), jnp.where(first, came, own)], axi...  6.15 us
  transfers between devices with their start and end apart: 51, of which 22 were waited for; matrix products, arithmetic and copies ran while one was open for 22% of the time, Pallas kernels for 9%

profile of v1, /device:TPU:0, one launch (start us, length us, event | category | flops | bytes accessed | tf_op | source)
XLA Modules:
  0.0 250.9 jit_solution(16352361018122966910)
XLA Ops:
  2.8 5.1 %collective-permute-start.2 = (bf16[32,2560]{1,0:T(8,128)(2,1)S(1)}, bf16[32,2560]{1,0:T(8,128)(2,1)S(1)}, u32[]{:S(2)}, u32[]{:S(2)}) collective-permute-start(bf16[32,2560]{1,0:T(8,128)(2,1)S(1)} %scatter.4), channel_id=1, source_target_pairs={{0,24},{4,28},{8,16},{12,20},{16,8},{20,12},{24,0},{28,4},{1,25},{... | collective-permute-start | bytes 491528 | tf_op jit(solution)/shard_map/ppermute | solution.py:260
  18.6 5.5 %collective-permute-done.5 = bf16[128,1024]{1,0:T(8,128)(2,1)S(1)} collective-permute-done((bf16[128,1024]{1,0:T(8,128)(2,1)S(1)}, bf16[128,1024]{1,0:T(8,128)(2,1)S(1)}, u32[]{:S(2)}, u32[]{:S(2)}) %collective-permute-start.5) | collective-permute-done | bytes 262176 | tf_op jit(solution)/shard_map/ppermute | solution.py:260
  28.7 8.4 %collective-permute-done.8 = bf16[4,32,1280]{2,1,0:T(8,128)(2,1)S(1)} collective-permute-done((bf16[4,32,1280]{2,1,0:T(8,128)(2,1)S(1)}, bf16[4,32,1280]{2,1,0:T(8,128)(2,1)S(1)}, u32[]{:S(2)}, u32[]{:S(2)}) %collective-permute-start.8) | collective-permute-done | bytes 327712 | tf_op jit(solution)/shard_map/ppermute | solution.py:260
  40.3 5.9 %collective-permute-done.7 = bf16[4,32,1280]{2,1,0:T(8,128)(2,1)S(1)} collective-permute-done((bf16[4,32,1280]{2,1,0:T(8,128)(2,1)S(1)}, bf16[4,32,1280]{2,1,0:T(8,128)(2,1)S(1)}, u32[]{:S(2)}, u32[]{:S(2)}) %collective-permute-start.7) | collective-permute-done | bytes 327712 | tf_op jit(solution)/shard_map/ppermute | solution.py:260
  49.8 2.4 collective-permute-start.12
  52.2 10.0 %collective-permute-done.10 = bf16[2,4,32,1280]{3,2,1,0:T(8,128)(2,1)S(1)} collective-permute-done((bf16[2,4,32,1280]{3,2,1,0:T(8,128)(2,1)S(1)}, bf16[2,4,32,1280]{3,2,1,0:T(8,128)(2,1)S(1)}, u32[]{:S(2)}, u32[]{:S(2)}) %collective-permute-start.10) | collective-permute-done | bytes 655392 | tf_op jit(solution)/shard_map/ppermute | solution.py:260
  68.2 1.8 pad_maximum_fusion.22
  70.0 3.2 %collective-permute-start.17 = (bf16[2,128,640]{2,1,0:T(8,128)(2,1)S(1)}, bf16[2,128,640]{2,1,0:T(8,128)(2,1)S(1)}, u32[]{:S(2)}, u32[]{:S(2)}) collective-permute-start(bf16[2,128,640]{2,1,0:T(8,128)(2,1)S(1)} %slice.204), channel_id=1, source_target_pairs={{0,24},{4,28},{8,16},{12,20},{16,8},{20,12},{24,0},{28,4},{1,25},{... | collective-permute-start | bytes 983048 | tf_op jit(solution)/shard_map/ppermute | solution.py:260
  73.8 2.6 %fusion.18.rows_ref = f32[128,1024]{1,0:T(8,128)} fusion(bf16[128,960]{0,1:T(8,128)(2,1)} %param.11, s32[1024]{0:T(1024)S(1)} %fusion.57), kind=kOutput, calls=%fused_computation.51 | convolution fusion | flops 252641280 | bytes 774144 | tf_op jit(solution)/shard_map/dot_general | solution.py:281
  76.4 5.1 %collective-permute-done.17 = bf16[2,128,640]{2,1,0:T(8,128)(2,1)S(1)} collective-permute-done((bf16[2,128,640]{2,1,0:T(8,128)(2,1)S(1)}, bf16[2,128,640]{2,1,0:T(8,128)(2,1)S(1)}, u32[]{:S(2)}, u32[]{:S(2)}) %collective-permute-start.17) | collective-permute-done | bytes 327712 | tf_op jit(solution)/shard_map/ppermute | solution.py:260
  89.0 1.9 pad_maximum_fusion.1
  90.9 3.2 %collective-permute-start.21 = (bf16[1,128,640]{2,1,0:T(8,128)(2,1)S(1)}, bf16[1,128,640]{2,1,0:T(8,128)(2,1)S(1)}, u32[]{:S(2)}, u32[]{:S(2)}) collective-permute-start(bf16[1,128,640]{2,1,0:T(8,128)(2,1)S(1)} %slice.205), channel_id=1, source_target_pairs={{0,24},{4,28},{8,16},{12,20},{16,8},{20,12},{24,0},{28,4},{1,25},{... | collective-permute-start | bytes 491528 | tf_op jit(solution)/shard_map/ppermute | solution.py:260
  94.1 3.8 %collective-permute-start.20 = (bf16[1,128,640]{2,1,0:T(8,128)(2,1)S(1)}, bf16[1,128,640]{2,1,0:T(8,128)(2,1)S(1)}, u32[]{:S(2)}, u32[]{:S(2)}) collective-permute-start(bf16[1,128,640]{2,1,0:T(8,128)(2,1)S(1)} %slice.205), channel_id=1, source_target_pairs={{0,16},{4,20},{8,24},{12,28},{16,0},{20,4},{24,8},{28,12},{1,17},{... | collective-permute-start | bytes 491528 | tf_op jit(solution)/shard_map/ppermute | solution.py:260
  98.5 10.4 %attn_forward.1 = (bf16[128,1024]{1,0:T(8,128)(2,1)}, bf16[128,1280]{1,0:T(8,128)(2,1)}, bf16[128,384]{1,0:T(8,128)(2,1)}, f32[128,15]{1,0:T(8,128)}, bf16[128,1...) custom-call(s32[1]{0:T(128)} %bitcast.2.place_ref, ...), custom_call_target="tpu_custom_call" | custom-call | flops 1000 | bytes 1000 | tf_op jit(solution)/shard_map/attn_forward/pallas_call | solution.py:465
  110.2 5.5 %collective-permute-done.15 = bf16[128,1024]{1,0:T(8,128)(2,1)S(1)} collective-permute-done((bf16[128,1024]{1,0:T(8,128)(2,1)}, bf16[128,1024]{1,0:T(8,128)(2,1)S(1)}, u32[]{:S(2)}, u32[]{:S(2)}) %collective-permute-start.15) | collective-permute-done | bytes 262176 | tf_op jit(solution)/shard_map/ppermute | solution.py:260
  123.4 10.3 %collective-permute-done.22 = bf16[4,1,128,640]{3,2,1,0:T(8,128)(2,1)S(1)} collective-permute-done((bf16[4,1,128,640]{3,2,1,0:T(8,128)(2,1)S(1)}, bf16[4,1,128,640]{3,2,1,0:T(8,128)(2,1)S(1)}, u32[]{:S(2)}, u32[]{:S(2)}) %collective-permute-start.22) | collective-permute-done | bytes 655392 | tf_op jit(solution)/shard_map/ppermute | solution.py:260
  143.9 6.8 %collective-permute-done.24.grad_b_ref = bf16[128,1024]{1,0:T(8,128)(2,1)S(1)} collective-permute-done((bf16[128,1024]{1,0:T(8,128)(2,1)S(1)}, bf16[128,1024]{1,0:T(8,128)(2,1)S(1)}, u32[]{:S(2)}, u32[]{:S(2)}) %collective-permute-start.24) | collective-permute-done | bytes 262176 | tf_op jit(solution)/shard_map/ppermute | solution.py:260
  151.8 4.1 %collective-permute-start.46 = (bf16[1,128,640]{2,1,0:T(8,128)(2,1)S(1)}, bf16[1,128,640]{2,1,0:T(8,128)(2,1)S(1)}, u32[]{:S(2)}, u32[]{:S(2)}) collective-permute-start(bf16[1,128,640]{2,1,0:T(8,128)(2,1)S(1)} %get-tuple-element.151), channel_id=1, source_target_pairs={{0,8},{4,12},{8,0},{12,4},{16,24},{20,28},{24,16},{28,20},{1,9},{5... | collective-permute-start | bytes 491528 | tf_op jit(solution)/shard_map/ppermute | solution.py:260
  156.2 2.2 collective-permute-start.48
  158.3 11.8 %attn_backward.1 = (bf16[1024,1280]{1,0:T(8,128)(2,1)}, bf16[1024,1280]{1,0:T(8,128)(2,1)}, f32[128,1024]{1,0:T(8,128)}) custom-call(s32[1]{0:T(128)} %bitcast.2.place_ref, bf16[128,1024]{1,0:T(8,128)(2,1)} %get-tuple-element.156.grad_a_ref, bf16[128,1024]{1,0:T(8,128)(2,1)} %copy-done.17, bf16[128,1024]{1,0:T(8,128)(2,1)} %bitcast.296, ...), custom_call_target="tpu_custom_call" | custom-call | flops 1000 | bytes 1000 | tf_op jit(solution)/shard_map/attn_backward/pallas_call | solution.py:465
  170.2 2.6 %dynamic-slice_bitcast_fusion = bf16[2,4,2,32,1280]{4,3,2,1,0:T(8,128)(2,1)} fusion(bf16[2,4,2,2,32,1280]{5,4,3,2,1,0:T(8,128)(2,1)} %bitcast.272, s32[]{:T(128)S(6)} %select_n.357), kind=kLoop, calls=%fused_computation.41 | loop fusion | bytes 2621444 | tf_op jit(solution)/shard_map/jit(dynamic_index_in_dim)/squeeze | solution.py:272
  173.0 2.7 %fusion = f32[128,960]{0,1:T(8,128)} fusion(f32[128,1024]{1,0:T(8,128)S(1)} %copy-done.21, s32[1024]{0:T(1024)S(1)} %fusion.57), kind=kOutput, calls=%fused_computation.1 | convolution fusion | flops 1510932480 | bytes 1019904 | tf_op jit(solution)/shard_map/dot_general | solution.py:627
  187.8 2.2 collective-permute-start.42
  197.7 9.6 %collective-permute-done.34 = bf16[4,2,32,1280]{3,2,1,0:T(8,128)(2,1)S(1)} collective-permute-done((bf16[4,2,32,1280]{3,2,1,0:T(8,128)(2,1)S(1)}, bf16[4,2,32,1280]{3,2,1,0:T(8,128)(2,1)S(1)}, u32[]{:S(2)}, u32[]{:S(2)}) %collective-permute-start.34) | collective-permute-done | bytes 655392 | tf_op jit(solution)/shard_map/ppermute | solution.py:260
  207.4 2.8 %collective-permute-done.28 = bf16[2,4,32,1280]{3,2,1,0:T(8,128)(2,1)S(1)} collective-permute-done((bf16[2,4,32,1280]{3,2,1,0:T(8,128)(2,1)S(1)}, bf16[2,4,32,1280]{3,2,1,0:T(8,128)(2,1)S(1)}, u32[]{:S(2)}, u32[]{:S(2)}) %collective-permute-start.28) | collective-permute-done | bytes 655392 | tf_op jit(solution)/shard_map/ppermute | solution.py:260
  210.5 2.2 collective-permute-done.41
  217.3 4.2 %collective-permute-done.44 = bf16[2,32,1280]{2,1,0:T(8,128)(2,1)S(1)} collective-permute-done((bf16[2,32,1280]{2,1,0:T(8,128)(2,1)S(1)}, bf16[2,32,1280]{2,1,0:T(8,128)(2,1)S(1)}, u32[]{:S(2)}, u32[]{:S(2)}) %collective-permute-start.44) | collective-permute-done | bytes 163872 | tf_op jit(solution)/shard_map/ppermute | solution.py:260
  221.6 6.2 %collective-permute-done.35 = bf16[4,32,1280]{2,1,0:T(8,128)(2,1)S(1)} collective-permute-done((bf16[4,32,1280]{2,1,0:T(8,128)(2,1)S(1)}, bf16[4,32,1280]{2,1,0:T(8,128)(2,1)S(1)}, u32[]{:S(2)}, u32[]{:S(2)}) %collective-permute-start.35) | collective-permute-done | bytes 327712 | tf_op jit(solution)/shard_map/ppermute | solution.py:260
  227.9 6.1 %collective-permute-start.36 = (bf16[32,1280]{1,0:T(8,128)(2,1)S(1)}, bf16[32,1280]{1,0:T(8,128)(2,1)S(1)}, u32[]{:S(2)}, u32[]{:S(2)}) collective-permute-start(bf16[32,1280]{1,0:T(8,128)(2,1)S(1)} %get-tuple-element.175), channel_id=1, source_target_pairs={{0,8},{4,12},{8,0},{12,4},{16,24},{20,28},{24,16},{28,20},{1,9},{5... | collective-permute-start | bytes 245768 | tf_op jit(solution)/shard_map/ppermute | solution.py:260
  234.2 2.2 collective-permute-start.38
  238.8 2.2 collective-permute-start.32
  243.8 5.7 %collective-permute-done.31 = bf16[32,1280]{1,0:T(8,128)(2,1)S(1)} collective-permute-done((bf16[32,1280]{1,0:T(8,128)(2,1)S(1)}, bf16[32,1280]{1,0:T(8,128)(2,1)S(1)}, u32[]{:S(2)}, u32[]{:S(2)}) %collective-permute-start.31) | collective-permute-done | bytes 81952 | tf_op jit(solution)/shard_map/ppermute | solution.py:260
  (246 shorter events, 89.6 us)
Async XLA Ops:
  2.8 21.5 %collective-permute-start.2 = (bf16[32,2560]{1,0:T(8,128)(2,1)S(1)}, bf16[32,2560]{1,0:T(8,128)(2,1)S(1)}, u32[]{:S(2)}, u32[]{:S(2)}) collective-permute-start(bf16[32,2560]{1,0:T(8,128)(2,1)S(1)} %scatter.4), channel_id=1, source_target_pairs={{0,24},{4,28},{8,16},{12,20},{16,8},{20,12},{24,0},{28,4},{1,25},{... | collective-permute-start | bytes 491528 | tf_op jit(solution)/shard_map/ppermute | solution.py:260
  7.9 16.4 %collective-permute-start.1 = (bf16[32,2560]{1,0:T(8,128)(2,1)S(1)}, bf16[32,2560]{1,0:T(8,128)(2,1)S(1)}, u32[]{:S(2)}, u32[]{:S(2)}) collective-permute-start(bf16[32,2560]{1,0:T(8,128)(2,1)S(1)} %scatter.4), channel_id=1, source_target_pairs={{0,16},{4,20},{8,24},{12,28},{16,0},{20,4},{24,8},{28,12},{1,17},{... | collective-permute-start | bytes 491528 | tf_op jit(solution)/shard_map/ppermute | solution.py:260
  7.9 16.4 %collective-permute-start = (bf16[32,2560]{1,0:T(8,128)(2,1)S(1)}, bf16[32,2560]{1,0:T(8,128)(2,1)S(1)}, u32[]{:S(2)}, u32[]{:S(2)}) collective-permute-start(bf16[32,2560]{1,0:T(8,128)(2,1)S(1)} %scatter.4), channel_id=1, source_target_pairs={{0,8},{4,12},{8,0},{12,4},{16,24},{20,28},{24,16},{28,20},{1,9},{5... | collective-permute-start | bytes 491528 | tf_op jit(solution)/shard_map/ppermute | solution.py:260
  47.5 14.7 %collective-permute-start.10 = (bf16[2,4,32,1280]{3,2,1,0:T(8,128)(2,1)S(1)}, bf16[2,4,32,1280]{3,2,1,0:T(8,128)(2,1)S(1)}, u32[]{:S(2)}, u32[]{:S(2)}) collective-permute-start(bf16[2,4,32,1280]{3,2,1,0:T(8,128)(2,1)S(1)} %pad_maximum_fusion.12), channel_id=1, source_target_pairs={{0,2},{1,3},{2,0},{3,1},{4,6},{5,7},{6,4},{7,5},{8,10},{9,11},{10,... | collective-permute-start | bytes 1966088 | tf_op jit(solution)/shard_map/ppermute | solution.py:260
  49.2 14.5 %collective-permute-start.11 = (bf16[4,2,32,1280]{3,2,0,1:T(8,128)(2,1)S(1)}, bf16[4,2,32,1280]{3,2,0,1:T(8,128)(2,1)S(1)}, u32[]{:S(2)}, u32[]{:S(2)}) collective-permute-start(bf16[4,2,32,1280]{3,2,0,1:T(8,128)(2,1)S(1)} %pad_maximum_fusion.13), channel_id=1, source_target_pairs={{0,4},{4,0},{8,12},{12,8},{16,20},{20,16},{24,28},{28,24},{1,5},{5... | collective-permute-start | bytes 1966088 | tf_op jit(solution)/shard_map/ppermute | solution.py:260
  49.8 15.2 %collective-permute-start.12 = (bf16[2,128,640]{2,1,0:T(8,128)(2,1)S(1)}, bf16[2,128,640]{2,1,0:T(8,128)(2,1)S(1)}, u32[]{:S(2)}, u32[]{:S(2)}) collective-permute-start(bf16[2,128,640]{2,1,0:T(8,128)(2,1)S(1)} %slice.204), channel_id=1, source_target_pairs={{0,16},{4,20},{8,24},{12,28},{16,0},{20,4},{24,8},{28,12},{1,17},{... | collective-permute-start | bytes 983048 | tf_op jit(solution)/shard_map/ppermute | solution.py:260
  65.1 20.1 %collective-permute-start.13 = (bf16[2,4,2,32,1280]{4,3,2,1,0:T(8,128)(2,1)S(1)}, bf16[2,4,2,32,1280]{4,3,2,1,0:T(8,128)(2,1)}, u32[]{:S(2)}, u32[]{:S(2)}) collective-permute-start(bf16[2,4,2,32,1280]{4,3,2,1,0:T(8,128)(2,1)S(1)} %pad_maximum_fusion.3), channel_id=1, source_target_pairs={{0,1},{1,0},{2,3},{3,2},{4,5},{5,4},{6,7},{7,6},{8,9},{9,8},{10,11... | collective-permute-start | bytes 3932168 | tf_op jit(solution)/shard_map/ppermute | solution.py:260
  66.9 19.9 %collective-permute-start.14 = (bf16[2,4,2,32,1280]{4,3,2,1,0:T(8,128)(2,1)S(1)}, bf16[2,4,2,32,1280]{4,3,2,1,0:T(8,128)(2,1)}, u32[]{:S(2)}, u32[]{:S(2)}) collective-permute-start(bf16[2,4,2,32,1280]{4,3,2,1,0:T(8,128)(2,1)S(1)} %copy.50), channel_id=1, source_target_pairs={{0,1},{1,0},{2,3},{3,2},{4,5},{5,4},{6,7},{7,6},{8,9},{9,8},{10,11... | collective-permute-start | bytes 3932168 | tf_op jit(solution)/shard_map/ppermute | solution.py:260
  70.0 11.5 %collective-permute-start.17 = (bf16[2,128,640]{2,1,0:T(8,128)(2,1)S(1)}, bf16[2,128,640]{2,1,0:T(8,128)(2,1)S(1)}, u32[]{:S(2)}, u32[]{:S(2)}) collective-permute-start(bf16[2,128,640]{2,1,0:T(8,128)(2,1)S(1)} %slice.204), channel_id=1, source_target_pairs={{0,24},{4,28},{8,16},{12,20},{16,8},{20,12},{24,0},{28,4},{1,25},{... | collective-permute-start | bytes 983048 | tf_op jit(solution)/shard_map/ppermute | solution.py:260
  83.7 32.4 %collective-permute-start.18 = (bf16[4,2,128,640]{3,2,0,1:T(8,128)(2,1)}, bf16[4,2,128,640]{3,2,0,1:T(8,128)(2,1)}, u32[]{:S(2)}, u32[]{:S(2)}) collective-permute-start(bf16[4,2,128,640]{3,2,0,1:T(8,128)(2,1)} %copy.39), channel_id=1, source_target_pairs={{0,4},{4,0},{8,12},{12,8},{16,20},{20,16},{24,28},{28,24},{1,5},{5... | collective-permute-start | bytes 3932168 | tf_op jit(solution)/shard_map/ppermute | solution.py:260
  90.9 19.2 %collective-permute-start.21 = (bf16[1,128,640]{2,1,0:T(8,128)(2,1)S(1)}, bf16[1,128,640]{2,1,0:T(8,128)(2,1)S(1)}, u32[]{:S(2)}, u32[]{:S(2)}) collective-permute-start(bf16[1,128,640]{2,1,0:T(8,128)(2,1)S(1)} %slice.205), channel_id=1, source_target_pairs={{0,24},{4,28},{8,16},{12,20},{16,8},{20,12},{24,0},{28,4},{1,25},{... | collective-permute-start | bytes 491528 | tf_op jit(solution)/shard_map/ppermute | solution.py:260
  94.1 16.0 %collective-permute-start.20 = (bf16[1,128,640]{2,1,0:T(8,128)(2,1)S(1)}, bf16[1,128,640]{2,1,0:T(8,128)(2,1)S(1)}, u32[]{:S(2)}, u32[]{:S(2)}) collective-permute-start(bf16[1,128,640]{2,1,0:T(8,128)(2,1)S(1)} %slice.205), channel_id=1, source_target_pairs={{0,16},{4,20},{8,24},{12,28},{16,0},{20,4},{24,8},{28,12},{1,17},{... | collective-permute-start | bytes 491528 | tf_op jit(solution)/shard_map/ppermute | solution.py:260
  97.9 12.2 %collective-permute-start.19 = (bf16[1,128,640]{2,1,0:T(8,128)(2,1)S(1)}, bf16[1,128,640]{2,1,0:T(8,128)(2,1)S(1)}, u32[]{:S(2)}, u32[]{:S(2)}) collective-permute-start(bf16[1,128,640]{2,1,0:T(8,128)(2,1)S(1)} %slice.205), channel_id=1, source_target_pairs={{0,8},{4,12},{8,0},{12,4},{16,24},{20,28},{24,16},{28,20},{1,9},{5... | collective-permute-start | bytes 491528 | tf_op jit(solution)/shard_map/ppermute | solution.py:260
  116.1 17.6 %collective-permute-start.22 = (bf16[4,1,128,640]{3,2,1,0:T(8,128)(2,1)S(1)}, bf16[4,1,128,640]{3,2,1,0:T(8,128)(2,1)S(1)}, u32[]{:S(2)}, u32[]{:S(2)}) collective-permute-start(bf16[4,1,128,640]{3,2,1,0:T(8,128)(2,1)S(1)} %pad_maximum_fusion.14), channel_id=1, source_target_pairs={{0,4},{4,0},{8,12},{12,8},{16,20},{20,16},{24,28},{28,24},{1,5},{5... | collective-permute-start | bytes 1966088 | tf_op jit(solution)/shard_map/ppermute | solution.py:260
  122.1 29.5 %collective-permute-start.45 = (bf16[1,4,128,640]{3,2,1,0:T(8,128)(2,1)S(1)}, bf16[1,4,128,640]{3,2,1,0:T(8,128)(2,1)S(1)}, u32[]{:S(2)}, u32[]{:S(2)}) collective-permute-start(bf16[1,4,128,640]{3,2,1,0:T(8,128)(2,1)S(1)} %slice_bitcast_fusion), channel_id=1, source_target_pairs={{0,4},{4,0},{8,12},{12,8},{16,20},{20,16},{24,28},{28,24},{1,5},{5... | collective-permute-start | bytes 1966088 | tf_op jit(solution)/shard_map/ppermute | solution.py:260
  140.5 43.2 %collective-permute-start.39 = (bf16[2,4,128,640]{3,2,1,0:T(8,128)(2,1)}, bf16[2,4,128,640]{3,2,1,0:T(8,128)(2,1)}, u32[]{:S(2)}, u32[]{:S(2)}) collective-permute-start(bf16[2,4,128,640]{3,2,1,0:T(8,128)(2,1)} %fusion.13), channel_id=1, source_target_pairs={{0,4},{4,0},{8,12},{12,8},{16,20},{20,16},{24,28},{28,24},{1,5},{5... | collective-permute-start | bytes 3932168 | tf_op jit(solution)/shard_map/ppermute | solution.py:260
  151.5 30.0 %collective-permute-start.25 = (bf16[256,1024]{1,0:T(8,128)(2,1)}, bf16[256,1024]{1,0:T(8,128)(2,1)}, u32[]{:S(2)}, u32[]{:S(2)}) collective-permute-start(bf16[256,1024]{1,0:T(8,128)(2,1)} %slice.303), channel_id=1, source_target_pairs={{0,1},{1,0},{2,3},{3,2},{4,5},{5,4},{6,7},{7,6},{8,9},{9,8},{10,11... | collective-permute-start | bytes 1572872 | tf_op jit(solution)/shard_map/ppermute | solution.py:260
  151.8 21.0 %collective-permute-start.46 = (bf16[1,128,640]{2,1,0:T(8,128)(2,1)S(1)}, bf16[1,128,640]{2,1,0:T(8,128)(2,1)S(1)}, u32[]{:S(2)}, u32[]{:S(2)}) collective-permute-start(bf16[1,128,640]{2,1,0:T(8,128)(2,1)S(1)} %get-tuple-element.151), channel_id=1, source_target_pairs={{0,8},{4,12},{8,0},{12,4},{16,24},{20,28},{24,16},{28,20},{1,9},{5... | collective-permute-start | bytes 491528 | tf_op jit(solution)/shard_map/ppermute | solution.py:260
  155.9 16.9 %collective-permute-start.47 = (bf16[1,128,640]{2,1,0:T(8,128)(2,1)S(1)}, bf16[1,128,640]{2,1,0:T(8,128)(2,1)S(1)}, u32[]{:S(2)}, u32[]{:S(2)}) collective-permute-start(bf16[1,128,640]{2,1,0:T(8,128)(2,1)S(1)} %get-tuple-element.150), channel_id=1, source_target_pairs={{0,16},{4,20},{8,24},{12,28},{16,0},{20,4},{24,8},{28,12},{1,17},{... | collective-permute-start | bytes 491528 | tf_op jit(solution)/shard_map/ppermute | solution.py:260
  156.2 16.6 %collective-permute-start.48 = (bf16[1,128,640]{2,1,0:T(8,128)(2,1)S(1)}, bf16[1,128,640]{2,1,0:T(8,128)(2,1)S(1)}, u32[]{:S(2)}, u32[]{:S(2)}) collective-permute-start(bf16[1,128,640]{2,1,0:T(8,128)(2,1)S(1)} %get-tuple-element.149), channel_id=1, source_target_pairs={{0,24},{4,28},{8,16},{12,20},{16,8},{20,12},{24,0},{28,4},{1,25},{... | collective-permute-start | bytes 491528 | tf_op jit(solution)/shard_map/ppermute | solution.py:260
  175.7 12.1 %collective-permute-start.33 = (bf16[2,4,2,32,1280]{4,3,2,1,0:T(8,128)(2,1)}, bf16[2,4,2,32,1280]{4,3,2,1,0:T(8,128)(2,1)}, u32[]{:S(2)}, u32[]{:S(2)}) collective-permute-start(bf16[2,4,2,32,1280]{4,3,2,1,0:T(8,128)(2,1)} %dynamic-slice_bitcast_fusion), channel_id=1, source_target_pairs={{0,1},{1,0},{2,3},{3,2},{4,5},{5,4},{6,7},{7,6},{8,9},{9,8},{10,11... | collective-permute-start | bytes 3932168 | tf_op jit(solution)/shard_map/ppermute | solution.py:260
  179.4 12.2 %collective-permute-start.27 = (bf16[2,4,2,32,1280]{4,3,1,0,2:T(8,128)(2,1)}, bf16[2,4,2,32,1280]{4,3,1,0,2:T(8,128)(2,1)}, u32[]{:S(2)}, u32[]{:S(2)}) collective-permute-start(bf16[2,4,2,32,1280]{4,3,1,0,2:T(8,128)(2,1)} %bitcast.253), channel_id=1, source_target_pairs={{0,1},{1,0},{2,3},{3,2},{4,5},{5,4},{6,7},{7,6},{8,9},{9,8},{10,11... | collective-permute-start | bytes 3932168 | tf_op jit(solution)/shard_map/ppermute | solution.py:260
  183.0 11.7 %collective-permute-start.26 = (bf16[128,1024]{1,0:T(8,128)(2,1)S(1)}, bf16[128,1024]{1,0:T(8,128)(2,1)S(1)}, u32[]{:S(2)}, u32[]{:S(2)}) collective-permute-start(bf16[128,1024]{1,0:T(8,128)(2,1)S(1)} %slice.305), channel_id=1, source_target_pairs={{0,2},{1,3},{2,0},{3,1},{4,6},{5,7},{6,4},{7,5},{8,10},{9,11},{10,... | collective-permute-start | bytes 786440 | tf_op jit(solution)/shard_map/ppermute | solution.py:260
  185.5 25.0 %collective-permute-start.40 = (bf16[2,128,640]{2,1,0:T(8,128)(2,1)S(1)}, bf16[2,128,640]{2,1,0:T(8,128)(2,1)S(1)}, u32[]{:S(2)}, u32[]{:S(2)}) collective-permute-start(bf16[2,128,640]{2,1,0:T(8,128)(2,1)S(1)} %get-tuple-element.136), channel_id=1, source_target_pairs={{0,8},{4,12},{8,0},{12,4},{16,24},{20,28},{24,16},{28,20},{1,9},{5... | collective-permute-start | bytes 983048 | tf_op jit(solution)/shard_map/ppermute | solution.py:260
  187.0 25.6 %collective-permute-start.41 = (bf16[2,128,640]{2,1,0:T(8,128)(2,1)S(1)}, bf16[2,128,640]{2,1,0:T(8,128)(2,1)S(1)}, u32[]{:S(2)}, u32[]{:S(2)}) collective-permute-start(bf16[2,128,640]{2,1,0:T(8,128)(2,1)S(1)} %get-tuple-element.138), channel_id=1, source_target_pairs={{0,16},{4,20},{8,24},{12,28},{16,0},{20,4},{24,8},{28,12},{1,17},{... | collective-permute-start | bytes 983048 | tf_op jit(solution)/shard_map/ppermute | solution.py:260
  187.8 24.9 %collective-permute-start.42 = (bf16[2,128,640]{2,1,0:T(8,128)(2,1)S(1)}, bf16[2,128,640]{2,1,0:T(8,128)(2,1)S(1)}, u32[]{:S(2)}, u32[]{:S(2)}) collective-permute-start(bf16[2,128,640]{2,1,0:T(8,128)(2,1)S(1)} %get-tuple-element.135), channel_id=1, source_target_pairs={{0,24},{4,28},{8,16},{12,20},{16,8},{20,12},{24,0},{28,4},{1,25},{... | collective-permute-start | bytes 983048 | tf_op jit(solution)/shard_map/ppermute | solution.py:260
  191.7 15.6 %collective-permute-start.34 = (bf16[4,2,32,1280]{3,2,1,0:T(8,128)(2,1)S(1)}, bf16[4,2,32,1280]{3,2,1,0:T(8,128)(2,1)S(1)}, u32[]{:S(2)}, u32[]{:S(2)}) collective-permute-start(bf16[4,2,32,1280]{3,2,1,0:T(8,128)(2,1)S(1)} %slice_bitcast_fusion.2), channel_id=1, source_target_pairs={{0,4},{4,0},{8,12},{12,8},{16,20},{20,16},{24,28},{28,24},{1,5},{5... | collective-permute-start | bytes 1966088 | tf_op jit(solution)/shard_map/ppermute | solution.py:260
  194.7 15.6 %collective-permute-start.28 = (bf16[2,4,32,1280]{3,2,1,0:T(8,128)(2,1)S(1)}, bf16[2,4,32,1280]{3,2,1,0:T(8,128)(2,1)S(1)}, u32[]{:S(2)}, u32[]{:S(2)}) collective-permute-start(bf16[2,4,32,1280]{3,2,1,0:T(8,128)(2,1)S(1)} %dynamic-slice_bitcast_fusion.1), channel_id=1, source_target_pairs={{0,2},{1,3},{2,0},{3,1},{4,6},{5,7},{6,4},{7,5},{8,10},{9,11},{10,... | collective-permute-start | bytes 1966088 | tf_op jit(solution)/shard_map/ppermute | solution.py:260
  215.9 11.9 %collective-permute-start.35 = (bf16[4,32,1280]{2,1,0:T(8,128)(2,1)S(1)}, bf16[4,32,1280]{2,1,0:T(8,128)(2,1)S(1)}, u32[]{:S(2)}, u32[]{:S(2)}) collective-permute-start(bf16[4,32,1280]{2,1,0:T(8,128)(2,1)S(1)} %dynamic-slice_bitcast_fusion.2), channel_id=1, source_target_pairs={{0,2},{1,3},{2,0},{3,1},{4,6},{5,7},{6,4},{7,5},{8,10},{9,11},{10,... | collective-permute-start | bytes 983048 | tf_op jit(solution)/shard_map/ppermute | solution.py:260
  216.6 19.8 %collective-permute-start.29 = (bf16[4,32,1280]{2,1,0:T(8,128)(2,1)S(1)}, bf16[4,32,1280]{2,1,0:T(8,128)(2,1)S(1)}, u32[]{:S(2)}, u32[]{:S(2)}) collective-permute-start(bf16[4,32,1280]{2,1,0:T(8,128)(2,1)S(1)} %slice_bitcast_fusion.12), channel_id=1, source_target_pairs={{0,4},{4,0},{8,12},{12,8},{16,20},{20,16},{24,28},{28,24},{1,5},{5... | collective-permute-start | bytes 983048 | tf_op jit(solution)/shard_map/ppermute | solution.py:260
  227.9 10.9 %collective-permute-start.36 = (bf16[32,1280]{1,0:T(8,128)(2,1)S(1)}, bf16[32,1280]{1,0:T(8,128)(2,1)S(1)}, u32[]{:S(2)}, u32[]{:S(2)}) collective-permute-start(bf16[32,1280]{1,0:T(8,128)(2,1)S(1)} %get-tuple-element.175), channel_id=1, source_target_pairs={{0,8},{4,12},{8,0},{12,4},{16,24},{20,28},{24,16},{28,20},{1,9},{5... | collective-permute-start | bytes 245768 | tf_op jit(solution)/shard_map/ppermute | solution.py:260
  237.6 11.8 %collective-permute-start.31 = (bf16[32,1280]{1,0:T(8,128)(2,1)S(1)}, bf16[32,1280]{1,0:T(8,128)(2,1)S(1)}, u32[]{:S(2)}, u32[]{:S(2)}) collective-permute-start(bf16[32,1280]{1,0:T(8,128)(2,1)S(1)} %get-tuple-element.170), channel_id=1, source_target_pairs={{0,16},{4,20},{8,24},{12,28},{16,0},{20,4},{24,8},{28,12},{1,17},{... | collective-permute-start | bytes 245768 | tf_op jit(solution)/shard_map/ppermute | solution.py:260
  (41 other events, 239.1 us)

commit v2 on v1

--- a/solution.py
+++ b/solution.py
@@ -260,12 +260,22 @@
     return lax.ppermute(value, axis, [(i, i ^ bit) for i in range(lax.axis_size(axis))])
 
 
+def meet(*values):
+    return lax.optimization_barrier(values)
+
+
 def after(value, *done):
     return lax.optimization_barrier((value, *done))[0]
 
 
 def add2(kept, came):
     return (kept.astype(F32) + came.astype(F32)).astype(BF)
+
+
+def far_pair(value, axis, odd):
+    shape = value.shape
+    value = value.reshape(shape[:axis] + (shape[axis] // 2, 2) + shape[axis + 1 :])
+    return lax.index_in_dim(value, odd, axis + 1, keepdims=False)
 
 
 def pick(value, index, axis):
@@ -326,23 +336,35 @@
     return place == group, place == group + n_fsdp // 2
 
 
-def slot_matrix(owner, inner, own, share):
-    per = share // own
+def slot_matrix(owner, inner, own, height):
+    per = D * 2 // 8 // own
     slot = jnp.where(inner < own, owner % per * own + inner, -1)
-    return (lax.broadcasted_iota(jnp.int32, (share, owner.shape[1]), 0) == slot).astype(F32).astype(BF)
-
-
-def make_forward(n_fsdp, own, padded, share):
+    return (lax.broadcasted_iota(jnp.int32, (height, owner.shape[1]), 0) == slot).astype(F32).astype(BF)
+
+
+def make_forward(n_fsdp, own, padded, share, by_fsdp):
     kv_width = KV * HD
 
     def kernel(
-        place_ref, rows_ref, pieces_ref, owner_ref, inner_ref, cos_ref, sin_ref, seg_ref,
-        attn_q_ref, attn_o_ref,
-        input1_ref, qk_ref, v_ref, logsum_ref, att_ref, hidden1_ref, input2_ref, gains_ref,
+        place_ref, rows_ref, owner_ref, inner_ref, cos_ref, sin_ref, seg_ref,
+        own_q_ref, came_q_ref, own_o_ref, came_o_ref,
+        input1_ref, qk_ref, v_ref, logsum_ref, att_ref, hidden1_ref, input2_ref, gains_ref, attn_q_ref, attn_o_ref,
     ):
+        core = place_ref[1]
+        for p in range(own_q_ref.shape[0] // padded):
+            here = pl.ds(pl.multiple_of((2 * p + core) * padded, padded), padded)
+            there = pl.ds(pl.multiple_of((2 * p + 1 - core) * padded, padded), padded)
+            block = slice(p * padded, (p + 1) * padded)
+            attn_q_ref[here, :] = own_q_ref[block, :]
+            attn_q_ref[there, :] = came_q_ref[block, :]
+            attn_o_ref[here, :] = own_o_ref[block, :]
+            attn_o_ref[there, :] = came_o_ref[block, :]
+        pieces = jnp.concatenate(
+            [attn_q_ref[p * padded + own : p * padded + own + 1, :share].astype(F32) for p in by_fsdp], axis=0
+        ).astype(BF)
         owner = owner_ref[...]
         first, second = gain_masks(owner, place_ref[0], n_fsdp, own, share)
-        spots = dot_f(pieces_ref[...], slot_matrix(owner, inner_ref[...], own, share))
+        spots = dot_f(pieces, slot_matrix(owner, inner_ref[...], own, share))
         gain1 = jnp.sum(jnp.where(first, spots, 0.0), axis=0, keepdims=True)
         gain2 = jnp.sum(jnp.where(second, spots, 0.0), axis=0, keepdims=True)
         gains_ref[0:1, :] = gain1
@@ -396,6 +418,7 @@
     ):
         count = rows_ref.shape[0]
         wide = rows_ref.shape[1]
+        core = place_ref[1]
         gain1 = gains_ref[0:1, :]
         gain2 = gains_ref[1:2, :]
         grad_in2 = grad_a_ref[...].astype(F32) + grad_b_ref[...].astype(F32)
@@ -438,7 +461,7 @@
             turned = jnp.where(low, pltpu.roll(scaled, 96, 1), -pltpu.roll(scaled, 32, 1))
             pieces.append((part * cosine + turned).astype(BF))
         proj_grad = jnp.concatenate(pieces, axis=1)
-        o_term_ref[...] = dot_0(left_ref[...], right_ref[...]).astype(BF)
+        o_term = dot_0(left_ref[...], right_ref[...]).astype(BF)
         owner = owner_ref[...]
         inner = inner_ref[...]
         grad_in1 = dot_t(proj_grad, attn_q_ref[...]) * jnp.where(inner < own, 1.0, 0.0) + dot_t(
@@ -449,10 +472,17 @@
         input_grad_ref[...] = grad_h1 + back1
         first, second = gain_masks(owner, place_ref[0], n_fsdp, own, share)
         both = jnp.where(first, gain1_term, 0.0) + jnp.where(second, gain2_term, 0.0)
-        gain_rows = dot_t(both.astype(BF), slot_matrix(owner, inner, own, share)).astype(BF)
+        gain_rows = dot_t(both.astype(BF), slot_matrix(owner, inner, own, 256)).astype(BF)
         q_term = dot_0(input1_ref[...], proj_grad)
-        q_term_ref[...] = q_term.astype(BF)
-        q_term_ref[:, :share] = (q_term[:, :share] + dot_f(spots_ref[...], gain_rows)).astype(BF)
+        q_start = (q_term[:, :256] + dot_f(spots_ref[...], gain_rows)).astype(BF)
+        q_term = q_term.astype(BF)
+        for p in range(wide // padded):
+            rel = p % 2 ^ core
+            block = slice(p * padded, (p + 1) * padded)
+            to = slice(p // 2 * padded, (p // 2 + 1) * padded)
+            q_term_ref[rel, to, :256] = q_start[block, :]
+            q_term_ref[rel, to, 256:] = q_term[block, 256:]
+            o_term_ref[rel, to, :] = o_term[block, :]
 
     return kernel
 
@@ -503,9 +533,6 @@
     def padded_block(flat):
         return jnp.pad(flat.reshape(own, FF), ((0, padded - own), (0, 0)))
 
-    def far_gather(block):
-        return jnp.stack([block] + [swap(block, "fsdp", 2 * k) for k in range(1, n_far)], axis=0)
-
     def columns(value, index, width):
         return lax.dynamic_slice_in_dim(value, index * width, width, axis=value.ndim - 1)
 
@@ -517,59 +544,59 @@
     rows32 = mm(rows, spread_mat)
     grad_outb = (live * mm(cotangent, spread_mat)).astype(BF)
 
-    def group_tokens(value):
-        value = jnp.stack([value, swap(value, "sub", 2)])
-        return jnp.stack([value, swap(value, "sub", 1)]).reshape(4 * count, wide)
-
-    def group_half(value):
-        value = value.astype(BF).reshape(2, 2 * count, wide)
-        value = add2(value[0], swap(value[1], "sub", 1)).reshape(2, count, wide)
-        return value[0], swap(value[1], "sub", 2)
+    of_place = [(p // n_sub) % n_far * 2 + p // (n_sub * n_far) for p in range(n_all)]
+    at_spot = jnp.where(inner == own, jnp.array(of_place)[place], -1)
+    spots = (at_spot[:, None] == jnp.arange(n_fsdp)[None, :]).astype(BF)
+    owner = ((rel ^ my_fsdp) * n_sub + place % n_sub)[None, :]
 
     attn_block = padded_block(attn_weight)
     attn_block = attn_block.at[own, :share].set(gains)
-    attn_far = far_gather(attn_block)
+    far = [swap(attn_block, "fsdp", 2 * k) for k in range(1, n_far)]
     mlp_block = jnp.stack([padded_block(w) for w in (gate_weight, up_weight, down_weight)])
     came = swap(columns(mlp_block, 1 - my_y, half_ff), "sub", 2)
     mlp_block = put2(columns(mlp_block, my_y, half_ff), came, my_y, 1)
     came = swap(columns(mlp_block, 1 - my_c, quarter), "sub", 1)
     mlp_block = put2(columns(mlp_block, my_c, quarter), came, my_c, 2)
     mlp_block = mlp_block.reshape(3, n_sub * padded, quarter)
-    cot_all = group_tokens(grad_outb)
-    attn_far, mlp_block, cot_all = lax.optimization_barrier((attn_far, mlp_block, cot_all))
-
+    far, mlp_block = meet(far, mlp_block)
+
+    attn_far = jnp.stack([attn_block] + list(far))
     half0 = attn_far[:, :, :half_ff]
     half1 = attn_far[:, :, half_ff:]
-    gate_up = [mlp_block[:2]]
-    half0 = jnp.stack([half0, swap(half0, "fsdp", 1)])
-    half1 = put2(half1, swap(half1, "sub", 2), my_y, 1)
-    gate_up.append(swap(mlp_block[:2], "fsdp", 2))
-    half0, half1, gate_up = lax.optimization_barrier((half0, half1, gate_up))
-
-    gate_up = gate_up + [swap(gate_up[0], "fsdp", 2 * k) for k in range(2, 3)]
-    half0 = put2(half0, swap(half0, "sub", 2), my_y, 2)
-    half1 = jnp.stack([half1, swap(half1, "fsdp", 1)])
-    half0, half1, gate_up, down_w = lax.optimization_barrier((half0, half1, gate_up, mlp_block[2:]))
-
-    attn_q = put2(half0, swap(half0, "sub", 1), my_c, 3).reshape(wide, half_ff)
-    attn_o = put2(half1, swap(half1, "sub", 1), my_c, 3).reshape(wide, half_ff)
-    gate_up = gate_up + [swap(gate_up[0], "fsdp", 2 * k) for k in range(3, n_far)]
-    attn_q, attn_o, down_w = lax.optimization_barrier((attn_q, attn_o, down_w))
-    gate_up = jnp.stack(gate_up)
-    gate_up_came = swap(gate_up, "fsdp", 1)
-    down_w = far_gather(down_w)
-
-    by_fsdp = [(f % 2) * n_far * n_sub + (f // 2) * n_sub for f in range(n_fsdp)]
-    pieces = attn_q.reshape(n_all, padded, half_ff)
-    pieces = jnp.stack([pieces[p, own, :share] for p in by_fsdp])
-    my_place = my_fsdp.reshape(1)
-    owner = (((rel ^ my_fsdp) * n_sub + place % n_sub))[None, :]
+    gate_up = mlp_block[:2]
+    down = mlp_block[2]
+    x0, y1, near = swap(half0, "fsdp", 1), swap(half1, "sub", 2), swap(gate_up, "fsdp", 2)
     tables = (owner, inner[None, :])
     angles = (cosine, sine, seg)
-    sizes = (n_fsdp, own, padded, share)
+    half0, half1, gate_up, down, x0, y1, near, rows32, grad_outb, spots, tables, angles = meet(
+        half0, half1, gate_up, down, x0, y1, near, rows32, grad_outb, spots, tables, angles
+    )
+
+    half0 = jnp.stack([half0, x0])
+    half1 = put2(half1, y1, my_y, 1)
+    y0, x1, third = swap(half0, "sub", 2), swap(half1, "fsdp", 1), swap(gate_up, "fsdp", 4)
+    half0, half1, gate_up, down, near, y0, x1, third, grad_outb = meet(
+        half0, half1, gate_up, down, near, y0, x1, third, grad_outb
+    )
+
+    half0 = put2(half0, y0, my_y, 2).reshape(wide // 2, half_ff)
+    half1 = jnp.stack([half1, x1]).reshape(wide // 2, half_ff)
+    c0, c1, last = swap(half0, "sub", 1), swap(half1, "sub", 1), swap(third, "fsdp", 2)
+    down_x = swap(down, "fsdp", 1)
+    cot_y = swap(grad_outb, "sub", 2)
+    half0, half1, c0, c1, gate_up, near, third, last, down, down_x, cot_y = meet(
+        half0, half1, c0, c1, gate_up, near, third, last, down, down_x, cot_y
+    )
+
+    gate_up = jnp.stack([gate_up, near, third, last])
+    gate_up_x = swap(gate_up, "fsdp", 1)
+    down = jnp.stack([down, down_x])
+    down_far = swap(down, "fsdp", 4)
+    by_fsdp = [(f % 2) * n_far * n_sub + (f // 2) * n_sub for f in range(n_fsdp)]
+    my_place = jnp.stack([my_fsdp, my_c])
     tall = (count, wide)
     forward = run_kernel(
-        make_forward(*sizes),
+        make_forward(n_fsdp, own, padded, share, by_fsdp),
         [
             (tall, BF),
             ((count, half_ff), BF),
@@ -579,40 +606,57 @@
             (tall, F32),
             (tall, BF),
             ((2, wide), F32),
+            ((wide, half_ff), BF),
+            ((wide, half_ff), BF),
         ],
-        (my_place, rows32, pieces, *tables, *angles, attn_q, attn_o),
+        (my_place, rows32, *tables, *angles, half0, c0, half1, c1),
         name="attn_forward",
     )
-    input1, qk, values, logsum, attended, hidden1, input2, gains_p = forward
-    in2_all = group_tokens(input2)
-    gate_up_came = after(gate_up_came, input2)
-    gate_w = jnp.stack([gate_up[:, 0], gate_up_came[:, 0]]).reshape(wide, quarter)
-    up_w = jnp.stack([gate_up[:, 1], gate_up_came[:, 1]]).reshape(wide, quarter)
-    down_w = after(down_w, gate_up_came)
-    down_came = swap(down_w, "fsdp", 1)
+    input1, qk, values, logsum, attended, hidden1, input2, gains_p, attn_q, attn_o = forward
+
+    in2_y = swap(input2, "sub", 2)
+    input2, in2_y, down_far, cot_y = meet(input2, in2_y, down_far, cot_y)
+    down = jnp.stack([down, down_far])
+    down_near = swap(down, "fsdp", 2)
+    in2_all = jnp.stack([input2, in2_y])
+    cot_all = jnp.stack([grad_outb, cot_y])
+    in2_c, cot_c = swap(in2_all, "sub", 1), swap(cot_all, "sub", 1)
+    in2_c, cot_c, gate_up_x = meet(in2_c, cot_c, gate_up_x)
+    in2_all = jnp.stack([in2_all, in2_c]).reshape(4 * count, wide)
+    cot_all = jnp.stack([cot_all, cot_c]).reshape(4 * count, wide)
+    gate_w = jnp.stack([gate_up[:, 0], gate_up_x[:, 0]]).reshape(wide, quarter)
+    up_w = jnp.stack([gate_up[:, 1], gate_up_x[:, 1]]).reshape(wide, quarter)
     gate = mm(in2_all, gate_w)
     up = mm(in2_all, up_w)
     sigma = jax.nn.sigmoid(gate)
     active = gate * sigma
     hidden = (active * up).astype(BF)
-    down_came = after(down_came, hidden)
-    down_w = jnp.stack([down_w, down_came]).reshape(wide, quarter)
     down_term = term(cot_all, hidden)
+    down_near = after(down_near, hidden)
+    down_w = jnp.stack([down, down_near])
+    down_w = down_w.transpose(2, 1, 0, 3, 4).reshape(wide, quarter)
+    down_term = down_term.reshape(2, n_far, n_sub * padded, quarter)
+    down_x_came = swap(down_term[1], "fsdp", 1)
     grad_hidden = mm(cot_all, down_w)
     grad_gate = (grad_hidden * up * sigma * (1.0 + gate * (1.0 - sigma))).astype(BF)
     grad_up = (grad_hidden * active).astype(BF)
-    grad_in2 = group_half(mm_t(grad_gate, gate_w) + mm_t(grad_up, up_w))
-    gate_term = term(in2_all, grad_gate)
-    up_term = term(in2_all, grad_up)
-    result = group_half(after(mm_t(hidden, down_w), *grad_in2))
-    of_place = [(p // n_sub) % n_far * 2 + p // (n_sub * n_far) for p in range(n_all)]
-    at_spot = jnp.where(inner == own, jnp.array(of_place)[place], -1)
-    spots = (at_spot[:, None] == jnp.arange(n_fsdp)[None, :]).astype(BF)
+    grad_in2 = (mm_t(grad_gate, gate_w) + mm_t(grad_up, up_w)).astype(BF).reshape(2, 2 * count, wide)
+    gate_up_term = jnp.stack([term(in2_all, grad_gate), term(in2_all, grad_up)])
+    gate_up_term = gate_up_term.reshape(2, 2, n_far, n_sub * padded, quarter)
+    result = mm_t(hidden, down_w).astype(BF).reshape(2, 2 * count, wide)
+
+    came = swap(grad_in2[1], "sub", 1)
+    came, down_x_came = meet(came, down_x_came)
+    grad_in2 = add2(grad_in2[0], came).reshape(2, count, wide)
+    grad_in2_y = swap(grad_in2[1], "sub", 2)
+    gate_up_x_came = swap(gate_up_term[:, 1], "fsdp", 1)
+    down_held = add2(down_term[0], down_x_came)
+    down_near_came = swap(far_pair(down_held, 0, 1), "fsdp", 2)
     q_term, o_term, input_grad = run_kernel(
-        make_backward(*sizes),
-        [((wide, half_ff), BF), ((wide, half_ff), BF), (tall, F32)],
+        make_backward(n_fsdp, own, padded, share),
+        [((2, wide // 2, half_ff), BF), ((2, wide // 2, half_ff), BF), (tall, F32)],
         (
-            my_place, *grad_in2, grad_outb, hidden1, rows32, gains_p, *tables, spots, *angles,
+            my_place, grad_in2[0], grad_in2_y, grad_outb, hidden1, rows32, gains_p, *tables, spots, *angles,
             input1, qk, values, logsum, attended, attn_q, attn_o,
         ),
         scratch=[
@@ -622,24 +666,51 @@
         ],
         name="attn_backward",
     )
-    result = hidden1 + result[0].astype(F32) + result[1].astype(F32)
-    output = mm_t((live * result).astype(BF), spread_mat).astype(BF)
+
+    q_c, o_c = swap(q_term[1], "sub", 1), swap(o_term[1], "sub", 1)
+    res_c = swap(after(result[1], q_term), "sub", 1)
+    q_c, o_c, res_c, down_near_came, gate_up_x_came = meet(q_c, o_c, res_c, down_near_came, gate_up_x_came)
+
+    full = (2, n_far, 2, padded, half_ff)
+    q_held = add2(q_term[0], q_c).reshape(full)
+    o_held = add2(o_term[0], o_c).reshape(full)
+    q_y = swap(pick(q_held, 1 - my_y, 2), "sub", 2)
+    o_x = swap(o_held[1], "fsdp", 1)
+    gate_up_held = add2(gate_up_term[:, 0], gate_up_x_came)
+    gate_up_near = swap(far_pair(gate_up_held, 1, 1), "fsdp", 2)
+    down_held = add2(far_pair(down_held, 0, 0), down_near_came)
+    input_grad = after(input_grad, q_c)
     input_grad = lax.dot_general(
         input_grad,
         spread_mat.astype(F32),
         (((1,), (1,)), ((), ())),
         precision=lax.Precision.HIGHEST,
     )
-
-    def far_sum(held, axis, *done):
-        parts = [lax.index_in_dim(held, 0, axis, keepdims=False)]
-        for k in range(1, n_far):
-            parts.append(swap(lax.index_in_dim(held, k, axis, keepdims=False), "fsdp", 2 * k))
-        parts = after(parts, *done)
-        total = parts[0].astype(F32)
-        for part in parts[1:]:
-            total = total + part.astype(F32)
-        return total.astype(BF)
+    q_y, o_x, gate_up_near, input_grad, down_held = meet(q_y, o_x, gate_up_near, input_grad, down_held)
+
+    q_held = add2(pick(q_held, my_y, 2), q_y)
+    o_held = add2(o_held[0], o_x)
+    q_x = swap(q_held[1], "fsdp", 1)
+    o_y = swap(pick(o_held, 1 - my_y, 1), "sub", 2)
+    down_far_came = swap(down_held[1], "fsdp", 4)
+    gate_up_held = add2(far_pair(gate_up_held, 1, 0), gate_up_near)
+    q_x, o_y, down_far_came = meet(q_x, o_y, down_far_came)
+
+    q_held = add2(q_held[0], q_x)
+    o_held = add2(pick(o_held, my_y, 1), o_y)
+    attn_held = jnp.concatenate([q_held, o_held], axis=-1)
+    attn_near = swap(far_pair(attn_held, 0, 1), "fsdp", 2)
+    gate_up_far = swap(gate_up_held[:, 1], "fsdp", 4)
+    result = add2(result[0], res_c).reshape(2, count, wide)
+    res_y = swap(result[1], "sub", 2)
+    attn_near, res_y = meet(attn_near, res_y)
+    attn_held = add2(far_pair(attn_held, 0, 0), attn_near)
+    attn_far = swap(attn_held[1], "fsdp", 4)
+    result = hidden1 + result[0].astype(F32) + res_y.astype(F32)
+    output = mm_t((live * result).astype(BF), spread_mat).astype(BF)
+    down_own = add2(down_held[0], down_far_came)[None]
+    mlp_own = jnp.concatenate([add2(gate_up_held[:, 0], gate_up_far), down_own])
+    mlp_own = mlp_own.reshape(3, 2, 2, padded, quarter)
 
     def sub_return(held):
         came = swap(pick(held, 1 - my_c, 2), "sub", 1)
@@ -655,31 +726,9 @@
             [jnp.where(first, mine, came), jnp.where(first, came, mine)], axis=-1
         )
 
-    def mlp_sum(terms, near_done, far_done):
-        k = len(terms)
-        held = jnp.stack(terms).reshape(k, 2, n_far, n_sub * padded, quarter)
-        held = add2(held[:, 0], after(swap(held[:, 1], "fsdp", 1), *near_done))
-        held = far_sum(held, 1, *far_done).reshape(k, 2, 2, padded, quarter)
-        return sub_return(held)
-
-    def core_sum(held):
-        held = held.reshape(2, n_far, 2, 2, padded, half_ff)
-        return add2(pick(held, my_c, 3), swap(pick(held, 1 - my_c, 3), "sub", 1))
-
-    def x_sum(held):
-        return add2(held[0], swap(held[1], "fsdp", 1))
-
-    def y_sum(held, axis):
-        return add2(pick(held, my_y, axis), swap(pick(held, 1 - my_y, axis), "sub", 2))
-
-    o_held = x_sum(core_sum(o_term))
-    q_held = y_sum(core_sum(q_term), 2)
-    down_own = mlp_sum([down_term], grad_in2, [q_term])
-    gate_up_own = mlp_sum([gate_term, up_term], [q_term], [o_held, q_held])
-    o_own = far_sum(y_sum(o_held, 1), 0)
-    q_own = far_sum(x_sum(q_held), 0)
-    gain_grad = q_own[own, :share].astype(F32)
-    attn_own = jnp.concatenate([q_own, o_own], axis=1)
+    mlp_own = sub_return(mlp_own)
+    attn_own = add2(attn_held[0], attn_far)
+    gain_grad = attn_own[own, :share].astype(F32)
 
     def flat(mine):
         return mine[:own].astype(F32).reshape(-1)
@@ -688,9 +737,9 @@
         output,
         input_grad,
         flat(attn_own),
-        flat(gate_up_own[0]),
-        flat(gate_up_own[1]),
-        flat(down_own[0]),
+        flat(mlp_own[0]),
+        flat(mlp_own[1]),
+        flat(mlp_own[2]),
         gain_grad,
     )
 
@@ -699,8 +748,7 @@
     n_fsdp, n_sub = mesh.shape["fsdp"], mesh.shape["sub"]
     n_all = n_fsdp * n_sub
     by_rows = (
-        n_fsdp == 8 and
-        D % n_all == 0 and n_fsdp & (n_fsdp - 1) == 0 and n_fsdp > 1 and n_sub == 4 and D // n_fsdp % (D // n_all) == 0
+        n_fsdp == 8 and D % n_all == 0 and n_fsdp & (n_fsdp - 1) == 0 and n_fsdp > 1 and n_sub == 4 and D // n_fsdp % (D // n_all) == 0
     )
     in_specs = (
         P(("fsdp", "sub"), None),

time: 252 us -> 239 us (0.948)
  starting transfers between devices: 64.7 us -> 41.2 us
  waiting for transfers between devices: 98.2 us -> 115 us
  other arithmetic: 24.9 us -> 19.9 us
  local copies, waits for them, and re-layouts: 21 us -> 18.1 us
    ppermute x51 -> x42, starting transfers between devices: 64.7 us -> 41.2 us  [swap(): lax.ppermute(value, axis, [(i, i ^ bit) for i in range(lax.axis_size(axis...]
    ppermute x51 -> x42, waiting for transfers between devices: 98.2 us -> 115 us  [swap(): lax.ppermute(value, axis, [(i, i ^ bit) for i in range(lax.axis_size(axis...]
    another operation x12 -> x8, other arithmetic: 6.15 us -> 0.62 us  [put2(): jnp.stack([jnp.where(first, own, came), jnp.where(first, came, own)], axi...]
    squeeze x7 -> x10, local copies, waits for them, and re-layouts: 0.36 us -> 4.73 us  [the longest x2 3.8 us: body(): q_c, o_c = (swap(q_term[1], 'sub', 1), swap(o_term[1], 'sub', 1))]
    another operation x7 -> x4, local copies, waits for them, and re-layouts: 4.16 us -> 1.02 us  [the longest x1 1.4 us: body(): jnp.stack([gate_up[:, 0], gate_up_came[:, 0]]).reshape(wide, quarter)]
    squeeze x4 -> x2, local copies, waits for them, and re-layouts: 2.67 us -> 0.08 us  [pick(): return lax.dynamic_index_in_dim(value, index, axis, keepdims=False)]
    dynamic_slice x4 -> x0, local copies, waits for them, and re-layouts: 2.59 us -> none  [pick(): return lax.dynamic_index_in_dim(value, index, axis, keepdims=False)]
    convert_element_type x10 -> x16, other arithmetic: 7.25 us -> 9.05 us  [add2(): return (kept.astype(F32) + came.astype(F32)).astype(BF)]
  transfers between devices with their start and end apart: 51 -> 42, of which waited for: 22 -> 22; matrix products, arithmetic and copies ran while one was open for 22% -> 16% of each run, Pallas kernels for 9% -> 10%
where the time goes in v2:
time: 239 us; the launch traced here: 238 us
  waiting for transfers between devices  115 us (48%)
  starting transfers between devices  41.2 us (17%)
  Pallas kernels  24.5 us (10%)
  other arithmetic  19.9 us (8%)
  local copies, waits for them, and re-layouts  18.1 us (8%)
  matrix products  16.9 us (7%)
  between operations  2.91 us (1%)
    ppermute x42, waiting for transfers between devices, swap(): lax.ppermute(value, axis, [(i, i ^ bit) for i in range(lax.axis_size(axis...  115 us
    ppermute x42, starting transfers between devices, swap(): lax.ppermute(value, axis, [(i, i ^ bit) for i in range(lax.axis_size(axis...  41.2 us
    pallas_call x2, Pallas kernels, run_kernel(): pl.pallas_call(kernel, out_shape=[jax.ShapeDtypeStruct(shape, kind) for s...  24.5 us
    convert_element_type x16, other arithmetic, add2(): return (kept.astype(F32) + came.astype(F32)).astype(BF)  9.05 us
    dot_general x5, matrix products, mm(): return jnp.dot(a, b, preferred_element_type=F32)  6.57 us
  transfers between devices with their start and end apart: 42, of which 22 were waited for; matrix products, arithmetic and copies ran while one was open for 16% of the time, Pallas kernels for 10%

profile of v2, /device:TPU:0, one launch (start us, length us, event | category | flops | bytes accessed | tf_op | source)
XLA Modules:
  0.0 238.4 jit_solution(16201741798158073987)
XLA Ops:
  2.8 5.1 %collective-permute-start.2 = (bf16[32,2560]{1,0:T(8,128)(2,1)S(1)}, bf16[32,2560]{1,0:T(8,128)(2,1)S(1)}, u32[]{:S(2)}, u32[]{:S(2)}) collective-permute-start(bf16[32,2560]{1,0:T(8,128)(2,1)S(1)} %scatter.4), channel_id=1, source_target_pairs={{0,24},{4,28},{8,16},{12,20},{16,8},{20,12},{24,0},{28,4},{1,25},{... | collective-permute-start | bytes 491528 | tf_op jit(solution)/shard_map/ppermute | solution.py:260
  10.2 1.7 collective-permute-start.3
  20.1 1.6 fusion.19.rows_ref
  26.1 6.2 %collective-permute-done.7 = bf16[2,128,640]{2,1,0:T(8,128)(2,1)S(1)} collective-permute-done((bf16[2,128,640]{2,1,0:T(8,128)(2,1)S(1)}, bf16[2,128,640]{2,1,0:T(8,128)(2,1)S(1)}, u32[]{:S(2)}, u32[]{:S(2)}) %collective-permute-start.7) | collective-permute-done | bytes 327712 | tf_op jit(solution)/shard_map/ppermute | solution.py:260
  35.2 1.6 collective-permute-start.8
  36.8 2.9 %collective-permute-start.10 = (bf16[2,128,640]{2,1,0:T(8,128)(2,1)S(1)}, bf16[2,128,640]{2,1,0:T(8,128)(2,1)S(1)}, u32[]{:S(2)}, u32[]{:S(2)}) collective-permute-start(bf16[2,128,640]{2,1,0:T(8,128)(2,1)S(1)} %slice.185), channel_id=1, source_target_pairs={{0,16},{4,20},{8,24},{12,28},{16,0},{20,4},{24,8},{28,12},{1,17},{... | collective-permute-start | bytes 983048 | tf_op jit(solution)/shard_map/ppermute | solution.py:260
  39.8 13.4 %collective-permute-done.10 = bf16[2,128,640]{2,1,0:T(8,128)(2,1)S(1)} collective-permute-done((bf16[2,128,640]{2,1,0:T(8,128)(2,1)S(1)}, bf16[2,128,640]{2,1,0:T(8,128)(2,1)S(1)}, u32[]{:S(2)}, u32[]{:S(2)}) %collective-permute-start.10) | collective-permute-done | bytes 327712 | tf_op jit(solution)/shard_map/ppermute | solution.py:260
  55.8 5.7 %collective-permute-done.14 = bf16[128,640]{1,0:T(8,128)(2,1)S(1)} collective-permute-done((bf16[128,640]{1,0:T(8,128)(2,1)S(1)}, bf16[128,640]{1,0:T(8,128)(2,1)S(1)}, u32[]{:S(2)}, u32[]{:S(2)}) %collective-permute-start.14) | collective-permute-done | bytes 163872 | tf_op jit(solution)/shard_map/ppermute | solution.py:260
  61.5 1.8 collective-permute-done.15
  66.6 1.7 collective-permute-start.17
  68.9 12.2 %attn_forward.1 = (bf16[128,1024]{1,0:T(8,128)(2,1)}, bf16[128,1280]{1,0:T(8,128)(2,1)}, bf16[128,384]{1,0:T(8,128)(2,1)}, f32[128,15]{1,0:T(8,128)}, bf16[128,1...) custom-call(s32[2]{0:T(128)} %pad_add_fusion.place_ref, ...), custom_call_target="tpu_custom_call" | custom-call | flops 1000 | bytes 1000 | tf_op jit(solution)/shard_map/attn_forward/pallas_call | solution.py:495
  81.8 7.1 %collective-permute-done.16 = bf16[128,1024]{1,0:T(8,128)(2,1)S(1)} collective-permute-done((bf16[128,1024]{1,0:T(8,128)(2,1)}, bf16[128,1024]{1,0:T(8,128)(2,1)S(1)}, u32[]{:S(2)}, u32[]{:S(2)}) %collective-permute-start.16) | collective-permute-done | bytes 262176 | tf_op jit(solution)/shard_map/ppermute | solution.py:260
  90.9 1.6 collective-permute-start.21
  92.7 3.7 %collective-permute-done.20 = bf16[4,2,128,640]{3,2,0,1:T(8,128)(2,1)S(1)} collective-permute-done((bf16[4,2,128,640]{3,2,0,1:T(8,128)(2,1)S(1)}, bf16[4,2,128,640]{3,2,0,1:T(8,128)(2,1)S(1)}, u32[]{:S(2)}, u32[]{:S(2)}) %collective-permute-start.20) | collective-permute-done | bytes 1310752 | tf_op jit(solution)/shard_map/ppermute | solution.py:260
  99.1 8.5 %collective-permute-done.21 = bf16[2,2,128,640]{3,2,1,0:T(8,128)(2,1)S(1)} collective-permute-done((bf16[2,2,128,640]{3,2,1,0:T(8,128)(2,1)S(1)}, bf16[2,2,128,640]{3,2,1,0:T(8,128)(2,1)S(1)}, u32[]{:S(2)}, u32[]{:S(2)}) %collective-permute-start.21) | collective-permute-done | bytes 655392 | tf_op jit(solution)/shard_map/ppermute | solution.py:260
  109.2 1.6 collective-permute-start.23
  116.1 9.0 %collective-permute-done.23 = bf16[4,128,640]{2,1,0:T(8,128)(2,1)S(1)} collective-permute-done((bf16[4,128,640]{2,1,0:T(8,128)(2,1)S(1)}, bf16[4,128,640]{2,1,0:T(8,128)(2,1)S(1)}, u32[]{:S(2)}, u32[]{:S(2)}) %collective-permute-start.23) | collective-permute-done | bytes 655392 | tf_op jit(solution)/shard_map/ppermute | solution.py:260
  130.3 2.2 collective-permute-done.24.grad_b_ref
  133.2 12.3 %attn_backward.1 = (bf16[2,512,1280]{2,1,0:T(8,128)(2,1)}, bf16[2,512,1280]{2,1,0:T(8,128)(2,1)}, f32[128,1024]{1,0:T(8,128)}) custom-call(s32[2]{0:T(128)} %pad_add_fusion.place_ref, bf16[128,1024]{1,0:T(8,128)(2,1)} %get-tuple-element.204.grad_a_ref, bf16[128,1024]{1,0:T(8,128)(2,1)} %copy-done.15, bf16[128,1024]{1,0:T(8,128)(2,1)} %fusion.23.grad_out_ref, ...), custom_call_target="tpu_custom_call" | custom-call | flops 1000 | bytes 1000 | tf_op jit(solution)/shard_map/attn_backward/pallas_call | solution.py:495
  145.5 2.6 %slice_bitcast_fusion = bf16[512,1280]{1,0:T(8,128)(2,1)} fusion(bf16[2,512,1280]{2,1,0:T(8,128)(2,1)} %get-tuple-element.157), kind=kLoop, calls=%fused_computation.40 | loop fusion | bytes 2621440 | tf_op jit(solution)/shard_map/squeeze | solution.py:670
  154.9 8.9 %collective-permute-done.28 = bf16[2,128,640]{2,1,0:T(8,128)(2,1)} collective-permute-done((bf16[2,128,640]{2,1,0:T(8,128)(2,1)}, bf16[2,128,640]{2,1,0:T(8,128)(2,1)}, u32[]{:S(2)}, u32[]{:S(2)}) %collective-permute-start.28) | collective-permute-done | bytes 327712 | tf_op jit(solution)/shard_map/ppermute | solution.py:260
  163.8 2.0 fusion.6
  165.9 1.8 fusion.4
  168.0 1.7 fusion.5
  170.5 1.7 collective-permute-start.32
  177.4 2.7 %fusion.1 = f32[128,960]{0,1:T(8,128)} fusion(f32[128,1024]{1,0:T(8,128)S(1)} %copy-done.21, s32[1024]{0:T(1024)S(1)} %fusion.64), kind=kOutput, calls=%fused_computation.2 | convolution fusion | flops 1510932480 | bytes 1019904 | tf_op jit(solution)/shard_map/dot_general | solution.py:683
  180.1 7.5 %collective-permute-done.30 = bf16[2,4,32,1280]{3,2,1,0:T(8,128)(2,1)S(1)} collective-permute-done((bf16[2,4,32,1280]{3,2,1,0:T(8,128)(2,1)S(1)}, bf16[2,4,32,1280]{3,2,1,0:T(8,128)(2,1)S(1)}, u32[]{:S(2)}, u32[]{:S(2)}) %collective-permute-start.30) | collective-permute-done | bytes 655392 | tf_op jit(solution)/shard_map/ppermute | solution.py:260
  191.9 2.7 %collective-permute-start.39 = (bf16[2,128,640]{2,1,0:T(8,128)(2,1)S(1)}, bf16[2,128,640]{2,1,0:T(8,128)(2,1)S(1)}, u32[]{:S(2)}, u32[]{:S(2)}) collective-permute-start(bf16[2,128,640]{2,1,0:T(8,128)(2,1)S(1)} %slice_bitcast_fusion.8), channel_id=1, source_target_pairs={{0,16},{4,20},{8,24},{12,28},{16,0},{20,4},{24,8},{28,12},{1,17},{... | collective-permute-start | bytes 983048 | tf_op jit(solution)/shard_map/ppermute | solution.py:260
  194.6 12.3 %collective-permute-done.35 = bf16[128,640]{1,0:T(8,128)(2,1)S(1)} collective-permute-done((bf16[128,640]{1,0:T(8,128)(2,1)S(1)}, bf16[128,640]{1,0:T(8,128)(2,1)S(1)}, u32[]{:S(2)}, u32[]{:S(2)}) %collective-permute-start.35) | collective-permute-done | bytes 163872 | tf_op jit(solution)/shard_map/ppermute | solution.py:260
  207.1 6.7 %collective-permute-done.39 = bf16[2,128,640]{2,1,0:T(8,128)(2,1)S(1)} collective-permute-done((bf16[2,128,640]{2,1,0:T(8,128)(2,1)S(1)}, bf16[2,128,640]{2,1,0:T(8,128)(2,1)S(1)}, u32[]{:S(2)}, u32[]{:S(2)}) %collective-permute-start.39) | collective-permute-done | bytes 327712 | tf_op jit(solution)/shard_map/ppermute | solution.py:260
  216.3 8.0 %collective-permute-done.36 = bf16[2,32,2560]{2,1,0:T(8,128)(2,1)S(1)} collective-permute-done((bf16[2,32,2560]{2,1,0:T(8,128)(2,1)S(1)}, bf16[2,32,2560]{2,1,0:T(8,128)(2,1)S(1)}, u32[]{:S(2)}, u32[]{:S(2)}) %collective-permute-start.36) | collective-permute-done | bytes 327712 | tf_op jit(solution)/shard_map/ppermute | solution.py:260
  226.0 8.6 %collective-permute-done.38 = bf16[32,2560]{1,0:T(8,128)(2,1)S(1)} collective-permute-done((bf16[32,2560]{1,0:T(8,128)(2,1)S(1)}, bf16[32,2560]{1,0:T(8,128)(2,1)S(1)}, u32[]{:S(2)}, u32[]{:S(2)}) %collective-permute-start.38) | collective-permute-done | bytes 163872 | tf_op jit(solution)/shard_map/ppermute | solution.py:260
  (224 shorter events, 68.4 us)
Async XLA Ops:
  2.8 19.1 %collective-permute-start.2 = (bf16[32,2560]{1,0:T(8,128)(2,1)S(1)}, bf16[32,2560]{1,0:T(8,128)(2,1)S(1)}, u32[]{:S(2)}, u32[]{:S(2)}) collective-permute-start(bf16[32,2560]{1,0:T(8,128)(2,1)S(1)} %scatter.4), channel_id=1, source_target_pairs={{0,24},{4,28},{8,16},{12,20},{16,8},{20,12},{24,0},{28,4},{1,25},{... | collective-permute-start | bytes 491528 | tf_op jit(solution)/shard_map/ppermute | solution.py:260
  7.9 14.0 %collective-permute-start.1 = (bf16[32,2560]{1,0:T(8,128)(2,1)S(1)}, bf16[32,2560]{1,0:T(8,128)(2,1)S(1)}, u32[]{:S(2)}, u32[]{:S(2)}) collective-permute-start(bf16[32,2560]{1,0:T(8,128)(2,1)S(1)} %scatter.4), channel_id=1, source_target_pairs={{0,16},{4,20},{8,24},{12,28},{16,0},{20,4},{24,8},{28,12},{1,17},{... | collective-permute-start | bytes 491528 | tf_op jit(solution)/shard_map/ppermute | solution.py:260
  7.9 14.1 %collective-permute-start = (bf16[32,2560]{1,0:T(8,128)(2,1)S(1)}, bf16[32,2560]{1,0:T(8,128)(2,1)S(1)}, u32[]{:S(2)}, u32[]{:S(2)}) collective-permute-start(bf16[32,2560]{1,0:T(8,128)(2,1)S(1)} %scatter.4), channel_id=1, source_target_pairs={{0,8},{4,12},{8,0},{12,4},{16,24},{20,28},{24,16},{28,20},{1,9},{5... | collective-permute-start | bytes 491528 | tf_op jit(solution)/shard_map/ppermute | solution.py:260
  22.1 10.2 %collective-permute-start.7 = (bf16[2,128,640]{2,1,0:T(8,128)(2,1)S(1)}, bf16[2,128,640]{2,1,0:T(8,128)(2,1)S(1)}, u32[]{:S(2)}, u32[]{:S(2)}) collective-permute-start(bf16[2,128,640]{2,1,0:T(8,128)(2,1)S(1)} %slice.185), channel_id=1, source_target_pairs={{0,8},{4,12},{8,0},{12,4},{16,24},{20,28},{24,16},{28,20},{1,9},{5... | collective-permute-start | bytes 983048 | tf_op jit(solution)/shard_map/ppermute | solution.py:260
  23.4 9.8 %collective-permute-start.6 = (bf16[4,32,1280]{2,1,0:T(8,128)(2,1)S(1)}, bf16[4,32,1280]{2,1,0:T(8,128)(2,1)S(1)}, u32[]{:S(2)}, u32[]{:S(2)}) collective-permute-start(bf16[4,32,1280]{2,1,0:T(8,128)(2,1)S(1)} %get-tuple-element.110), channel_id=1, source_target_pairs={{0,2},{1,3},{2,0},{3,1},{4,6},{5,7},{6,4},{7,5},{8,10},{9,11},{10,... | collective-permute-start | bytes 983048 | tf_op jit(solution)/shard_map/ppermute | solution.py:260
  23.9 9.6 %collective-permute-start.5 = (bf16[4,32,1280]{2,1,0:T(8,128)(2,1)S(1)}, bf16[4,32,1280]{2,1,0:T(8,128)(2,1)S(1)}, u32[]{:S(2)}, u32[]{:S(2)}) collective-permute-start(bf16[4,32,1280]{2,1,0:T(8,128)(2,1)S(1)} %get-tuple-element.108), channel_id=1, source_target_pairs={{0,4},{4,0},{8,12},{12,8},{16,20},{20,16},{24,28},{28,24},{1,5},{5... | collective-permute-start | bytes 983048 | tf_op jit(solution)/shard_map/ppermute | solution.py:260
  33.6 19.5 %collective-permute-start.9 = (bf16[4,2,32,1280]{3,2,1,0:T(8,128)(2,1)S(1)}, bf16[4,2,32,1280]{3,2,1,0:T(8,128)(2,1)S(1)}, u32[]{:S(2)}, u32[]{:S(2)}) collective-permute-start(bf16[4,2,32,1280]{3,2,1,0:T(8,128)(2,1)S(1)} %pad_maximum_fusion.10), channel_id=1, source_target_pairs={{0,4},{4,0},{8,12},{12,8},{16,20},{20,16},{24,28},{28,24},{1,5},{5... | collective-permute-start | bytes 1966088 | tf_op jit(solution)/shard_map/ppermute | solution.py:260
  35.2 17.9 %collective-permute-start.8 = (bf16[2,4,32,1280]{3,2,1,0:T(8,128)(2,1)S(1)}, bf16[2,4,32,1280]{3,2,1,0:T(8,128)(2,1)S(1)}, u32[]{:S(2)}, u32[]{:S(2)}) collective-permute-start(bf16[2,4,32,1280]{3,2,1,0:T(8,128)(2,1)S(1)} %pad_maximum_fusion.9), channel_id=1, source_target_pairs={{0,2},{1,3},{2,0},{3,1},{4,6},{5,7},{6,4},{7,5},{8,10},{9,11},{10,... | collective-permute-start | bytes 1966088 | tf_op jit(solution)/shard_map/ppermute | solution.py:260
  36.8 16.3 %collective-permute-start.10 = (bf16[2,128,640]{2,1,0:T(8,128)(2,1)S(1)}, bf16[2,128,640]{2,1,0:T(8,128)(2,1)S(1)}, u32[]{:S(2)}, u32[]{:S(2)}) collective-permute-start(bf16[2,128,640]{2,1,0:T(8,128)(2,1)S(1)} %slice.185), channel_id=1, source_target_pairs={{0,16},{4,20},{8,24},{12,28},{16,0},{20,4},{24,8},{28,12},{1,17},{... | collective-permute-start | bytes 983048 | tf_op jit(solution)/shard_map/ppermute | solution.py:260
  53.7 11.0 %collective-permute-start.12 = (bf16[512,1280]{1,0:T(8,128)(2,1)S(1)}, bf16[512,1280]{1,0:T(8,128)(2,1)S(1)}, u32[]{:S(2)}, u32[]{:S(2)}) collective-permute-start(bf16[512,1280]{1,0:T(8,128)(2,1)S(1)} %bitcast.239), channel_id=1, source_target_pairs={{0,1},{1,0},{2,3},{3,2},{4,5},{5,4},{6,7},{7,6},{8,9},{9,8},{10,11... | collective-permute-start | bytes 3932168 | tf_op jit(solution)/shard_map/ppermute | solution.py:260
  54.6 10.1 %collective-permute-start.11 = (bf16[512,1280]{1,0:T(8,128)(2,1)S(1)}, bf16[512,1280]{1,0:T(8,128)(2,1)S(1)}, u32[]{:S(2)}, u32[]{:S(2)}) collective-permute-start(bf16[512,1280]{1,0:T(8,128)(2,1)S(1)} %bitcast.237), channel_id=1, source_target_pairs={{0,1},{1,0},{2,3},{3,2},{4,5},{5,4},{6,7},{7,6},{8,9},{9,8},{10,11... | collective-permute-start | bytes 3932168 | tf_op jit(solution)/shard_map/ppermute | solution.py:260
  54.6 10.1 %collective-permute-start.13 = (bf16[2,128,640]{2,1,0:T(8,128)(2,1)S(1)}, bf16[2,128,640]{2,1,0:T(8,128)(2,1)S(1)}, u32[]{:S(2)}, u32[]{:S(2)}) collective-permute-start(bf16[2,128,640]{2,1,0:T(8,128)(2,1)S(1)} %collective-permute-done.10), channel_id=1, source_target_pairs={{0,8},{4,12},{8,0},{12,4},{16,24},{20,28},{24,16},{28,20},{1,9},{5... | collective-permute-start | bytes 983048 | tf_op jit(solution)/shard_map/ppermute | solution.py:260
  66.0 30.5 %collective-permute-start.20 = (bf16[4,2,128,640]{3,2,0,1:T(8,128)(2,1)S(1)}, bf16[4,2,128,640]{3,2,0,1:T(8,128)(2,1)S(1)}, u32[]{:S(2)}, u32[]{:S(2)}) collective-permute-start(bf16[4,2,128,640]{3,2,0,1:T(8,128)(2,1)S(1)} %copy.62), channel_id=1, source_target_pairs={{0,4},{4,0},{8,12},{12,8},{16,20},{20,16},{24,28},{28,24},{1,5},{5... | collective-permute-start | bytes 3932168 | tf_op jit(solution)/shard_map/ppermute | solution.py:260
  66.6 22.3 %collective-permute-start.17 = (bf16[2,128,640]{2,1,0:T(8,128)(2,1)S(1)}, bf16[2,128,640]{2,1,0:T(8,128)(2,1)S(1)}, u32[]{:S(2)}, u32[]{:S(2)}) collective-permute-start(bf16[2,128,640]{2,1,0:T(8,128)(2,1)S(1)} %get-tuple-element.213), channel_id=1, source_target_pairs={{0,16},{4,20},{8,24},{12,28},{16,0},{20,4},{24,8},{28,12},{1,17},{... | collective-permute-start | bytes 983048 | tf_op jit(solution)/shard_map/ppermute | solution.py:260
  90.9 16.7 %collective-permute-start.21 = (bf16[2,2,128,640]{3,2,1,0:T(8,128)(2,1)S(1)}, bf16[2,2,128,640]{3,2,1,0:T(8,128)(2,1)S(1)}, u32[]{:S(2)}, u32[]{:S(2)}) collective-permute-start(bf16[2,2,128,640]{3,2,1,0:T(8,128)(2,1)S(1)} %get-tuple-element.198), channel_id=1, source_target_pairs={{0,8},{4,12},{8,0},{12,4},{16,24},{20,28},{24,16},{28,20},{1,9},{5... | collective-permute-start | bytes 1966088 | tf_op jit(solution)/shard_map/ppermute | solution.py:260
  109.2 15.9 %collective-permute-start.23 = (bf16[4,128,640]{2,1,0:T(8,128)(2,1)S(1)}, bf16[4,128,640]{2,1,0:T(8,128)(2,1)S(1)}, u32[]{:S(2)}, u32[]{:S(2)}) collective-permute-start(bf16[4,128,640]{2,1,0:T(8,128)(2,1)S(1)} %bitcast.277), channel_id=1, source_target_pairs={{0,4},{4,0},{8,12},{12,8},{16,20},{20,16},{24,28},{28,24},{1,5},{5... | collective-permute-start | bytes 1966088 | tf_op jit(solution)/shard_map/ppermute | solution.py:260
  128.8 35.0 %collective-permute-start.29 = (bf16[2,4,128,640]{3,2,1,0:T(8,128)(2,1)}, bf16[2,4,128,640]{3,2,1,0:T(8,128)(2,1)}, u32[]{:S(2)}, u32[]{:S(2)}) collective-permute-start(bf16[2,4,128,640]{3,2,1,0:T(8,128)(2,1)} %fusion.12), channel_id=1, source_target_pairs={{0,4},{4,0},{8,12},{12,8},{16,20},{20,16},{24,28},{28,24},{1,5},{5... | collective-permute-start | bytes 3932168 | tf_op jit(solution)/shard_map/ppermute | solution.py:260
  149.3 14.5 %collective-permute-start.25 = (bf16[512,1280]{1,0:T(8,128)(2,1)}, bf16[512,1280]{1,0:T(8,128)(2,1)}, u32[]{:S(2)}, u32[]{:S(2)}) collective-permute-start(bf16[512,1280]{1,0:T(8,128)(2,1)} %slice_bitcast_fusion.1), channel_id=1, source_target_pairs={{0,1},{1,0},{2,3},{3,2},{4,5},{5,4},{6,7},{7,6},{8,9},{9,8},{10,11... | collective-permute-start | bytes 3932168 | tf_op jit(solution)/shard_map/ppermute | solution.py:260
  149.3 14.5 %collective-permute-start.26 = (bf16[512,1280]{1,0:T(8,128)(2,1)}, bf16[512,1280]{1,0:T(8,128)(2,1)}, u32[]{:S(2)}, u32[]{:S(2)}) collective-permute-start(bf16[512,1280]{1,0:T(8,128)(2,1)} %slice_bitcast_fusion), channel_id=1, source_target_pairs={{0,1},{1,0},{2,3},{3,2},{4,5},{5,4},{6,7},{7,6},{8,9},{9,8},{10,11... | collective-permute-start | bytes 3932168 | tf_op jit(solution)/shard_map/ppermute | solution.py:260
  152.6 11.3 %collective-permute-start.27 = (bf16[256,1024]{1,0:T(8,128)(2,1)}, bf16[256,1024]{1,0:T(8,128)(2,1)}, u32[]{:S(2)}, u32[]{:S(2)}) collective-permute-start(bf16[256,1024]{1,0:T(8,128)(2,1)} %slice.271), channel_id=1, source_target_pairs={{0,1},{1,0},{2,3},{3,2},{4,5},{5,4},{6,7},{7,6},{8,9},{9,8},{10,11... | collective-permute-start | bytes 1572872 | tf_op jit(solution)/shard_map/ppermute | solution.py:260
  153.4 10.4 %collective-permute-start.28 = (bf16[2,128,640]{2,1,0:T(8,128)(2,1)}, bf16[2,128,640]{2,1,0:T(8,128)(2,1)}, u32[]{:S(2)}, u32[]{:S(2)}) collective-permute-start(bf16[2,128,640]{2,1,0:T(8,128)(2,1)} %slice_bitcast_fusion.15), channel_id=1, source_target_pairs={{0,8},{4,12},{8,0},{12,4},{16,24},{20,28},{24,16},{28,20},{1,9},{5... | collective-permute-start | bytes 983048 | tf_op jit(solution)/shard_map/ppermute | solution.py:260
  169.9 17.7 %collective-permute-start.30 = (bf16[2,4,32,1280]{3,2,1,0:T(8,128)(2,1)S(1)}, bf16[2,4,32,1280]{3,2,1,0:T(8,128)(2,1)S(1)}, u32[]{:S(2)}, u32[]{:S(2)}) collective-permute-start(bf16[2,4,32,1280]{3,2,1,0:T(8,128)(2,1)S(1)} %dynamic-slice_bitcast_fusion), channel_id=1, source_target_pairs={{0,2},{1,3},{2,0},{3,1},{4,6},{5,7},{6,4},{7,5},{8,10},{9,11},{10,... | collective-permute-start | bytes 1966088 | tf_op jit(solution)/shard_map/ppermute | solution.py:260
  170.5 17.1 %collective-permute-start.32 = (bf16[2,2,128,640]{3,2,1,0:T(8,128)(2,1)S(1)}, bf16[2,2,128,640]{3,2,1,0:T(8,128)(2,1)S(1)}, u32[]{:S(2)}, u32[]{:S(2)}) collective-permute-start(bf16[2,2,128,640]{3,2,1,0:T(8,128)(2,1)S(1)} %slice_bitcast_fusion.3), channel_id=1, source_target_pairs={{0,8},{4,12},{8,0},{12,4},{16,24},{20,28},{24,16},{28,20},{1,9},{5... | collective-permute-start | bytes 1966088 | tf_op jit(solution)/shard_map/ppermute | solution.py:260
  172.1 15.8 %collective-permute-start.31 = (bf16[4,2,32,1280]{3,2,1,0:T(8,128)(2,1)S(1)}, bf16[4,2,32,1280]{3,2,1,0:T(8,128)(2,1)S(1)}, u32[]{:S(2)}, u32[]{:S(2)}) collective-permute-start(bf16[4,2,32,1280]{3,2,1,0:T(8,128)(2,1)S(1)} %bitcast.274), channel_id=1, source_target_pairs={{0,4},{4,0},{8,12},{12,8},{16,20},{20,16},{24,28},{28,24},{1,5},{5... | collective-permute-start | bytes 1966088 | tf_op jit(solution)/shard_map/ppermute | solution.py:260
  174.9 41.4 %collective-permute-start.37 = (bf16[128,1024]{1,0:T(8,128)(2,1)S(1)}, bf16[128,1024]{1,0:T(8,128)(2,1)S(1)}, u32[]{:S(2)}, u32[]{:S(2)}) collective-permute-start(bf16[128,1024]{1,0:T(8,128)(2,1)S(1)} %slice.284), channel_id=1, source_target_pairs={{0,2},{1,3},{2,0},{3,1},{4,6},{5,7},{6,4},{7,5},{8,10},{9,11},{10,... | collective-permute-start | bytes 786440 | tf_op jit(solution)/shard_map/ppermute | solution.py:260
  188.5 18.4 %collective-permute-start.33 = (bf16[4,32,1280]{2,1,0:T(8,128)(2,1)S(1)}, bf16[4,32,1280]{2,1,0:T(8,128)(2,1)S(1)}, u32[]{:S(2)}, u32[]{:S(2)}) collective-permute-start(bf16[4,32,1280]{2,1,0:T(8,128)(2,1)S(1)} %slice_bitcast_fusion.12), channel_id=1, source_target_pairs={{0,4},{4,0},{8,12},{12,8},{16,20},{20,16},{24,28},{28,24},{1,5},{5... | collective-permute-start | bytes 983048 | tf_op jit(solution)/shard_map/ppermute | solution.py:260
  190.1 16.8 %collective-permute-start.34 = (bf16[4,32,1280]{2,1,0:T(8,128)(2,1)S(1)}, bf16[4,32,1280]{2,1,0:T(8,128)(2,1)S(1)}, u32[]{:S(2)}, u32[]{:S(2)}) collective-permute-start(bf16[4,32,1280]{2,1,0:T(8,128)(2,1)S(1)} %dynamic-slice_bitcast_fusion.1), channel_id=1, source_target_pairs={{0,2},{1,3},{2,0},{3,1},{4,6},{5,7},{6,4},{7,5},{8,10},{9,11},{10,... | collective-permute-start | bytes 983048 | tf_op jit(solution)/shard_map/ppermute | solution.py:260
  191.5 15.4 %collective-permute-start.35 = (bf16[128,640]{1,0:T(8,128)(2,1)S(1)}, bf16[128,640]{1,0:T(8,128)(2,1)S(1)}, u32[]{:S(2)}, u32[]{:S(2)}) collective-permute-start(bf16[128,640]{1,0:T(8,128)(2,1)S(1)} %slice_bitcast_fusion.18), channel_id=1, source_target_pairs={{0,16},{4,20},{8,24},{12,28},{16,0},{20,4},{24,8},{28,12},{1,17},{... | collective-permute-start | bytes 491528 | tf_op jit(solution)/shard_map/ppermute | solution.py:260
  191.9 21.9 %collective-permute-start.39 = (bf16[2,128,640]{2,1,0:T(8,128)(2,1)S(1)}, bf16[2,128,640]{2,1,0:T(8,128)(2,1)S(1)}, u32[]{:S(2)}, u32[]{:S(2)}) collective-permute-start(bf16[2,128,640]{2,1,0:T(8,128)(2,1)S(1)} %slice_bitcast_fusion.8), channel_id=1, source_target_pairs={{0,16},{4,20},{8,24},{12,28},{16,0},{20,4},{24,8},{28,12},{1,17},{... | collective-permute-start | bytes 983048 | tf_op jit(solution)/shard_map/ppermute | solution.py:260
  214.1 10.2 %collective-permute-start.36 = (bf16[2,32,2560]{2,1,0:T(8,128)(2,1)S(1)}, bf16[2,32,2560]{2,1,0:T(8,128)(2,1)S(1)}, u32[]{:S(2)}, u32[]{:S(2)}) collective-permute-start(bf16[2,32,2560]{2,1,0:T(8,128)(2,1)S(1)} %slice_bitcast_fusion.11), channel_id=1, source_target_pairs={{0,8},{4,12},{8,0},{12,4},{16,24},{20,28},{24,16},{28,20},{1,9},{5... | collective-permute-start | bytes 983048 | tf_op jit(solution)/shard_map/ppermute | solution.py:260
  215.6 20.4 %collective-permute-start.41 = (bf16[3,32,1280]{2,1,0:T(8,128)(2,1)S(1)}, bf16[3,32,1280]{2,1,0:T(8,128)(2,1)S(1)}, u32[]{:S(2)}, u32[]{:S(2)}) collective-permute-start(bf16[3,32,1280]{2,1,0:T(8,128)(2,1)S(1)} %fusion.39), channel_id=1, source_target_pairs={{0,2},{1,3},{2,0},{3,1},{4,6},{5,7},{6,4},{7,5},{8,10},{9,11},{10,... | collective-permute-start | bytes 737288 | tf_op jit(solution)/shard_map/ppermute | solution.py:260
  224.4 10.2 %collective-permute-start.38 = (bf16[32,2560]{1,0:T(8,128)(2,1)S(1)}, bf16[32,2560]{1,0:T(8,128)(2,1)S(1)}, u32[]{:S(2)}, u32[]{:S(2)}) collective-permute-start(bf16[32,2560]{1,0:T(8,128)(2,1)S(1)} %slice_bitcast_fusion.16), channel_id=1, source_target_pairs={{0,16},{4,20},{8,24},{12,28},{16,0},{20,4},{24,8},{28,12},{1,17},{... | collective-permute-start | bytes 491528 | tf_op jit(solution)/shard_map/ppermute | solution.py:260
  (33 other events, 159.5 us)

commit v3 on v2

--- a/solution.py
+++ b/solution.py
@@ -413,7 +413,7 @@
         place_ref, grad_a_ref, grad_b_ref, grad_out_ref, hidden1_ref, rows_ref, gains_ref, owner_ref, inner_ref,
         spots_ref, cos_ref, sin_ref, seg_ref, input1_ref, qk_ref, v_ref, logsum_ref, att_ref,
         attn_q_ref, attn_o_ref,
-        q_term_ref, o_term_ref, input_grad_ref,
+        q_keep_ref, q_send_ref, o_keep_ref, o_send_ref, input_grad_ref,
         left_ref, right_ref, turn_ref,
     ):
         count = rows_ref.shape[0]
@@ -476,13 +476,16 @@
         q_term = dot_0(input1_ref[...], proj_grad)
         q_start = (q_term[:, :256] + dot_f(spots_ref[...], gain_rows)).astype(BF)
         q_term = q_term.astype(BF)
-        for p in range(wide // padded):
-            rel = p % 2 ^ core
-            block = slice(p * padded, (p + 1) * padded)
-            to = slice(p // 2 * padded, (p // 2 + 1) * padded)
-            q_term_ref[rel, to, :256] = q_start[block, :]
-            q_term_ref[rel, to, 256:] = q_term[block, 256:]
-            o_term_ref[rel, to, :] = o_term[block, :]
+        q_term = jnp.concatenate([q_start, q_term[:, 256:]], axis=1)
+        low_core = core == 0
+        for p in range(wide // padded // 2):
+            even = slice(2 * p * padded, (2 * p + 1) * padded)
+            odd = slice((2 * p + 1) * padded, (2 * p + 2) * padded)
+            to = slice(p * padded, (p + 1) * padded)
+            q_keep_ref[to, :] = jnp.where(low_core, q_term[even, :], q_term[odd, :])
+            q_send_ref[to, :] = jnp.where(low_core, q_term[odd, :], q_term[even, :])
+            o_keep_ref[to, :] = jnp.where(low_core, o_term[even, :], o_term[odd, :])
+            o_send_ref[to, :] = jnp.where(low_core, o_term[odd, :], o_term[even, :])
 
     return kernel
 
@@ -575,23 +578,23 @@
     half0 = jnp.stack([half0, x0])
     half1 = put2(half1, y1, my_y, 1)
     y0, x1, third = swap(half0, "sub", 2), swap(half1, "fsdp", 1), swap(gate_up, "fsdp", 4)
-    half0, half1, gate_up, down, near, y0, x1, third, grad_outb = meet(
-        half0, half1, gate_up, down, near, y0, x1, third, grad_outb
+    down_x = swap(down, "fsdp", 1)
+    half0, half1, gate_up, down, down_x, near, y0, x1, third, grad_outb = meet(
+        half0, half1, gate_up, down, down_x, near, y0, x1, third, grad_outb
     )
 
     half0 = put2(half0, y0, my_y, 2).reshape(wide // 2, half_ff)
     half1 = jnp.stack([half1, x1]).reshape(wide // 2, half_ff)
     c0, c1, last = swap(half0, "sub", 1), swap(half1, "sub", 1), swap(third, "fsdp", 2)
-    down_x = swap(down, "fsdp", 1)
     cot_y = swap(grad_outb, "sub", 2)
-    half0, half1, c0, c1, gate_up, near, third, last, down, down_x, cot_y = meet(
-        half0, half1, c0, c1, gate_up, near, third, last, down, down_x, cot_y
+    down = jnp.stack([down, down_x])
+    half0, half1, c0, c1, gate_up, near, third, last, down, cot_y = meet(
+        half0, half1, c0, c1, gate_up, near, third, last, down, cot_y
     )
 
     gate_up = jnp.stack([gate_up, near, third, last])
     gate_up_x = swap(gate_up, "fsdp", 1)
-    down = jnp.stack([down, down_x])
-    down_far = swap(down, "fsdp", 4)
+    down_near, down_third = swap(down, "fsdp", 2), swap(down, "fsdp", 4)
     by_fsdp = [(f % 2) * n_far * n_sub + (f // 2) * n_sub for f in range(n_fsdp)]
     my_place = jnp.stack([my_fsdp, my_c])
     tall = (count, wide)
@@ -615,13 +618,12 @@
     input1, qk, values, logsum, attended, hidden1, input2, gains_p, attn_q, attn_o = forward
 
     in2_y = swap(input2, "sub", 2)
-    input2, in2_y, down_far, cot_y = meet(input2, in2_y, down_far, cot_y)
-    down = jnp.stack([down, down_far])
-    down_near = swap(down, "fsdp", 2)
+    input2, in2_y, cot_y, down_near, down_third = meet(input2, in2_y, cot_y, down_near, down_third)
+    down_last = swap(down_third, "fsdp", 2)
     in2_all = jnp.stack([input2, in2_y])
     cot_all = jnp.stack([grad_outb, cot_y])
     in2_c, cot_c = swap(in2_all, "sub", 1), swap(cot_all, "sub", 1)
-    in2_c, cot_c, gate_up_x = meet(in2_c, cot_c, gate_up_x)
+    in2_c, cot_c, gate_up_x, down_last = meet(in2_c, cot_c, gate_up_x, down_last)
     in2_all = jnp.stack([in2_all, in2_c]).reshape(4 * count, wide)
     cot_all = jnp.stack([cot_all, cot_c]).reshape(4 * count, wide)
     gate_w = jnp.stack([gate_up[:, 0], gate_up_x[:, 0]]).reshape(wide, quarter)
@@ -631,12 +633,10 @@
     sigma = jax.nn.sigmoid(gate)
     active = gate * sigma
     hidden = (active * up).astype(BF)
-    down_term = term(cot_all, hidden)
-    down_near = after(down_near, hidden)
-    down_w = jnp.stack([down, down_near])
-    down_w = down_w.transpose(2, 1, 0, 3, 4).reshape(wide, quarter)
-    down_term = down_term.reshape(2, n_far, n_sub * padded, quarter)
-    down_x_came = swap(down_term[1], "fsdp", 1)
+    down_term = term(cot_all, hidden).reshape(2, n_far, n_sub * padded, quarter)
+    down_w = jnp.stack([down, down_near, down_third, down_last])
+    down_w = down_w.transpose(1, 0, 2, 3).reshape(wide, quarter)
+    down_near_came = swap(far_pair(down_term, 1, 1), "fsdp", 2)
     grad_hidden = mm(cot_all, down_w)
     grad_gate = (grad_hidden * up * sigma * (1.0 + gate * (1.0 - sigma))).astype(BF)
     grad_up = (grad_hidden * active).astype(BF)
@@ -646,15 +646,15 @@
     result = mm_t(hidden, down_w).astype(BF).reshape(2, 2 * count, wide)
 
     came = swap(grad_in2[1], "sub", 1)
-    came, down_x_came = meet(came, down_x_came)
     grad_in2 = add2(grad_in2[0], came).reshape(2, count, wide)
     grad_in2_y = swap(grad_in2[1], "sub", 2)
     gate_up_x_came = swap(gate_up_term[:, 1], "fsdp", 1)
-    down_held = add2(down_term[0], down_x_came)
-    down_near_came = swap(far_pair(down_held, 0, 1), "fsdp", 2)
-    q_term, o_term, input_grad = run_kernel(
+    grad_in2, grad_in2_y, down_near_came = meet(grad_in2, grad_in2_y, down_near_came)
+    down_held = add2(far_pair(down_term, 1, 0), down_near_came)
+    down_far_came = swap(down_held[:, 1], "fsdp", 4)
+    q_keep, q_send, o_keep, o_send, input_grad = run_kernel(
         make_backward(n_fsdp, own, padded, share),
-        [((2, wide // 2, half_ff), BF), ((2, wide // 2, half_ff), BF), (tall, F32)],
+        [((wide // 2, half_ff), BF)] * 4 + [(tall, F32)],
         (
             my_place, grad_in2[0], grad_in2_y, grad_outb, hidden1, rows32, gains_p, *tables, spots, *angles,
             input1, qk, values, logsum, attended, attn_q, attn_o,
@@ -667,18 +667,24 @@
         name="attn_backward",
     )
 
-    q_c, o_c = swap(q_term[1], "sub", 1), swap(o_term[1], "sub", 1)
-    res_c = swap(after(result[1], q_term), "sub", 1)
-    q_c, o_c, res_c, down_near_came, gate_up_x_came = meet(q_c, o_c, res_c, down_near_came, gate_up_x_came)
+    q_keep, q_send, o_keep, o_send, down_far_came, gate_up_x_came = meet(
+        q_keep, q_send, o_keep, o_send, down_far_came, gate_up_x_came
+    )
+
+    q_c, o_c = swap(q_send, "sub", 1), swap(o_send, "sub", 1)
+    gate_up_held = add2(gate_up_term[:, 0], gate_up_x_came)
+    gate_up_near = swap(far_pair(gate_up_held, 1, 1), "fsdp", 2)
+    down_held = add2(down_held[:, 0], down_far_came)
+    down_x_came = swap(down_held[1], "fsdp", 1)
+    q_c, o_c, gate_up_near, down_x_came = meet(q_c, o_c, gate_up_near, down_x_came)
 
     full = (2, n_far, 2, padded, half_ff)
-    q_held = add2(q_term[0], q_c).reshape(full)
-    o_held = add2(o_term[0], o_c).reshape(full)
+    q_held = add2(q_keep, q_c).reshape(full)
+    o_held = add2(o_keep, o_c).reshape(full)
     q_y = swap(pick(q_held, 1 - my_y, 2), "sub", 2)
     o_x = swap(o_held[1], "fsdp", 1)
-    gate_up_held = add2(gate_up_term[:, 0], gate_up_x_came)
-    gate_up_near = swap(far_pair(gate_up_held, 1, 1), "fsdp", 2)
-    down_held = add2(far_pair(down_held, 0, 0), down_near_came)
+    gate_up_held = add2(far_pair(gate_up_held, 1, 0), gate_up_near)
+    gate_up_far = swap(gate_up_held[:, 1], "fsdp", 4)
     input_grad = after(input_grad, q_c)
     input_grad = lax.dot_general(
         input_grad,
@@ -686,47 +692,37 @@
         (((1,), (1,)), ((), ())),
         precision=lax.Precision.HIGHEST,
     )
-    q_y, o_x, gate_up_near, input_grad, down_held = meet(q_y, o_x, gate_up_near, input_grad, down_held)
+    res_c = swap(after(result[1], q_c), "sub", 1)
+    q_y, o_x, gate_up_far, input_grad, res_c = meet(q_y, o_x, gate_up_far, input_grad, res_c)
 
     q_held = add2(pick(q_held, my_y, 2), q_y)
     o_held = add2(o_held[0], o_x)
     q_x = swap(q_held[1], "fsdp", 1)
     o_y = swap(pick(o_held, 1 - my_y, 1), "sub", 2)
-    down_far_came = swap(down_held[1], "fsdp", 4)
-    gate_up_held = add2(far_pair(gate_up_held, 1, 0), gate_up_near)
-    q_x, o_y, down_far_came = meet(q_x, o_y, down_far_came)
+    down_own = add2(down_held[0], down_x_came)[None]
+    mlp_own = jnp.concatenate([add2(gate_up_held[:, 0], gate_up_far), down_own])
+    mlp_own = mlp_own.reshape(3, 2, 2, padded, quarter)
+    mlp_c = swap(pick(mlp_own, 1 - my_c, 2), "sub", 1)
+    q_x, o_y, mlp_c = meet(q_x, o_y, mlp_c)
+
+    def side_by_side(mine, came, bit):
+        first = bit == 0
+        return jnp.concatenate([jnp.where(first, mine, came), jnp.where(first, came, mine)], axis=-1)
 
     q_held = add2(q_held[0], q_x)
     o_held = add2(pick(o_held, my_y, 1), o_y)
     attn_held = jnp.concatenate([q_held, o_held], axis=-1)
     attn_near = swap(far_pair(attn_held, 0, 1), "fsdp", 2)
-    gate_up_far = swap(gate_up_held[:, 1], "fsdp", 4)
     result = add2(result[0], res_c).reshape(2, count, wide)
     res_y = swap(result[1], "sub", 2)
-    attn_near, res_y = meet(attn_near, res_y)
+    mlp_own = side_by_side(pick(mlp_own, my_c, 2), mlp_c, my_c)
+    mlp_y = swap(pick(mlp_own, 1 - my_y, 1), "sub", 2)
+    attn_near, res_y, mlp_y = meet(attn_near, res_y, mlp_y)
     attn_held = add2(far_pair(attn_held, 0, 0), attn_near)
     attn_far = swap(attn_held[1], "fsdp", 4)
     result = hidden1 + result[0].astype(F32) + res_y.astype(F32)
     output = mm_t((live * result).astype(BF), spread_mat).astype(BF)
-    down_own = add2(down_held[0], down_far_came)[None]
-    mlp_own = jnp.concatenate([add2(gate_up_held[:, 0], gate_up_far), down_own])
-    mlp_own = mlp_own.reshape(3, 2, 2, padded, quarter)
-
-    def sub_return(held):
-        came = swap(pick(held, 1 - my_c, 2), "sub", 1)
-        mine = pick(held, my_c, 2)
-        first = my_c == 0
-        held = jnp.concatenate(
-            [jnp.where(first, mine, came), jnp.where(first, came, mine)], axis=-1
-        )
-        came = swap(pick(held, 1 - my_y, 1), "sub", 2)
-        mine = pick(held, my_y, 1)
-        first = my_y == 0
-        return jnp.concatenate(
-            [jnp.where(first, mine, came), jnp.where(first, came, mine)], axis=-1
-        )
-
-    mlp_own = sub_return(mlp_own)
+    mlp_own = side_by_side(pick(mlp_own, my_y, 1), mlp_y, my_y)
     attn_own = add2(attn_held[0], attn_far)
     gain_grad = attn_own[own, :share].astype(F32)
 

time: 239 us -> 220 us (0.921)
  waiting for transfers between devices: 115 us -> 105 us
  other arithmetic: 19.9 us -> 15.9 us
  local copies, waits for them, and re-layouts: 18.1 us -> 14.5 us
    ppermute x42 -> x43, waiting for transfers between devices: 115 us -> 105 us  [swap(): lax.ppermute(value, axis, [(i, i ^ bit) for i in range(lax.axis_size(axis...]
    convert_element_type x16, other arithmetic: 9.05 us -> 4.89 us  [add2(): return (kept.astype(F32) + came.astype(F32)).astype(BF)]
    ppermute x42 -> x43, starting transfers between devices: 41.2 us -> 39.9 us  [swap(): lax.ppermute(value, axis, [(i, i ^ bit) for i in range(lax.axis_size(axis...]
  transfers between devices with their start and end apart: 42 -> 43, of which waited for: 22 -> 18; matrix products, arithmetic and copies ran while one was open for 16% -> 13% of each run, Pallas kernels for 10% -> 11%
where the time goes in v3:
time: 220 us
  waiting for transfers between devices  105 us (48%)
  starting transfers between devices  39.9 us (18%)
  Pallas kernels  24.9 us (11%)
  matrix products  17 us (8%)
  other arithmetic  15.9 us (7%)
  local copies, waits for them, and re-layouts  14.5 us (7%)
  between operations  2.97 us (1%)
    ppermute x43, waiting for transfers between devices, swap(): lax.ppermute(value, axis, [(i, i ^ bit) for i in range(lax.axis_size(axis...  105 us
    ppermute x43, starting transfers between devices, swap(): lax.ppermute(value, axis, [(i, i ^ bit) for i in range(lax.axis_size(axis...  39.9 us
    pallas_call x2, Pallas kernels, run_kernel(): pl.pallas_call(kernel, out_shape=[jax.ShapeDtypeStruct(shape, kind) for s...  24.9 us
    dot_general x5, matrix products, mm(): return jnp.dot(a, b, preferred_element_type=F32)  6.69 us
    convert_element_type x16, other arithmetic, add2(): return (kept.astype(F32) + came.astype(F32)).astype(BF)  4.89 us
    dot_general x4, matrix products, mm_t(): lax.dot_general(a, b, (((1,), (1,)), ((), ())), preferred_element_type=F32)  4.55 us
  transfers between devices with their start and end apart: 43, of which 18 were waited for; matrix products, arithmetic and copies ran while one was open for 13% of the time, Pallas kernels for 11%

profile of v3, /device:TPU:0, one launch (start us, length us, event | category | flops | bytes accessed | tf_op | source)
XLA Modules:
  0.0 219.7 jit_solution(15906117241390163520)
XLA Ops:
  2.8 5.1 %collective-permute-start.2 = (bf16[32,2560]{1,0:T(8,128)(2,1)S(1)}, bf16[32,2560]{1,0:T(8,128)(2,1)S(1)}, u32[]{:S(2)}, u32[]{:S(2)}) collective-permute-start(bf16[32,2560]{1,0:T(8,128)(2,1)S(1)} %scatter.4), channel_id=1, source_target_pairs={{0,24},{4,28},{8,16},{12,20},{16,8},{20,12},{24,0},{28,4},{1,25},{... | collective-permute-start | bytes 491528 | tf_op jit(solution)/shard_map/ppermute | solution.py:260
  10.2 1.7 collective-permute-start.3
  17.5 1.5 fusion.21.grad_out_ref
  20.1 1.7 fusion.17.rows_ref
  24.0 1.5 collective-permute-start.5
  26.1 6.2 %collective-permute-done.7 = bf16[2,128,640]{2,1,0:T(8,128)(2,1)S(1)} collective-permute-done((bf16[2,128,640]{2,1,0:T(8,128)(2,1)S(1)}, bf16[2,128,640]{2,1,0:T(8,128)(2,1)S(1)}, u32[]{:S(2)}, u32[]{:S(2)}) %collective-permute-start.7) | collective-permute-done | bytes 327712 | tf_op jit(solution)/shard_map/ppermute | solution.py:260
  33.6 1.6 collective-permute-start.10
  35.3 1.6 collective-permute-start.9
  36.9 2.9 %collective-permute-start.11 = (bf16[2,128,640]{2,1,0:T(8,128)(2,1)S(1)}, bf16[2,128,640]{2,1,0:T(8,128)(2,1)S(1)}, u32[]{:S(2)}, u32[]{:S(2)}) collective-permute-start(bf16[2,128,640]{2,1,0:T(8,128)(2,1)S(1)} %slice.170), channel_id=1, source_target_pairs={{0,16},{4,20},{8,24},{12,28},{16,0},{20,4},{24,8},{28,12},{1,17},{... | collective-permute-start | bytes 983048 | tf_op jit(solution)/shard_map/ppermute | solution.py:260
  40.3 12.7 %collective-permute-done.8 = bf16[128,640]{1,0:T(8,128)(2,1)S(1)} collective-permute-done((bf16[128,640]{1,0:T(8,128)(2,1)S(1)}, bf16[128,640]{1,0:T(8,128)(2,1)S(1)}, u32[]{:S(2)}, u32[]{:S(2)}) %collective-permute-start.8) | collective-permute-done | bytes 163872 | tf_op jit(solution)/shard_map/ppermute | solution.py:260
  56.8 7.0 %collective-permute-done.15 = bf16[128,1024]{1,0:T(8,128)(2,1)S(1)} collective-permute-done((bf16[128,1024]{1,0:T(8,128)(2,1)S(1)}, bf16[128,1024]{1,0:T(8,128)(2,1)S(1)}, u32[]{:S(2)}, u32[]{:S(2)}) %collective-permute-start.15) | collective-permute-done | bytes 262176 | tf_op jit(solution)/shard_map/ppermute | solution.py:260
  67.5 2.9 %collective-permute-start.18 = (bf16[2,128,640]{2,1,0:T(8,128)(2,1)S(1)}, bf16[2,128,640]{2,1,0:T(8,128)(2,1)S(1)}, u32[]{:S(2)}, u32[]{:S(2)}) collective-permute-start(bf16[2,128,640]{2,1,0:T(8,128)(2,1)S(1)} %pad_maximum_fusion.16), channel_id=1, source_target_pairs={{0,16},{4,20},{8,24},{12,28},{16,0},{20,4},{24,8},{28,12},{1,17},{... | collective-permute-start | bytes 983048 | tf_op jit(solution)/shard_map/ppermute | solution.py:260
  71.8 12.2 %attn_forward.1 = (bf16[128,1024]{1,0:T(8,128)(2,1)}, bf16[128,1280]{1,0:T(8,128)(2,1)}, bf16[128,384]{1,0:T(8,128)(2,1)}, f32[128,15]{1,0:T(8,128)}, bf16[128,1...) custom-call(s32[2]{0:T(128)} %pad_add_fusion.place_ref, ...), custom_call_target="tpu_custom_call" | custom-call | flops 1000 | bytes 1000 | tf_op jit(solution)/shard_map/attn_forward/pallas_call | solution.py:498
  84.0 1.5 collective-permute-start.16
  85.5 5.9 %collective-permute-done.16 = bf16[128,1024]{1,0:T(8,128)(2,1)S(1)} collective-permute-done((bf16[128,1024]{1,0:T(8,128)(2,1)}, bf16[128,1024]{1,0:T(8,128)(2,1)S(1)}, u32[]{:S(2)}, u32[]{:S(2)}) %collective-permute-start.16) | collective-permute-done | bytes 262176 | tf_op jit(solution)/shard_map/ppermute | solution.py:260
  94.7 8.2 %collective-permute-done.22 = bf16[2,128,640]{2,1,0:T(8,128)(2,1)S(1)} collective-permute-done((bf16[2,128,640]{2,1,0:T(8,128)(2,1)S(1)}, bf16[2,128,640]{2,1,0:T(8,128)(2,1)S(1)}, u32[]{:S(2)}, u32[]{:S(2)}) %collective-permute-start.22) | collective-permute-done | bytes 327712 | tf_op jit(solution)/shard_map/ppermute | solution.py:260
  116.9 1.5 collective-permute-start.24
  118.3 11.3 %collective-permute-done.25 = bf16[2,2,128,640]{3,2,1,0:T(8,128)(2,1)S(1)} collective-permute-done((bf16[2,2,128,640]{3,2,1,0:T(8,128)(2,1)S(1)}, bf16[2,2,128,640]{3,2,1,0:T(8,128)(2,1)S(1)}, u32[]{:S(2)}, u32[]{:S(2)}) %collective-permute-start.25) | collective-permute-done | bytes 655392 | tf_op jit(solution)/shard_map/ppermute | solution.py:260
  130.8 1.7 slice_bitcast_fusion.16.grad_a_ref
  132.5 12.7 %attn_backward.1 = (bf16[512,1280]{1,0:T(8,128)(2,1)}, bf16[512,1280]{1,0:T(8,128)(2,1)}, bf16[512,1280]{1,0:T(8,128)(2,1)}, bf16[512,1280]{1,0:T(8,128)(2,1)}, f32[128,1024]{1,0:T(8,128)}) custom-call(s32[2]{0:T(128)} %pad_add_fusion.place_ref, bf16[128,1024]{1,0:T(8,128)(2,1)} %slice_bitcast_fusion.16.grad_a_ref, bf16[128,1024]{1,0:T(8,128)(2,1)} %copy-done.16, ...), custom_call_target="tpu_custom_call" | custom-call | flops 1000 | bytes 1000 | tf_op jit(solution)/shard_map/attn_backward/pallas_call | solution.py:498
  145.2 3.0 %collective-permute-done.26 = bf16[2,128,640]{2,1,0:T(8,128)(2,1)} collective-permute-done((bf16[2,128,640]{2,1,0:T(8,128)(2,1)}, bf16[2,128,640]{2,1,0:T(8,128)(2,1)}, u32[]{:S(2)}, u32[]{:S(2)}) %collective-permute-start.26) | collective-permute-done | bytes 327712 | tf_op jit(solution)/shard_map/ppermute | solution.py:260
  148.8 1.6 fusion.4
  153.4 4.5 %collective-permute-done.31 = bf16[128,640]{1,0:T(8,128)(2,1)S(1)} collective-permute-done((bf16[128,640]{1,0:T(8,128)(2,1)S(1)}, bf16[128,640]{1,0:T(8,128)(2,1)S(1)}, u32[]{:S(2)}, u32[]{:S(2)}) %collective-permute-start.31) | collective-permute-done | bytes 163872 | tf_op jit(solution)/shard_map/ppermute | solution.py:260
  157.9 9.3 %collective-permute-done.30 = bf16[2,2,128,640]{3,2,1,0:T(8,128)(2,1)S(1)} collective-permute-done((bf16[2,2,128,640]{3,2,1,0:T(8,128)(2,1)S(1)}, bf16[2,2,128,640]{3,2,1,0:T(8,128)(2,1)S(1)}, u32[]{:S(2)}, u32[]{:S(2)}) %collective-permute-start.30) | collective-permute-done | bytes 655392 | tf_op jit(solution)/shard_map/ppermute | solution.py:260
  171.7 2.7 %fusion.1 = f32[128,960]{0,1:T(8,128)} fusion(f32[128,1024]{1,0:T(8,128)S(1)} %copy-done.22, s32[1024]{0:T(1024)S(1)} %fusion.62), kind=kOutput, calls=%fused_computation.2 | convolution fusion | flops 1510932480 | bytes 1019904 | tf_op jit(solution)/shard_map/dot_general | solution.py:689
  174.4 14.4 %collective-permute-done.34 = bf16[2,128,640]{2,1,0:T(8,128)(2,1)S(1)} collective-permute-done((bf16[2,128,640]{2,1,0:T(8,128)(2,1)S(1)}, bf16[2,128,640]{2,1,0:T(8,128)(2,1)S(1)}, u32[]{:S(2)}, u32[]{:S(2)}) %collective-permute-start.34) | collective-permute-done | bytes 327712 | tf_op jit(solution)/shard_map/ppermute | solution.py:260
  190.0 1.5 collective-permute-start.36
  193.3 6.6 %collective-permute-done.37 = bf16[4,32,1280]{2,1,0:T(8,128)(2,1)S(1)} collective-permute-done((bf16[4,32,1280]{2,1,0:T(8,128)(2,1)S(1)}, bf16[4,32,1280]{2,1,0:T(8,128)(2,1)S(1)}, u32[]{:S(2)}, u32[]{:S(2)}) %collective-permute-start.37) | collective-permute-done | bytes 327712 | tf_op jit(solution)/shard_map/ppermute | solution.py:260
  201.3 4.3 %collective-permute-done.40 = bf16[128,1024]{1,0:T(8,128)(2,1)S(1)} collective-permute-done((bf16[128,1024]{1,0:T(8,128)(2,1)S(1)}, bf16[128,1024]{1,0:T(8,128)(2,1)S(1)}, u32[]{:S(2)}, u32[]{:S(2)}) %collective-permute-start.40) | collective-permute-done | bytes 262176 | tf_op jit(solution)/shard_map/ppermute | solution.py:260
  205.6 4.3 %collective-permute-done.41 = bf16[3,32,1280]{2,1,0:T(8,128)(2,1)S(1)} collective-permute-done((bf16[3,32,1280]{2,1,0:T(8,128)(2,1)S(1)}, bf16[3,32,1280]{2,1,0:T(8,128)(2,1)S(1)}, u32[]{:S(2)}, u32[]{:S(2)}) %collective-permute-start.41) | collective-permute-done | bytes 245792 | tf_op jit(solution)/shard_map/ppermute | solution.py:260
  212.5 1.5 fusion.20
  214.0 4.2 %collective-permute-done.42 = bf16[32,2560]{1,0:T(8,128)(2,1)S(1)} collective-permute-done((bf16[32,2560]{1,0:T(8,128)(2,1)S(1)}, bf16[32,2560]{1,0:T(8,128)(2,1)S(1)}, u32[]{:S(2)}, u32[]{:S(2)}) %collective-permute-start.42) | collective-permute-done | bytes 163872 | tf_op jit(solution)/shard_map/ppermute | solution.py:260
  (230 shorter events, 57.2 us)
Async XLA Ops:
  2.8 19.2 %collective-permute-start.2 = (bf16[32,2560]{1,0:T(8,128)(2,1)S(1)}, bf16[32,2560]{1,0:T(8,128)(2,1)S(1)}, u32[]{:S(2)}, u32[]{:S(2)}) collective-permute-start(bf16[32,2560]{1,0:T(8,128)(2,1)S(1)} %scatter.4), channel_id=1, source_target_pairs={{0,24},{4,28},{8,16},{12,20},{16,8},{20,12},{24,0},{28,4},{1,25},{... | collective-permute-start | bytes 491528 | tf_op jit(solution)/shard_map/ppermute | solution.py:260
  7.9 14.1 %collective-permute-start.1 = (bf16[32,2560]{1,0:T(8,128)(2,1)S(1)}, bf16[32,2560]{1,0:T(8,128)(2,1)S(1)}, u32[]{:S(2)}, u32[]{:S(2)}) collective-permute-start(bf16[32,2560]{1,0:T(8,128)(2,1)S(1)} %scatter.4), channel_id=1, source_target_pairs={{0,16},{4,20},{8,24},{12,28},{16,0},{20,4},{24,8},{28,12},{1,17},{... | collective-permute-start | bytes 491528 | tf_op jit(solution)/shard_map/ppermute | solution.py:260
  7.9 14.1 %collective-permute-start = (bf16[32,2560]{1,0:T(8,128)(2,1)S(1)}, bf16[32,2560]{1,0:T(8,128)(2,1)S(1)}, u32[]{:S(2)}, u32[]{:S(2)}) collective-permute-start(bf16[32,2560]{1,0:T(8,128)(2,1)S(1)} %scatter.4), channel_id=1, source_target_pairs={{0,8},{4,12},{8,0},{12,4},{16,24},{20,28},{24,16},{28,20},{1,9},{5... | collective-permute-start | bytes 491528 | tf_op jit(solution)/shard_map/ppermute | solution.py:260
  22.1 10.2 %collective-permute-start.7 = (bf16[2,128,640]{2,1,0:T(8,128)(2,1)S(1)}, bf16[2,128,640]{2,1,0:T(8,128)(2,1)S(1)}, u32[]{:S(2)}, u32[]{:S(2)}) collective-permute-start(bf16[2,128,640]{2,1,0:T(8,128)(2,1)S(1)} %slice.170), channel_id=1, source_target_pairs={{0,8},{4,12},{8,0},{12,4},{16,24},{20,28},{24,16},{28,20},{1,9},{5... | collective-permute-start | bytes 983048 | tf_op jit(solution)/shard_map/ppermute | solution.py:260
  23.5 9.8 %collective-permute-start.6 = (bf16[4,32,1280]{2,1,0:T(8,128)(2,1)S(1)}, bf16[4,32,1280]{2,1,0:T(8,128)(2,1)S(1)}, u32[]{:S(2)}, u32[]{:S(2)}) collective-permute-start(bf16[4,32,1280]{2,1,0:T(8,128)(2,1)S(1)} %get-tuple-element.120), channel_id=1, source_target_pairs={{0,2},{1,3},{2,0},{3,1},{4,6},{5,7},{6,4},{7,5},{8,10},{9,11},{10,... | collective-permute-start | bytes 983048 | tf_op jit(solution)/shard_map/ppermute | solution.py:260
  33.6 19.5 %collective-permute-start.10 = (bf16[4,2,32,1280]{3,2,1,0:T(8,128)(2,1)S(1)}, bf16[4,2,32,1280]{3,2,1,0:T(8,128)(2,1)S(1)}, u32[]{:S(2)}, u32[]{:S(2)}) collective-permute-start(bf16[4,2,32,1280]{3,2,1,0:T(8,128)(2,1)S(1)} %pad_maximum_fusion.10), channel_id=1, source_target_pairs={{0,4},{4,0},{8,12},{12,8},{16,20},{20,16},{24,28},{28,24},{1,5},{5... | collective-permute-start | bytes 1966088 | tf_op jit(solution)/shard_map/ppermute | solution.py:260
  35.3 17.9 %collective-permute-start.9 = (bf16[2,4,32,1280]{3,2,1,0:T(8,128)(2,1)S(1)}, bf16[2,4,32,1280]{3,2,1,0:T(8,128)(2,1)S(1)}, u32[]{:S(2)}, u32[]{:S(2)}) collective-permute-start(bf16[2,4,32,1280]{3,2,1,0:T(8,128)(2,1)S(1)} %pad_maximum_fusion.9), channel_id=1, source_target_pairs={{0,2},{1,3},{2,0},{3,1},{4,6},{5,7},{6,4},{7,5},{8,10},{9,11},{10,... | collective-permute-start | bytes 1966088 | tf_op jit(solution)/shard_map/ppermute | solution.py:260
  36.9 16.3 %collective-permute-start.11 = (bf16[2,128,640]{2,1,0:T(8,128)(2,1)S(1)}, bf16[2,128,640]{2,1,0:T(8,128)(2,1)S(1)}, u32[]{:S(2)}, u32[]{:S(2)}) collective-permute-start(bf16[2,128,640]{2,1,0:T(8,128)(2,1)S(1)} %slice.170), channel_id=1, source_target_pairs={{0,16},{4,20},{8,24},{12,28},{16,0},{20,4},{24,8},{28,12},{1,17},{... | collective-permute-start | bytes 983048 | tf_op jit(solution)/shard_map/ppermute | solution.py:260
  39.8 13.3 %collective-permute-start.8 = (bf16[128,640]{1,0:T(8,128)(2,1)S(1)}, bf16[128,640]{1,0:T(8,128)(2,1)S(1)}, u32[]{:S(2)}, u32[]{:S(2)}) collective-permute-start(bf16[128,640]{1,0:T(8,128)(2,1)S(1)} %slice_bitcast_fusion.21), channel_id=1, source_target_pairs={{0,4},{4,0},{8,12},{12,8},{16,20},{20,16},{24,28},{28,24},{1,5},{5... | collective-permute-start | bytes 491528 | tf_op jit(solution)/shard_map/ppermute | solution.py:260
  53.8 11.0 %collective-permute-start.13 = (bf16[512,1280]{1,0:T(8,128)(2,1)S(1)}, bf16[512,1280]{1,0:T(8,128)(2,1)S(1)}, u32[]{:S(2)}, u32[]{:S(2)}) collective-permute-start(bf16[512,1280]{1,0:T(8,128)(2,1)S(1)} %bitcast.238), channel_id=1, source_target_pairs={{0,1},{1,0},{2,3},{3,2},{4,5},{5,4},{6,7},{7,6},{8,9},{9,8},{10,11... | collective-permute-start | bytes 3932168 | tf_op jit(solution)/shard_map/ppermute | solution.py:260
  54.7 10.1 %collective-permute-start.12 = (bf16[512,1280]{1,0:T(8,128)(2,1)S(1)}, bf16[512,1280]{1,0:T(8,128)(2,1)S(1)}, u32[]{:S(2)}, u32[]{:S(2)}) collective-permute-start(bf16[512,1280]{1,0:T(8,128)(2,1)S(1)} %bitcast.236), channel_id=1, source_target_pairs={{0,1},{1,0},{2,3},{3,2},{4,5},{5,4},{6,7},{7,6},{8,9},{9,8},{10,11... | collective-permute-start | bytes 3932168 | tf_op jit(solution)/shard_map/ppermute | solution.py:260
  54.7 10.1 %collective-permute-start.14 = (bf16[2,128,640]{2,1,0:T(8,128)(2,1)S(1)}, bf16[2,128,640]{2,1,0:T(8,128)(2,1)S(1)}, u32[]{:S(2)}, u32[]{:S(2)}) collective-permute-start(bf16[2,128,640]{2,1,0:T(8,128)(2,1)S(1)} %collective-permute-done.11), channel_id=1, source_target_pairs={{0,8},{4,12},{8,0},{12,4},{16,24},{20,28},{24,16},{28,20},{1,9},{5... | collective-permute-start | bytes 983048 | tf_op jit(solution)/shard_map/ppermute | solution.py:260
  66.1 36.8 %collective-permute-start.21 = (bf16[4,2,128,640]{3,2,0,1:T(8,128)(2,1)S(1)}, bf16[4,2,128,640]{3,2,0,1:T(8,128)(2,1)S(1)}, u32[]{:S(2)}, u32[]{:S(2)}) collective-permute-start(bf16[4,2,128,640]{3,2,0,1:T(8,128)(2,1)S(1)} %copy.67), channel_id=1, source_target_pairs={{0,4},{4,0},{8,12},{12,8},{16,20},{20,16},{24,28},{28,24},{1,5},{5... | collective-permute-start | bytes 3932168 | tf_op jit(solution)/shard_map/ppermute | solution.py:260
  67.5 23.9 %collective-permute-start.18 = (bf16[2,128,640]{2,1,0:T(8,128)(2,1)S(1)}, bf16[2,128,640]{2,1,0:T(8,128)(2,1)S(1)}, u32[]{:S(2)}, u32[]{:S(2)}) collective-permute-start(bf16[2,128,640]{2,1,0:T(8,128)(2,1)S(1)} %pad_maximum_fusion.16), channel_id=1, source_target_pairs={{0,16},{4,20},{8,24},{12,28},{16,0},{20,4},{24,8},{28,12},{1,17},{... | collective-permute-start | bytes 983048 | tf_op jit(solution)/shard_map/ppermute | solution.py:260
  70.5 21.0 %collective-permute-start.17 = (bf16[2,128,640]{2,1,0:T(8,128)(2,1)S(1)}, bf16[2,128,640]{2,1,0:T(8,128)(2,1)S(1)}, u32[]{:S(2)}, u32[]{:S(2)}) collective-permute-start(bf16[2,128,640]{2,1,0:T(8,128)(2,1)S(1)} %pad_maximum_fusion.16), channel_id=1, source_target_pairs={{0,8},{4,12},{8,0},{12,4},{16,24},{20,28},{24,16},{28,20},{1,9},{5... | collective-permute-start | bytes 983048 | tf_op jit(solution)/shard_map/ppermute | solution.py:260
  92.5 10.4 %collective-permute-start.19 = (bf16[2,128,1024]{2,1,0:T(8,128)(2,1)S(1)}, bf16[2,128,1024]{2,1,0:T(8,128)(2,1)S(1)}, u32[]{:S(2)}, u32[]{:S(2)}) collective-permute-start(bf16[2,128,1024]{2,1,0:T(8,128)(2,1)S(1)} %get-tuple-element.223), channel_id=1, source_target_pairs={{0,1},{1,0},{2,3},{3,2},{4,5},{5,4},{6,7},{7,6},{8,9},{9,8},{10,11... | collective-permute-start | bytes 1572872 | tf_op jit(solution)/shard_map/ppermute | solution.py:260
  92.7 10.2 %collective-permute-start.20 = (bf16[2,128,1024]{2,1,0:T(8,128)(2,1)S(1)}, bf16[2,128,1024]{2,1,0:T(8,128)(2,1)S(1)}, u32[]{:S(2)}, u32[]{:S(2)}) collective-permute-start(bf16[2,128,1024]{2,1,0:T(8,128)(2,1)S(1)} %get-tuple-element.221), channel_id=1, source_target_pairs={{0,1},{1,0},{2,3},{3,2},{4,5},{5,4},{6,7},{7,6},{8,9},{9,8},{10,11... | collective-permute-start | bytes 1572872 | tf_op jit(solution)/shard_map/ppermute | solution.py:260
  93.2 9.7 %collective-permute-start.22 = (bf16[2,128,640]{2,1,0:T(8,128)(2,1)S(1)}, bf16[2,128,640]{2,1,0:T(8,128)(2,1)S(1)}, u32[]{:S(2)}, u32[]{:S(2)}) collective-permute-start(bf16[2,128,640]{2,1,0:T(8,128)(2,1)S(1)} %collective-permute-done.18), channel_id=1, source_target_pairs={{0,8},{4,12},{8,0},{12,4},{16,24},{20,28},{24,16},{28,20},{1,9},{5... | collective-permute-start | bytes 983048 | tf_op jit(solution)/shard_map/ppermute | solution.py:260
  112.4 17.2 %collective-permute-start.25 = (bf16[2,2,128,640]{3,2,1,0:T(8,128)(2,1)S(1)}, bf16[2,2,128,640]{3,2,1,0:T(8,128)(2,1)S(1)}, u32[]{:S(2)}, u32[]{:S(2)}) collective-permute-start(bf16[2,2,128,640]{3,2,1,0:T(8,128)(2,1)S(1)} %slice_bitcast_fusion.3), channel_id=1, source_target_pairs={{0,8},{4,12},{8,0},{12,4},{16,24},{20,28},{24,16},{28,20},{1,9},{5... | collective-permute-start | bytes 1966088 | tf_op jit(solution)/shard_map/ppermute | solution.py:260
  116.1 32.2 %collective-permute-start.27 = (bf16[2,4,128,640]{3,2,1,0:T(8,128)(2,1)}, bf16[2,4,128,640]{3,2,1,0:T(8,128)(2,1)}, u32[]{:S(2)}, u32[]{:S(2)}) collective-permute-start(bf16[2,4,128,640]{3,2,1,0:T(8,128)(2,1)} %fusion.10), channel_id=1, source_target_pairs={{0,4},{4,0},{8,12},{12,8},{16,20},{20,16},{24,28},{28,24},{1,5},{5... | collective-permute-start | bytes 3932168 | tf_op jit(solution)/shard_map/ppermute | solution.py:260
  116.9 12.8 %collective-permute-start.24 = (bf16[128,1024]{1,0:T(8,128)(2,1)S(1)}, bf16[128,1024]{1,0:T(8,128)(2,1)S(1)}, u32[]{:S(2)}, u32[]{:S(2)}) collective-permute-start(bf16[128,1024]{1,0:T(8,128)(2,1)S(1)} %slice.249), channel_id=1, source_target_pairs={{0,2},{1,3},{2,0},{3,1},{4,6},{5,7},{6,4},{7,5},{8,10},{9,11},{10,... | collective-permute-start | bytes 786440 | tf_op jit(solution)/shard_map/ppermute | solution.py:260
  130.6 17.7 %collective-permute-start.26 = (bf16[2,128,640]{2,1,0:T(8,128)(2,1)}, bf16[2,128,640]{2,1,0:T(8,128)(2,1)}, u32[]{:S(2)}, u32[]{:S(2)}) collective-permute-start(bf16[2,128,640]{2,1,0:T(8,128)(2,1)} %slice_bitcast_fusion.15), channel_id=1, source_target_pairs={{0,16},{4,20},{8,24},{12,28},{16,0},{20,4},{24,8},{28,12},{1,17},{... | collective-permute-start | bytes 983048 | tf_op jit(solution)/shard_map/ppermute | solution.py:260
  148.2 18.9 %collective-permute-start.28 = (bf16[512,1280]{1,0:T(8,128)(2,1)}, bf16[512,1280]{1,0:T(8,128)(2,1)S(1)}, u32[]{:S(2)}, u32[]{:S(2)}) collective-permute-start(bf16[512,1280]{1,0:T(8,128)(2,1)} %get-tuple-element.174), channel_id=1, source_target_pairs={{0,1},{1,0},{2,3},{3,2},{4,5},{5,4},{6,7},{7,6},{8,9},{9,8},{10,11... | collective-permute-start | bytes 3932168 | tf_op jit(solution)/shard_map/ppermute | solution.py:260
  148.2 18.9 %collective-permute-start.29 = (bf16[512,1280]{1,0:T(8,128)(2,1)}, bf16[512,1280]{1,0:T(8,128)(2,1)S(1)}, u32[]{:S(2)}, u32[]{:S(2)}) collective-permute-start(bf16[512,1280]{1,0:T(8,128)(2,1)} %get-tuple-element.175), channel_id=1, source_target_pairs={{0,1},{1,0},{2,3},{3,2},{4,5},{5,4},{6,7},{7,6},{8,9},{9,8},{10,11... | collective-permute-start | bytes 3932168 | tf_op jit(solution)/shard_map/ppermute | solution.py:260
  150.5 16.7 %collective-permute-start.30 = (bf16[2,2,128,640]{3,2,1,0:T(8,128)(2,1)S(1)}, bf16[2,2,128,640]{3,2,1,0:T(8,128)(2,1)S(1)}, u32[]{:S(2)}, u32[]{:S(2)}) collective-permute-start(bf16[2,2,128,640]{3,2,1,0:T(8,128)(2,1)S(1)} %slice_bitcast_fusion.1), channel_id=1, source_target_pairs={{0,8},{4,12},{8,0},{12,4},{16,24},{20,28},{24,16},{28,20},{1,9},{5... | collective-permute-start | bytes 1966088 | tf_op jit(solution)/shard_map/ppermute | solution.py:260
  169.3 19.4 %collective-permute-start.35 = (bf16[256,1024]{1,0:T(8,128)(2,1)S(1)}, bf16[256,1024]{1,0:T(8,128)(2,1)S(1)}, u32[]{:S(2)}, u32[]{:S(2)}) collective-permute-start(bf16[256,1024]{1,0:T(8,128)(2,1)S(1)} %slice.261), channel_id=1, source_target_pairs={{0,1},{1,0},{2,3},{3,2},{4,5},{5,4},{6,7},{7,6},{8,9},{9,8},{10,11... | collective-permute-start | bytes 1572872 | tf_op jit(solution)/shard_map/ppermute | solution.py:260
  169.5 19.3 %collective-permute-start.32 = (bf16[2,4,32,1280]{3,2,1,0:T(8,128)(2,1)S(1)}, bf16[2,4,32,1280]{3,2,1,0:T(8,128)(2,1)S(1)}, u32[]{:S(2)}, u32[]{:S(2)}) collective-permute-start(bf16[2,4,32,1280]{3,2,1,0:T(8,128)(2,1)S(1)} %dynamic-slice_bitcast_fusion), channel_id=1, source_target_pairs={{0,2},{1,3},{2,0},{3,1},{4,6},{5,7},{6,4},{7,5},{8,10},{9,11},{10,... | collective-permute-start | bytes 1966088 | tf_op jit(solution)/shard_map/ppermute | solution.py:260
  171.0 17.8 %collective-permute-start.33 = (bf16[4,2,32,1280]{3,2,1,0:T(8,128)(2,1)S(1)}, bf16[4,2,32,1280]{3,2,1,0:T(8,128)(2,1)S(1)}, u32[]{:S(2)}, u32[]{:S(2)}) collective-permute-start(bf16[4,2,32,1280]{3,2,1,0:T(8,128)(2,1)S(1)} %bitcast.274), channel_id=1, source_target_pairs={{0,4},{4,0},{8,12},{12,8},{16,20},{20,16},{24,28},{28,24},{1,5},{5... | collective-permute-start | bytes 1966088 | tf_op jit(solution)/shard_map/ppermute | solution.py:260
  171.5 17.3 %collective-permute-start.34 = (bf16[2,128,640]{2,1,0:T(8,128)(2,1)S(1)}, bf16[2,128,640]{2,1,0:T(8,128)(2,1)S(1)}, u32[]{:S(2)}, u32[]{:S(2)}) collective-permute-start(bf16[2,128,640]{2,1,0:T(8,128)(2,1)S(1)} %slice_bitcast_fusion.13), channel_id=1, source_target_pairs={{0,16},{4,20},{8,24},{12,28},{16,0},{20,4},{24,8},{28,12},{1,17},{... | collective-permute-start | bytes 983048 | tf_op jit(solution)/shard_map/ppermute | solution.py:260
  189.3 10.6 %collective-permute-start.37 = (bf16[4,32,1280]{2,1,0:T(8,128)(2,1)S(1)}, bf16[4,32,1280]{2,1,0:T(8,128)(2,1)S(1)}, u32[]{:S(2)}, u32[]{:S(2)}) collective-permute-start(bf16[4,32,1280]{2,1,0:T(8,128)(2,1)S(1)} %dynamic-slice_bitcast_fusion.1), channel_id=1, source_target_pairs={{0,2},{1,3},{2,0},{3,1},{4,6},{5,7},{6,4},{7,5},{8,10},{9,11},{10,... | collective-permute-start | bytes 983048 | tf_op jit(solution)/shard_map/ppermute | solution.py:260
  190.0 10.0 %collective-permute-start.36 = (bf16[4,32,1280]{2,1,0:T(8,128)(2,1)S(1)}, bf16[4,32,1280]{2,1,0:T(8,128)(2,1)S(1)}, u32[]{:S(2)}, u32[]{:S(2)}) collective-permute-start(bf16[4,32,1280]{2,1,0:T(8,128)(2,1)S(1)} %slice_bitcast_fusion.11), channel_id=1, source_target_pairs={{0,4},{4,0},{8,12},{12,8},{16,20},{20,16},{24,28},{28,24},{1,5},{5... | collective-permute-start | bytes 983048 | tf_op jit(solution)/shard_map/ppermute | solution.py:260
  191.8 13.7 %collective-permute-start.40 = (bf16[128,1024]{1,0:T(8,128)(2,1)S(1)}, bf16[128,1024]{1,0:T(8,128)(2,1)S(1)}, u32[]{:S(2)}, u32[]{:S(2)}) collective-permute-start(bf16[128,1024]{1,0:T(8,128)(2,1)S(1)} %slice.269), channel_id=1, source_target_pairs={{0,2},{1,3},{2,0},{3,1},{4,6},{5,7},{6,4},{7,5},{8,10},{9,11},{10,... | collective-permute-start | bytes 786440 | tf_op jit(solution)/shard_map/ppermute | solution.py:260
  (37 other events, 206.2 us)

commit v4 on v3

--- a/solution.py
+++ b/solution.py
@@ -348,7 +348,7 @@
     def kernel(
         place_ref, rows_ref, owner_ref, inner_ref, cos_ref, sin_ref, seg_ref,
         own_q_ref, came_q_ref, own_o_ref, came_o_ref,
-        input1_ref, qk_ref, v_ref, logsum_ref, att_ref, hidden1_ref, input2_ref, gains_ref, attn_q_ref, attn_o_ref,
+        att_ref, qk_ref, v_ref, logsum_ref, hidden1_ref, input2_ref, gains_ref, attn_q_ref, attn_o_ref,
     ):
         core = place_ref[1]
         for p in range(own_q_ref.shape[0] // padded):
@@ -372,7 +372,6 @@
         rows = rows_ref[...]
         normed, _ = norm_rows(rows)
         input1 = (normed * gain1).astype(BF)
-        input1_ref[...] = input1
         projected = dot_f(input1, attn_q_ref[...])
         cosine = cos_ref[...]
         sine = sin_ref[...]
@@ -384,7 +383,8 @@
         values = dot_f(input1, attn_o_ref[:, :384]).astype(BF)
         v_ref[...] = values
         allowed = seg_ref[...] > 0.0
-        att_ref[:, :384] = jnp.zeros((rows.shape[0], 384), BF)
+        att_ref[:, :128] = jnp.zeros((rows.shape[0], 128), BF)
+        shift = kv_width - 256
         for k in range(KV):
             keys = qk_ref[:, D + HD * k : D + HD * (k + 1)]
             value = values[:, HD * k : HD * (k + 1)]
@@ -397,8 +397,8 @@
                 total = jnp.sum(expo, axis=1, keepdims=True)
                 logsum_ref[:, h : h + 1] = top + jnp.log(total)
                 weights = (expo / total).astype(BF)
-                att_ref[:, kv_width + HD * h : kv_width + HD * (h + 1)] = dot_f(weights, value).astype(BF)
-        hidden1 = rows + dot_t(att_ref[...], attn_o_ref[...])
+                att_ref[:, shift + HD * h : shift + HD * (h + 1)] = dot_f(weights, value).astype(BF)
+        hidden1 = rows + dot_t(att_ref[...], attn_o_ref[:, 256:])
         hidden1_ref[...] = hidden1
         normed2, _ = norm_rows(hidden1)
         input2_ref[...] = (normed2 * gain2).astype(BF)
@@ -406,32 +406,33 @@
     return kernel
 
 
-def make_backward(n_fsdp, own, padded, share):
+def norm_kernel(
+    place_ref, grad_a_ref, grad_b_ref, grad_out_ref, hidden1_ref, gains_ref,
+    grad_h1_ref, grad_h1b_ref, gain2_ref,
+):
+    grad_in2 = grad_a_ref[...].astype(F32) + grad_b_ref[...].astype(F32)
+    normed2, scale2 = norm_rows(hidden1_ref[...])
+    back2, gain2_term = norm_rows_back(grad_in2, normed2, scale2, gains_ref[1:2, :])
+    grad_h1 = grad_out_ref[...].astype(F32) + back2
+    grad_h1_ref[...] = grad_h1
+    grad_h1b_ref[...] = grad_h1.astype(BF)
+    gain2_ref[...] = gain2_term
+
+
+def make_backward(n_fsdp, own):
     kv_width = KV * HD
 
     def kernel(
-        place_ref, grad_a_ref, grad_b_ref, grad_out_ref, hidden1_ref, rows_ref, gains_ref, owner_ref, inner_ref,
-        spots_ref, cos_ref, sin_ref, seg_ref, input1_ref, qk_ref, v_ref, logsum_ref, att_ref,
-        attn_q_ref, attn_o_ref,
-        q_keep_ref, q_send_ref, o_keep_ref, o_send_ref, input_grad_ref,
-        left_ref, right_ref, turn_ref,
+        place_ref, grad_h1_ref, grad_h1b_ref, gain2_ref, rows_ref, gains_ref, owner_ref, inner_ref,
+        cos_ref, sin_ref, seg_ref, qk_ref, v_ref, logsum_ref, attn_q_ref, attn_o_ref,
+        grads_ref, input_grad_ref,
+        turn_ref,
     ):
         count = rows_ref.shape[0]
-        wide = rows_ref.shape[1]
-        core = place_ref[1]
-        gain1 = gains_ref[0:1, :]
-        gain2 = gains_ref[1:2, :]
-        grad_in2 = grad_a_ref[...].astype(F32) + grad_b_ref[...].astype(F32)
-        normed2, scale2 = norm_rows(hidden1_ref[...])
-        back2, gain2_term = norm_rows_back(grad_in2, normed2, scale2, gain2)
-        grad_h1 = grad_out_ref[...].astype(F32) + back2
-        grad_h1b = grad_h1.astype(BF)
-        left_ref[:count, :] = input1_ref[...]
-        left_ref[count:, :] = grad_h1b
-        right_ref[:count, :] = jnp.zeros((count, right_ref.shape[1]), BF)
-        right_ref[count:, :] = att_ref[...]
-        grad_att = dot_f(grad_h1b, attn_o_ref[...]).astype(BF)
+        qk_width = turn_ref.shape[1]
+        grad_att = dot_f(grad_h1b_ref[...], attn_o_ref[...]).astype(BF)
         allowed = seg_ref[...] > 0.0
+        grads_ref[:count, qk_width:] = jnp.zeros((count, 384), BF)
         for k in range(KV):
             keys = qk_ref[:, D + HD * k : D + HD * (k + 1)]
             value = v_ref[:, HD * k : HD * (k + 1)]
@@ -450,42 +451,77 @@
                 turn_ref[:, HD * h : HD * (h + 1)] = dot_f(score_grad, keys)
                 key_grad = key_grad + dot_0(score_grad, queries)
             turn_ref[:, D + HD * k : D + HD * (k + 1)] = key_grad
-            right_ref[:count, HD * k : HD * (k + 1)] = value_grad.astype(BF)
+            grads_ref[:count, qk_width + HD * k : qk_width + HD * (k + 1)] = value_grad.astype(BF)
         cosine = cos_ref[...]
         sine = sin_ref[...]
         low = first_half(cosine.shape)
-        pieces = []
-        for i in range(turn_ref.shape[1] // 128):
+        for i in range(qk_width // 128):
             part = turn_ref[:, 128 * i : 128 * (i + 1)]
             scaled = part * sine
             turned = jnp.where(low, pltpu.roll(scaled, 96, 1), -pltpu.roll(scaled, 32, 1))
-            pieces.append((part * cosine + turned).astype(BF))
-        proj_grad = jnp.concatenate(pieces, axis=1)
-        o_term = dot_0(left_ref[...], right_ref[...]).astype(BF)
+            grads_ref[:count, 128 * i : 128 * (i + 1)] = (part * cosine + turned).astype(BF)
         owner = owner_ref[...]
         inner = inner_ref[...]
-        grad_in1 = dot_t(proj_grad, attn_q_ref[...]) * jnp.where(inner < own, 1.0, 0.0) + dot_t(
-            right_ref[:count, :], attn_o_ref[...]
-        )
+        grad_in1 = dot_t(grads_ref[:count, :qk_width], attn_q_ref[...]) * jnp.where(inner < own, 1.0, 0.0)
+        grad_in1 = grad_in1 + dot_t(grads_ref[:count, qk_width:], attn_o_ref[:, :384])
         normed1, scale1 = norm_rows(rows_ref[...])
-        back1, gain1_term = norm_rows_back(grad_in1, normed1, scale1, gain1)
-        input_grad_ref[...] = grad_h1 + back1
-        first, second = gain_masks(owner, place_ref[0], n_fsdp, own, share)
-        both = jnp.where(first, gain1_term, 0.0) + jnp.where(second, gain2_term, 0.0)
-        gain_rows = dot_t(both.astype(BF), slot_matrix(owner, inner, own, 256)).astype(BF)
-        q_term = dot_0(input1_ref[...], proj_grad)
-        q_start = (q_term[:, :256] + dot_f(spots_ref[...], gain_rows)).astype(BF)
-        q_term = q_term.astype(BF)
-        q_term = jnp.concatenate([q_start, q_term[:, 256:]], axis=1)
-        low_core = core == 0
-        for p in range(wide // padded // 2):
-            even = slice(2 * p * padded, (2 * p + 1) * padded)
-            odd = slice((2 * p + 1) * padded, (2 * p + 2) * padded)
-            to = slice(p * padded, (p + 1) * padded)
-            q_keep_ref[to, :] = jnp.where(low_core, q_term[even, :], q_term[odd, :])
-            q_send_ref[to, :] = jnp.where(low_core, q_term[odd, :], q_term[even, :])
-            o_keep_ref[to, :] = jnp.where(low_core, o_term[even, :], o_term[odd, :])
-            o_send_ref[to, :] = jnp.where(low_core, o_term[odd, :], o_term[even, :])
+        back1, gain1_term = norm_rows_back(grad_in1, normed1, scale1, gains_ref[0:1, :])
+        input_grad_ref[...] = grad_h1_ref[...] + back1
+        first, second = gain_masks(owner, place_ref[0], n_fsdp, own, D * 2 // n_fsdp)
+        both = jnp.where(first, gain1_term, 0.0) + jnp.where(second, gain2_ref[...], 0.0)
+        gain_rows = dot_t(both.astype(BF), slot_matrix(owner, inner, own, 256))
+        extra = grads_ref.shape[0] - count
+        grads_ref[count:, :] = jnp.zeros((extra, grads_ref.shape[1]), BF)
+        gain_rows = jnp.concatenate([gain_rows, jnp.zeros((extra - n_fsdp, 256), F32)], axis=0)
+        grads_ref[count:, :256] = gain_rows.astype(BF)
+
+    return kernel
+
+
+def make_terms(n_far, n_sub, own, padded, count):
+    def kernel(place_ref, rows_ref, gains_ref, *refs):
+        att_refs = refs[:n_sub]
+        grad_h1_refs = refs[n_sub : 2 * n_sub]
+        grads_refs = refs[2 * n_sub : 3 * n_sub]
+        keep_ref, send_ref = refs[3 * n_sub :]
+        half_ff = FF // 2
+        rows = keep_ref.shape[0] * 2
+        wide = grad_h1_refs[0].shape[1]
+
+        def tokens(pieces):
+            return jnp.concatenate(pieces, axis=0)
+
+        spot = lax.broadcasted_iota(jnp.int32, (wide, rows), 1)
+        source = (spot // padded * n_sub + place_ref[2]) * padded + spot % padded
+        select = (lax.broadcasted_iota(jnp.int32, (wide, rows), 0) == source).astype(F32).astype(BF)
+        spot = lax.broadcasted_iota(jnp.int32, (D, rows), 1)
+        block = spot // padded
+        owner = ((block % n_far * 2 + block // n_far) ^ place_ref[0]) * n_sub + place_ref[2]
+        source = jnp.where(spot % padded < own, owner * own + spot % padded, -1)
+        select_d = (lax.broadcasted_iota(jnp.int32, (D, rows), 0) == source).astype(F32).astype(BF)
+        group = rows_ref[...].astype(F32)
+        scale = lax.rsqrt(jnp.sum(group * group, axis=1, keepdims=True) * (1.0 / D) + EPS)
+        gain = dot_f(gains_ref[...].astype(BF), select)[0:1, :]
+        left1 = (dot_f(rows_ref[...], select_d) * scale * gain).astype(BF)
+        left2 = dot_f(tokens([ref[...] for ref in grad_h1_refs]), select).astype(BF)
+        right = tokens([ref[:count, :] for ref in grads_refs])
+        extra = tokens([ref[count:, :256] for ref in grads_refs])
+        spot = lax.broadcasted_iota(jnp.int32, (extra.shape[0], rows), 1)
+        block = spot // padded
+        here = lax.broadcasted_iota(jnp.int32, spot.shape, 0) % (extra.shape[0] // n_sub)
+        wanted = jnp.where(spot % padded == own, block % n_far * 2 + block // n_far, -1)
+        spots = (here == wanted).astype(F32).astype(BF)
+        q_term = dot_0(left1, right)
+        start = q_term[:, :256] + dot_0(spots, extra)
+        o_term = dot_0(left2, tokens([ref[...] for ref in att_refs]))
+        mixed = o_term[:, :128] + q_term[:, half_ff + 256 :]
+        for ref, at in ((keep_ref, 0), (send_ref, rows // 2)):
+            to = slice(at, at + rows // 2)
+            ref[:, :256] = start[to, :].astype(BF)
+            ref[:, 256:half_ff] = q_term[to, 256:half_ff].astype(BF)
+            ref[:, half_ff : half_ff + 256] = q_term[to, half_ff : half_ff + 256].astype(BF)
+            ref[:, half_ff + 256 : half_ff + 384] = mixed[to, :].astype(BF)
+            ref[:, half_ff + 384 :] = o_term[to, 128:].astype(BF)
 
     return kernel
 
@@ -545,11 +581,9 @@
     sine = jnp.concatenate([sine, sine], axis=1)
     seg = allowed.astype(F32)
     rows32 = mm(rows, spread_mat)
-    grad_outb = (live * mm(cotangent, spread_mat)).astype(BF)
-
-    of_place = [(p // n_sub) % n_far * 2 + p // (n_sub * n_far) for p in range(n_all)]
-    at_spot = jnp.where(inner == own, jnp.array(of_place)[place], -1)
-    spots = (at_spot[:, None] == jnp.arange(n_fsdp)[None, :]).astype(BF)
+    cot = (live * cotangent.astype(F32)).astype(BF)
+    cot_y = swap(cot, "sub", 2)
+
     owner = ((rel ^ my_fsdp) * n_sub + place % n_sub)[None, :]
 
     attn_block = padded_block(attn_weight)
@@ -561,7 +595,7 @@
     came = swap(columns(mlp_block, 1 - my_c, quarter), "sub", 1)
     mlp_block = put2(columns(mlp_block, my_c, quarter), came, my_c, 2)
     mlp_block = mlp_block.reshape(3, n_sub * padded, quarter)
-    far, mlp_block = meet(far, mlp_block)
+    far, mlp_block, cot, cot_y = meet(far, mlp_block, cot, cot_y)
 
     attn_far = jnp.stack([attn_block] + list(far))
     half0 = attn_far[:, :, :half_ff]
@@ -569,43 +603,47 @@
     gate_up = mlp_block[:2]
     down = mlp_block[2]
     x0, y1, near = swap(half0, "fsdp", 1), swap(half1, "sub", 2), swap(gate_up, "fsdp", 2)
+    cot = jnp.concatenate([cot, cot_y])
+    cot_c = swap(cot, "sub", 1)
     tables = (owner, inner[None, :])
     angles = (cosine, sine, seg)
-    half0, half1, gate_up, down, x0, y1, near, rows32, grad_outb, spots, tables, angles = meet(
-        half0, half1, gate_up, down, x0, y1, near, rows32, grad_outb, spots, tables, angles
+    half0, half1, gate_up, down, x0, y1, near, rows32, cot, cot_c, tables, angles = meet(
+        half0, half1, gate_up, down, x0, y1, near, rows32, cot, cot_c, tables, angles
     )
 
     half0 = jnp.stack([half0, x0])
     half1 = put2(half1, y1, my_y, 1)
     y0, x1, third = swap(half0, "sub", 2), swap(half1, "fsdp", 1), swap(gate_up, "fsdp", 4)
     down_x = swap(down, "fsdp", 1)
-    half0, half1, gate_up, down, down_x, near, y0, x1, third, grad_outb = meet(
-        half0, half1, gate_up, down, down_x, near, y0, x1, third, grad_outb
-    )
+    cot_all = mm(jnp.concatenate([cot, cot_c]), spread_mat).astype(BF)
+    half0, half1, gate_up, down, down_x, near, y0, x1, third, cot_all, rows = meet(
+        half0, half1, gate_up, down, down_x, near, y0, x1, third, cot_all, rows
+    )
+    grad_outb = cot_all[:count]
 
     half0 = put2(half0, y0, my_y, 2).reshape(wide // 2, half_ff)
     half1 = jnp.stack([half1, x1]).reshape(wide // 2, half_ff)
     c0, c1, last = swap(half0, "sub", 1), swap(half1, "sub", 1), swap(third, "fsdp", 2)
-    cot_y = swap(grad_outb, "sub", 2)
     down = jnp.stack([down, down_x])
-    half0, half1, c0, c1, gate_up, near, third, last, down, cot_y = meet(
-        half0, half1, c0, c1, gate_up, near, third, last, down, cot_y
-    )
+    rows_y = swap(rows, "sub", 2)
+    half0, half1, c0, c1, gate_up, near, third, last, down, rows_y = meet(
+        half0, half1, c0, c1, gate_up, near, third, last, down, rows_y
+    )
+    rows_all = jnp.concatenate([rows, rows_y])
 
     gate_up = jnp.stack([gate_up, near, third, last])
     gate_up_x = swap(gate_up, "fsdp", 1)
     down_near, down_third = swap(down, "fsdp", 2), swap(down, "fsdp", 4)
     by_fsdp = [(f % 2) * n_far * n_sub + (f // 2) * n_sub for f in range(n_fsdp)]
-    my_place = jnp.stack([my_fsdp, my_c])
+    my_place = jnp.stack([my_fsdp, my_c, my_sub])
     tall = (count, wide)
     forward = run_kernel(
         make_forward(n_fsdp, own, padded, share, by_fsdp),
         [
-            (tall, BF),
+            ((count, half_ff - 256), BF),
             ((count, half_ff), BF),
             ((count, 384), BF),
             ((count, KV * GROUP), F32),
-            ((count, half_ff), BF),
             (tall, F32),
             (tall, BF),
             ((2, wide), F32),
@@ -615,17 +653,18 @@
         (my_place, rows32, *tables, *angles, half0, c0, half1, c1),
         name="attn_forward",
     )
-    input1, qk, values, logsum, attended, hidden1, input2, gains_p, attn_q, attn_o = forward
+    att, qk, values, logsum, hidden1, input2, gains_p, attn_q, attn_o = forward
 
     in2_y = swap(input2, "sub", 2)
-    input2, in2_y, cot_y, down_near, down_third = meet(input2, in2_y, cot_y, down_near, down_third)
+    input2, in2_y, down_near, down_third = meet(input2, in2_y, down_near, down_third)
     down_last = swap(down_third, "fsdp", 2)
     in2_all = jnp.stack([input2, in2_y])
-    cot_all = jnp.stack([grad_outb, cot_y])
-    in2_c, cot_c = swap(in2_all, "sub", 1), swap(cot_all, "sub", 1)
-    in2_c, cot_c, gate_up_x, down_last = meet(in2_c, cot_c, gate_up_x, down_last)
+    in2_c = swap(in2_all, "sub", 1)
+    rows_c = swap(rows_all, "sub", 1)
+    in2_c, gate_up_x, rows_c = meet(in2_c, gate_up_x, rows_c)
+    rows_all = jnp.concatenate([rows_all, rows_c])
+    att_y = swap(att, "sub", 2)
     in2_all = jnp.stack([in2_all, in2_c]).reshape(4 * count, wide)
-    cot_all = jnp.stack([cot_all, cot_c]).reshape(4 * count, wide)
     gate_w = jnp.stack([gate_up[:, 0], gate_up_x[:, 0]]).reshape(wide, quarter)
     up_w = jnp.stack([gate_up[:, 1], gate_up_x[:, 1]]).reshape(wide, quarter)
     gate = mm(in2_all, gate_w)
@@ -633,109 +672,117 @@
     sigma = jax.nn.sigmoid(gate)
     active = gate * sigma
     hidden = (active * up).astype(BF)
+    hidden, att_y, down_last = meet(hidden, att_y, down_last)
     down_term = term(cot_all, hidden).reshape(2, n_far, n_sub * padded, quarter)
     down_w = jnp.stack([down, down_near, down_third, down_last])
     down_w = down_w.transpose(1, 0, 2, 3).reshape(wide, quarter)
     down_near_came = swap(far_pair(down_term, 1, 1), "fsdp", 2)
-    grad_hidden = mm(cot_all, down_w)
+    grad_hidden = mm(after(cot_all, down_term), down_w)
     grad_gate = (grad_hidden * up * sigma * (1.0 + gate * (1.0 - sigma))).astype(BF)
     grad_up = (grad_hidden * active).astype(BF)
     grad_in2 = (mm_t(grad_gate, gate_w) + mm_t(grad_up, up_w)).astype(BF).reshape(2, 2 * count, wide)
-    gate_up_term = jnp.stack([term(in2_all, grad_gate), term(in2_all, grad_up)])
-    gate_up_term = gate_up_term.reshape(2, 2, n_far, n_sub * padded, quarter)
+    gate_up_term = [
+        term(in2_all, grad).reshape(2, n_far, n_sub * padded, quarter) for grad in (grad_gate, grad_up)
+    ]
+    gate_up_x_came = [swap(part[1], "fsdp", 1) for part in gate_up_term]
     result = mm_t(hidden, down_w).astype(BF).reshape(2, 2 * count, wide)
 
     came = swap(grad_in2[1], "sub", 1)
+    atts = [att, att_y, swap(att, "sub", 1), swap(att_y, "sub", 1)]
+    came, atts = meet(came, atts)
     grad_in2 = add2(grad_in2[0], came).reshape(2, count, wide)
     grad_in2_y = swap(grad_in2[1], "sub", 2)
-    gate_up_x_came = swap(gate_up_term[:, 1], "fsdp", 1)
-    grad_in2, grad_in2_y, down_near_came = meet(grad_in2, grad_in2_y, down_near_came)
+    grad_h1, grad_h1b, gain2_term = run_kernel(
+        norm_kernel,
+        [(tall, F32), (tall, BF), ((1, wide), F32)],
+        (my_place, grad_in2[0], grad_in2_y, grad_outb, hidden1, gains_p),
+        name="norm_backward",
+    )
+    grad_h1_y = swap(grad_h1b, "sub", 2)
+    grad_h1, down_near_came = meet(grad_h1, down_near_came)
     down_held = add2(far_pair(down_term, 1, 0), down_near_came)
     down_far_came = swap(down_held[:, 1], "fsdp", 4)
-    q_keep, q_send, o_keep, o_send, input_grad = run_kernel(
-        make_backward(n_fsdp, own, padded, share),
-        [((wide // 2, half_ff), BF)] * 4 + [(tall, F32)],
+    grads, input_grad = run_kernel(
+        make_backward(n_fsdp, own),
+        [((count + 16, half_ff + 384), BF), (tall, F32)],
         (
-            my_place, grad_in2[0], grad_in2_y, grad_outb, hidden1, rows32, gains_p, *tables, spots, *angles,
-            input1, qk, values, logsum, attended, attn_q, attn_o,
+            my_place, grad_h1, grad_h1b, gain2_term, rows32, gains_p, *tables, *angles,
+            qk, values, logsum, attn_q, attn_o,
         ),
-        scratch=[
-            pltpu.VMEM((2 * count, wide), BF),
-            pltpu.VMEM((2 * count, half_ff), BF),
-            pltpu.VMEM((count, half_ff), F32),
-        ],
+        scratch=[pltpu.VMEM((count, half_ff), F32)],
         name="attn_backward",
     )
 
-    q_keep, q_send, o_keep, o_send, down_far_came, gate_up_x_came = meet(
-        q_keep, q_send, o_keep, o_send, down_far_came, gate_up_x_came
-    )
-
-    q_c, o_c = swap(q_send, "sub", 1), swap(o_send, "sub", 1)
-    gate_up_held = add2(gate_up_term[:, 0], gate_up_x_came)
+    grads_y = swap(grads, "sub", 2)
+    grads_c = swap(grads, "sub", 1)
+    grads, grad_h1_y, gate_up_x_came, down_far_came = meet(
+        grads, grad_h1_y, gate_up_x_came, down_far_came
+    )
+    grad_h1_c, grad_h1_yc = swap(grad_h1b, "sub", 1), swap(grad_h1_y, "sub", 1)
+    gate_up_held = jnp.stack([add2(part[0], came) for part, came in zip(gate_up_term, gate_up_x_came)])
     gate_up_near = swap(far_pair(gate_up_held, 1, 1), "fsdp", 2)
     down_held = add2(down_held[:, 0], down_far_came)
     down_x_came = swap(down_held[1], "fsdp", 1)
-    q_c, o_c, gate_up_near, down_x_came = meet(q_c, o_c, gate_up_near, down_x_came)
-
-    full = (2, n_far, 2, padded, half_ff)
-    q_held = add2(q_keep, q_c).reshape(full)
-    o_held = add2(o_keep, o_c).reshape(full)
-    q_y = swap(pick(q_held, 1 - my_y, 2), "sub", 2)
-    o_x = swap(o_held[1], "fsdp", 1)
-    gate_up_held = add2(far_pair(gate_up_held, 1, 0), gate_up_near)
+    grads_y, grads_c, grad_h1_c, grad_h1_yc, down_x_came = meet(
+        grads_y, grads_c, grad_h1_c, grad_h1_yc, down_x_came
+    )
+
+    grads_yc = swap(grads_y, "sub", 1)
+    res_c = swap(after(result[1], grads_y), "sub", 1)
+    attn_keep, attn_send = run_kernel(
+        make_terms(n_far, n_sub, own, padded, count),
+        [((n_far * padded, FF), BF)] * 2,
+        (
+            my_place, rows_all, gains_p, *atts, grad_h1b, grad_h1_y, grad_h1_c, grad_h1_yc, grads, grads_y, grads_c, grads_yc,
+        ),
+        name="attn_terms",
+    )
+
+    attn_x = swap(attn_send, "fsdp", 1)
+    gate_up_held = add2(far_pair(gate_up_held, 1, 0), after(gate_up_near, attn_send))
     gate_up_far = swap(gate_up_held[:, 1], "fsdp", 4)
-    input_grad = after(input_grad, q_c)
+    result = add2(result[0], res_c).reshape(2, count, wide)
+    res_y = swap(result[1], "sub", 2)
+    input_grad = after(input_grad, attn_send)
     input_grad = lax.dot_general(
         input_grad,
         spread_mat.astype(F32),
         (((1,), (1,)), ((), ())),
         precision=lax.Precision.HIGHEST,
     )
-    res_c = swap(after(result[1], q_c), "sub", 1)
-    q_y, o_x, gate_up_far, input_grad, res_c = meet(q_y, o_x, gate_up_far, input_grad, res_c)
-
-    q_held = add2(pick(q_held, my_y, 2), q_y)
-    o_held = add2(o_held[0], o_x)
-    q_x = swap(q_held[1], "fsdp", 1)
-    o_y = swap(pick(o_held, 1 - my_y, 1), "sub", 2)
+    attn_x, gate_up_far, input_grad, res_y = meet(attn_x, gate_up_far, input_grad, res_y)
+
+    def side_by_side(mine, came, bit):
+        first = bit == 0
+        return jnp.concatenate([jnp.where(first, mine, came), jnp.where(first, came, mine)], axis=-1)
+
+    attn_held = add2(attn_keep, attn_x).reshape(n_far, padded, FF)
+    attn_near = swap(far_pair(attn_held, 0, 1), "fsdp", 2)
     down_own = add2(down_held[0], down_x_came)[None]
     mlp_own = jnp.concatenate([add2(gate_up_held[:, 0], gate_up_far), down_own])
     mlp_own = mlp_own.reshape(3, 2, 2, padded, quarter)
     mlp_c = swap(pick(mlp_own, 1 - my_c, 2), "sub", 1)
-    q_x, o_y, mlp_c = meet(q_x, o_y, mlp_c)
-
-    def side_by_side(mine, came, bit):
-        first = bit == 0
-        return jnp.concatenate([jnp.where(first, mine, came), jnp.where(first, came, mine)], axis=-1)
-
-    q_held = add2(q_held[0], q_x)
-    o_held = add2(pick(o_held, my_y, 1), o_y)
-    attn_held = jnp.concatenate([q_held, o_held], axis=-1)
-    attn_near = swap(far_pair(attn_held, 0, 1), "fsdp", 2)
-    result = add2(result[0], res_c).reshape(2, count, wide)
-    res_y = swap(result[1], "sub", 2)
+    attn_near, mlp_c = meet(attn_near, mlp_c)
     mlp_own = side_by_side(pick(mlp_own, my_c, 2), mlp_c, my_c)
     mlp_y = swap(pick(mlp_own, 1 - my_y, 1), "sub", 2)
-    attn_near, res_y, mlp_y = meet(attn_near, res_y, mlp_y)
     attn_held = add2(far_pair(attn_held, 0, 0), attn_near)
     attn_far = swap(attn_held[1], "fsdp", 4)
     result = hidden1 + result[0].astype(F32) + res_y.astype(F32)
     output = mm_t((live * result).astype(BF), spread_mat).astype(BF)
     mlp_own = side_by_side(pick(mlp_own, my_y, 1), mlp_y, my_y)
+
+    def flat(part):
+        return part[:own].astype(F32).reshape(-1)
+
+    mlp_flat = [flat(mlp_own[i]) for i in range(3)]
+    attn_far, mlp_flat, output = meet(attn_far, mlp_flat, output)
     attn_own = add2(attn_held[0], attn_far)
     gain_grad = attn_own[own, :share].astype(F32)
-
-    def flat(mine):
-        return mine[:own].astype(F32).reshape(-1)
-
     return (
         output,
         input_grad,
         flat(attn_own),
-        flat(mlp_own[0]),
-        flat(mlp_own[1]),
-        flat(mlp_own[2]),
+        *mlp_flat,
         gain_grad,
     )
 

time: 220 us -> 213 us (0.968)
  waiting for transfers between devices: 105 us -> 85.6 us
  other arithmetic: 15.9 us -> 19.3 us
  Pallas kernels: 24.9 us -> 27.1 us
    ppermute x43 -> x50, waiting for transfers between devices: 105 us -> 85.6 us  [swap(): lax.ppermute(value, axis, [(i, i ^ bit) for i in range(lax.axis_size(axis...]
    pallas_call x2 -> x4, Pallas kernels: 24.9 us -> 27.1 us  [run_kernel(): pl.pallas_call(kernel, out_shape=[jax.ShapeDtypeStruct(shape, kind) for s...]
    ppermute x43 -> x50, starting transfers between devices: 39.9 us -> 41.8 us  [swap(): lax.ppermute(value, axis, [(i, i ^ bit) for i in range(lax.axis_size(axis...]
    convert_element_type x16 -> x12, other arithmetic: 4.89 us -> 5.84 us  [add2(): return (kept.astype(F32) + came.astype(F32)).astype(BF)]
    unnamed x52 -> x57, local copies, waits for them, and re-layouts: 3.81 us -> 4.57 us
  transfers between devices with their start and end apart: 43 -> 50, of which waited for: 18 -> 23; matrix products, arithmetic and copies ran while one was open for 13% -> 21% of each run, Pallas kernels for 11% -> 13%
where the time goes in v4:
time: 213 us; the launch traced here: 212 us
  waiting for transfers between devices  85.6 us (40%)
  starting transfers between devices  41.8 us (20%)
  Pallas kernels  27.1 us (13%)
  other arithmetic  19.3 us (9%)
  matrix products  18.8 us (9%)
  local copies, waits for them, and re-layouts  16.4 us (8%)
  between operations  2.88 us (1%)
    ppermute x50, waiting for transfers between devices, swap(): lax.ppermute(value, axis, [(i, i ^ bit) for i in range(lax.axis_size(axis...  85.6 us
    ppermute x50, starting transfers between devices, swap(): lax.ppermute(value, axis, [(i, i ^ bit) for i in range(lax.axis_size(axis...  41.8 us
    pallas_call x4, Pallas kernels, run_kernel(): pl.pallas_call(kernel, out_shape=[jax.ShapeDtypeStruct(shape, kind) for s...  27.1 us
    dot_general x5, matrix products, mm(): return jnp.dot(a, b, preferred_element_type=F32)  7.37 us
    convert_element_type x12, other arithmetic, add2(): return (kept.astype(F32) + came.astype(F32)).astype(BF)  5.84 us
    dot_general x4, matrix products, mm_t(): lax.dot_general(a, b, (((1,), (1,)), ((), ())), preferred_element_type=F32)  5.68 us
    unnamed x57, local copies, waits for them, and re-layouts  4.57 us
  transfers between devices with their start and end apart: 50, of which 23 were waited for; matrix products, arithmetic and copies ran while one was open for 21% of the time, Pallas kernels for 13%

profile of v4, /device:TPU:0, one launch (start us, length us, event | category | flops | bytes accessed | tf_op | source)
XLA Modules:
  0.0 211.9 jit_solution(7184066853722150297)
XLA Ops:
  2.7 3.1 %collective-permute-start = (bf16[32,2560]{1,0:T(8,128)(2,1)S(1)}, bf16[32,2560]{1,0:T(8,128)(2,1)S(1)}, u32[]{:S(2)}, u32[]{:S(2)}) collective-permute-start(bf16[32,2560]{1,0:T(8,128)(2,1)S(1)} %scatter.4), channel_id=1, source_target_pairs={{0,8},{4,12},{8,0},{12,4},{16,24},{20,28},{24,16},{28,20},{1,9},{5... | collective-permute-start | bytes 491528 | tf_op jit(solution)/shard_map/ppermute | solution.py:260
  5.8 2.6 %collective-permute-start.1 = (bf16[32,2560]{1,0:T(8,128)(2,1)S(1)}, bf16[32,2560]{1,0:T(8,128)(2,1)S(1)}, u32[]{:S(2)}, u32[]{:S(2)}) collective-permute-start(bf16[32,2560]{1,0:T(8,128)(2,1)S(1)} %scatter.4), channel_id=1, source_target_pairs={{0,16},{4,20},{8,24},{12,28},{16,0},{20,4},{24,8},{28,12},{1,17},{... | collective-permute-start | bytes 491528 | tf_op jit(solution)/shard_map/ppermute | solution.py:260
  11.0 1.8 collective-permute-start.3
  19.1 1.6 fusion.14.rows_ref
  21.0 2.5 %collective-permute-done.5 = bf16[128,960]{0,1:T(8,128)(2,1)S(1)} collective-permute-done((bf16[128,960]{0,1:T(8,128)(2,1)S(1)}, bf16[128,960]{0,1:T(8,128)(2,1)S(1)}, u32[]{:S(2)}, u32[]{:S(2)}) %collective-permute-start.5) | collective-permute-done | bytes 245792 | tf_op jit(solution)/shard_map/ppermute | solution.py:260
  23.9 1.6 collective-permute-start.6
  25.4 1.5 collective-permute-start.7
  28.2 5.8 %collective-permute-done.6 = bf16[4,32,1280]{2,1,0:T(8,128)(2,1)S(1)} collective-permute-done((bf16[4,32,1280]{2,1,0:T(8,128)(2,1)S(1)}, bf16[4,32,1280]{2,1,0:T(8,128)(2,1)S(1)}, u32[]{:S(2)}, u32[]{:S(2)}) %collective-permute-start.6) | collective-permute-done | bytes 327712 | tf_op jit(solution)/shard_map/ppermute | solution.py:260
  37.9 2.4 %collective-permute-start.13 = (bf16[2,128,640]{2,1,0:T(8,128)(2,1)S(1)}, bf16[2,128,640]{2,1,0:T(8,128)(2,1)}, u32[]{:S(2)}, u32[]{:S(2)}) collective-permute-start(bf16[2,128,640]{2,1,0:T(8,128)(2,1)S(1)} %slice.170), channel_id=1, source_target_pairs={{0,16},{4,20},{8,24},{12,28},{16,0},{20,4},{24,8},{28,12},{1,17},{... | collective-permute-start | bytes 983048 | tf_op jit(solution)/shard_map/ppermute | solution.py:260
  41.7 2.3 %fusion.8 = bf16[512,1024]{1,0:T(8,128)(2,1)} fusion(s32[1024]{0:T(1024)S(1)} %fusion.59, bf16[256,960]{0,1:T(8,128)(2,1)S(1)} %collective-permute-done.9, bf16[256,960]{0,1:T(8,128)(2,1)S(1)} %constant_dynamic-update-slice_fusion), kind=kOutput, calls=%fused_computation.13 | convolution fusion | flops 1010106368 | bytes 2035712 | tf_op jit(solution)/shard_map/dot_general | solution.py:291
  44.1 12.3 %collective-permute-done.10 = bf16[128,640]{1,0:T(8,128)(2,1)S(1)} collective-permute-done((bf16[128,640]{1,0:T(8,128)(2,1)S(1)}, bf16[128,640]{1,0:T(8,128)(2,1)S(1)}, u32[]{:S(2)}, u32[]{:S(2)}) %collective-permute-start.10) | collective-permute-done | bytes 163872 | tf_op jit(solution)/shard_map/ppermute | solution.py:260
  62.3 6.0 %collective-permute-done.17 = bf16[128,960]{1,0:T(8,128)(2,1)S(1)} collective-permute-done((bf16[128,960]{1,0:T(8,128)(2,1)S(1)}, bf16[128,960]{1,0:T(8,128)(2,1)S(1)}, u32[]{:S(2)}, u32[]{:S(2)}) %collective-permute-start.17) | collective-permute-done | bytes 245792 | tf_op jit(solution)/shard_map/ppermute | solution.py:260
  71.9 2.8 %collective-permute-start.20 = (bf16[2,128,640]{2,1,0:T(8,128)(2,1)S(1)}, bf16[2,128,640]{2,1,0:T(8,128)(2,1)S(1)}, u32[]{:S(2)}, u32[]{:S(2)}) collective-permute-start(bf16[2,128,640]{2,1,0:T(8,128)(2,1)S(1)} %pad_maximum_fusion.15), channel_id=1, source_target_pairs={{0,16},{4,20},{8,24},{12,28},{16,0},{20,4},{24,8},{28,12},{1,17},{... | collective-permute-start | bytes 983048 | tf_op jit(solution)/shard_map/ppermute | solution.py:260
  75.4 10.3 %attn_forward.1 = (bf16[128,1024]{1,0:T(8,128)(2,1)}, bf16[128,1280]{1,0:T(8,128)(2,1)}, bf16[128,384]{1,0:T(8,128)(2,1)}, f32[128,15]{1,0:T(8,128)}, f32[128,10...) custom-call(s32[3]{0:T(128)} %pad_add_fusion.place_ref, ...), custom_call_target="tpu_custom_call" | custom-call | flops 1000 | bytes 1000 | tf_op jit(solution)/shard_map/attn_forward/pallas_call | solution.py:534
  87.1 6.0 %collective-permute-done.18 = bf16[128,1024]{1,0:T(8,128)(2,1)S(1)} collective-permute-done((bf16[128,1024]{1,0:T(8,128)(2,1)}, bf16[128,1024]{1,0:T(8,128)(2,1)S(1)}, u32[]{:S(2)}, u32[]{:S(2)}) %collective-permute-start.18) | collective-permute-done | bytes 262176 | tf_op jit(solution)/shard_map/ppermute | solution.py:260
  103.9 4.4 %collective-permute-done.25 = bf16[2,128,640]{2,1,0:T(8,128)(2,1)S(1)} collective-permute-done((bf16[2,128,640]{2,1,0:T(8,128)(2,1)S(1)}, bf16[2,128,640]{2,1,0:T(8,128)(2,1)S(1)}, u32[]{:S(2)}, u32[]{:S(2)}) %collective-permute-start.25) | collective-permute-done | bytes 327712 | tf_op jit(solution)/shard_map/ppermute | solution.py:260
  116.0 1.6 collective-permute-start.32
  120.9 6.5 %collective-permute-done.29.grad_b_ref = bf16[128,1024]{1,0:T(8,128)(2,1)S(1)} collective-permute-done((bf16[128,1024]{1,0:T(8,128)(2,1)S(1)}, bf16[128,1024]{1,0:T(8,128)(2,1)S(1)}, u32[]{:S(2)}, u32[]{:S(2)}) %collective-permute-start.29) | collective-permute-done | bytes 262176 | tf_op jit(solution)/shard_map/ppermute | solution.py:260
  128.0 2.5 %norm_backward.1 = (f32[128,1024]{1,0:T(8,128)}, bf16[128,1024]{1,0:T(8,128)(2,1)}, f32[1,1024]{1,0:T(1,128)}) custom-call(s32[3]{0:T(128)} %pad_add_fusion.place_ref, bf16[128,1024]{1,0:T(8,128)(2,1)} %get-tuple-element.242.grad_a_ref, bf16[128,1024]{1,0:T(8,128)(2,1)} %copy-done.10, bf16[128,1024]{1,0:T(8,128)(2,1)} %slice.180.grad_out_ref, ...), custom_call_target="tpu_custom_call" | custom-call | flops 1000 | bytes 1000 | tf_op jit(solution)/shard_map/norm_backward/pallas_call | solution.py:534
  133.9 9.1 %attn_backward.1 = (bf16[144,1664]{1,0:T(8,128)(2,1)}, f32[128,1024]{1,0:T(8,128)}) custom-call(s32[3]{0:T(128)} %pad_add_fusion.place_ref, f32[128,1024]{1,0:T(8,128)} %get-tuple-element.181.grad_h1_ref, bf16[128,1024]{1,0:T(8,128)(2,1)} %get-tuple-element.178.grad_h1b_ref.refs_4_, f32[1,1024]{1,0:T(1,128)} %get-tuple-element.182.gain2_ref, ...), custom_call_target="tpu_custom_call" | custom-call | flops 1000 | bytes 1000 | tf_op jit(solution)/shard_map/attn_backward/pallas_call | solution.py:534
  144.4 2.2 %collective-permute-done.33 = bf16[4,128,640]{2,1,0:T(8,128)(2,1)} collective-permute-done((bf16[4,128,640]{2,1,0:T(8,128)(2,1)S(1)}, bf16[4,128,640]{2,1,0:T(8,128)(2,1)}, u32[]{:S(2)}, u32[]{:S(2)}) %collective-permute-start.33) | collective-permute-done | bytes 655392 | tf_op jit(solution)/shard_map/ppermute | solution.py:260
  146.7 3.1 %collective-permute-done.34 = bf16[2,128,640]{2,1,0:T(8,128)(2,1)S(1)} collective-permute-done((bf16[2,128,640]{2,1,0:T(8,128)(2,1)S(1)}, bf16[2,128,640]{2,1,0:T(8,128)(2,1)S(1)}, u32[]{:S(2)}, u32[]{:S(2)}) %collective-permute-start.34) | collective-permute-done | bytes 327712 | tf_op jit(solution)/shard_map/ppermute | solution.py:260
  153.3 1.6 collective-permute-start.39
  155.0 5.0 %collective-permute-done.39 = bf16[128,640]{1,0:T(8,128)(2,1)S(1)} collective-permute-done((bf16[128,640]{1,0:T(8,128)(2,1)S(1)}, bf16[128,640]{1,0:T(8,128)(2,1)S(1)}, u32[]{:S(2)}, u32[]{:S(2)}) %collective-permute-start.39) | collective-permute-done | bytes 163872 | tf_op jit(solution)/shard_map/ppermute | solution.py:260
  161.4 2.1 %convolution_convert_fusion.3 = bf16[512,1024]{1,0:T(8,128)(2,1)S(1)} fusion(bf16[512,640]{1,0:T(8,128)(2,1)} %copy-done.27, bf16[1024,640]{1,0:T(8,128)(2,1)S(1)} %bitcast.213), kind=kOutput, calls=%fused_computation.14 | convolution fusion | flops 671612928 | bytes 3014656 | tf_op jit(solution)/shard_map/dot_general | solution.py:295
  165.7 5.2 %attn_terms.1 = (bf16[128,2560]{1,0:T(8,128)(2,1)}, bf16[128,2560]{1,0:T(8,128)(2,1)}) custom-call(s32[3]{0:T(128)} %pad_add_fusion.place_ref, bf16[512,960]{1,0:T(8,128)(2,1)} %pad_maximum_fusion.5.rows_ref, f32[2,1024]{1,0:T(2,128)} %get-tuple-element.163.gains_ref, bf16[128,1024]{1,0:T(8,128)(2,1)} %get-tuple-element.172.refs_0_, ...), custom_call_target="tpu_custom_call" | custom-call | flops 1000 | bytes 1000 | tf_op jit(solution)/shard_map/attn_terms/pallas_call | solution.py:534
  175.7 2.7 %fusion.1 = f32[128,960]{0,1:T(8,128)} fusion(f32[128,1024]{1,0:T(8,128)S(1)} %copy-done.26, s32[1024]{0:T(1024)S(1)} %fusion.59), kind=kOutput, calls=%fused_computation.2 | convolution fusion | flops 1510932480 | bytes 1019904 | tf_op jit(solution)/shard_map/dot_general | solution.py:747
  178.4 4.9 %collective-permute-done.45 = bf16[128,1024]{1,0:T(8,128)(2,1)S(1)} collective-permute-done((bf16[128,1024]{1,0:T(8,128)(2,1)S(1)}, bf16[128,1024]{1,0:T(8,128)(2,1)S(1)}, u32[]{:S(2)}, u32[]{:S(2)}) %collective-permute-start.45) | collective-permute-done | bytes 262176 | tf_op jit(solution)/shard_map/ppermute | solution.py:260
  183.3 8.2 %collective-permute-done.43 = bf16[2,128,640]{2,1,0:T(8,128)(2,1)S(1)} collective-permute-done((bf16[2,128,640]{2,1,0:T(8,128)(2,1)S(1)}, bf16[2,128,640]{2,1,0:T(8,128)(2,1)S(1)}, u32[]{:S(2)}, u32[]{:S(2)}) %collective-permute-start.43) | collective-permute-done | bytes 327712 | tf_op jit(solution)/shard_map/ppermute | solution.py:260
  192.7 1.5 fusion.15
  194.2 6.6 %collective-permute-done.46 = bf16[2,32,2560]{2,1,0:T(8,128)(2,1)S(1)} collective-permute-done((bf16[2,32,2560]{2,1,0:T(8,128)(2,1)S(1)}, bf16[2,32,2560]{2,1,0:T(8,128)(2,1)S(1)}, u32[]{:S(2)}, u32[]{:S(2)}) %collective-permute-start.46) | collective-permute-done | bytes 327712 | tf_op jit(solution)/shard_map/ppermute | solution.py:260
  202.4 5.0 %collective-permute-done.49 = bf16[3,32,1280]{2,1,0:T(8,128)(2,1)S(1)} collective-permute-done((bf16[3,32,1280]{2,1,0:T(8,128)(2,1)S(1)}, bf16[3,32,1280]{2,1,0:T(8,128)(2,1)S(1)}, u32[]{:S(2)}, u32[]{:S(2)}) %collective-permute-start.49) | collective-permute-done | bytes 245792 | tf_op jit(solution)/shard_map/ppermute | solution.py:260
  (232 shorter events, 74.1 us)
Async XLA Ops:
  2.7 18.2 %collective-permute-start = (bf16[32,2560]{1,0:T(8,128)(2,1)S(1)}, bf16[32,2560]{1,0:T(8,128)(2,1)S(1)}, u32[]{:S(2)}, u32[]{:S(2)}) collective-permute-start(bf16[32,2560]{1,0:T(8,128)(2,1)S(1)} %scatter.4), channel_id=1, source_target_pairs={{0,8},{4,12},{8,0},{12,4},{16,24},{20,28},{24,16},{28,20},{1,9},{5... | collective-permute-start | bytes 491528 | tf_op jit(solution)/shard_map/ppermute | solution.py:260
  5.8 15.1 %collective-permute-start.1 = (bf16[32,2560]{1,0:T(8,128)(2,1)S(1)}, bf16[32,2560]{1,0:T(8,128)(2,1)S(1)}, u32[]{:S(2)}, u32[]{:S(2)}) collective-permute-start(bf16[32,2560]{1,0:T(8,128)(2,1)S(1)} %scatter.4), channel_id=1, source_target_pairs={{0,16},{4,20},{8,24},{12,28},{16,0},{20,4},{24,8},{28,12},{1,17},{... | collective-permute-start | bytes 491528 | tf_op jit(solution)/shard_map/ppermute | solution.py:260
  8.4 12.6 %collective-permute-start.2 = (bf16[32,2560]{1,0:T(8,128)(2,1)S(1)}, bf16[32,2560]{1,0:T(8,128)(2,1)S(1)}, u32[]{:S(2)}, u32[]{:S(2)}) collective-permute-start(bf16[32,2560]{1,0:T(8,128)(2,1)S(1)} %scatter.4), channel_id=1, source_target_pairs={{0,24},{4,28},{8,16},{12,20},{16,8},{20,12},{24,0},{28,4},{1,25},{... | collective-permute-start | bytes 491528 | tf_op jit(solution)/shard_map/ppermute | solution.py:260
  23.6 12.9 %collective-permute-start.9 = (bf16[256,960]{0,1:T(8,128)(2,1)S(1)}, bf16[256,960]{0,1:T(8,128)(2,1)S(1)}, u32[]{:S(2)}, u32[]{:S(2)}) collective-permute-start(bf16[256,960]{0,1:T(8,128)(2,1)S(1)} %constant_dynamic-update-slice_fusion), channel_id=1, source_target_pairs={{0,1},{1,0},{2,3},{3,2},{4,5},{5,4},{6,7},{7,6},{8,9},{9,8},{10,11... | collective-permute-start | bytes 1474568 | tf_op jit(solution)/shard_map/ppermute | solution.py:260
  23.9 10.2 %collective-permute-start.6 = (bf16[4,32,1280]{2,1,0:T(8,128)(2,1)S(1)}, bf16[4,32,1280]{2,1,0:T(8,128)(2,1)S(1)}, u32[]{:S(2)}, u32[]{:S(2)}) collective-permute-start(bf16[4,32,1280]{2,1,0:T(8,128)(2,1)S(1)} %get-tuple-element.124), channel_id=1, source_target_pairs={{0,4},{4,0},{8,12},{12,8},{16,20},{20,16},{24,28},{28,24},{1,5},{5... | collective-permute-start | bytes 983048 | tf_op jit(solution)/shard_map/ppermute | solution.py:260
  25.4 9.8 %collective-permute-start.7 = (bf16[4,32,1280]{2,1,0:T(8,128)(2,1)S(1)}, bf16[4,32,1280]{2,1,0:T(8,128)(2,1)S(1)}, u32[]{:S(2)}, u32[]{:S(2)}) collective-permute-start(bf16[4,32,1280]{2,1,0:T(8,128)(2,1)S(1)} %get-tuple-element.126), channel_id=1, source_target_pairs={{0,2},{1,3},{2,0},{3,1},{4,6},{5,7},{6,4},{7,5},{8,10},{9,11},{10,... | collective-permute-start | bytes 983048 | tf_op jit(solution)/shard_map/ppermute | solution.py:260
  27.0 9.5 %collective-permute-start.8 = (bf16[2,128,640]{2,1,0:T(8,128)(2,1)S(1)}, bf16[2,128,640]{2,1,0:T(8,128)(2,1)S(1)}, u32[]{:S(2)}, u32[]{:S(2)}) collective-permute-start(bf16[2,128,640]{2,1,0:T(8,128)(2,1)S(1)} %slice.170), channel_id=1, source_target_pairs={{0,8},{4,12},{8,0},{12,4},{16,24},{20,28},{24,16},{28,20},{1,9},{5... | collective-permute-start | bytes 983048 | tf_op jit(solution)/shard_map/ppermute | solution.py:260
  36.6 19.8 %collective-permute-start.11 = (bf16[2,4,32,1280]{3,2,1,0:T(8,128)(2,1)S(1)}, bf16[2,4,32,1280]{3,2,1,0:T(8,128)(2,1)S(1)}, u32[]{:S(2)}, u32[]{:S(2)}) collective-permute-start(bf16[2,4,32,1280]{3,2,1,0:T(8,128)(2,1)S(1)} %pad_maximum_fusion.9), channel_id=1, source_target_pairs={{0,2},{1,3},{2,0},{3,1},{4,6},{5,7},{6,4},{7,5},{8,10},{9,11},{10,... | collective-permute-start | bytes 1966088 | tf_op jit(solution)/shard_map/ppermute | solution.py:260
  37.3 19.1 %collective-permute-start.12 = (bf16[4,2,32,1280]{3,2,1,0:T(8,128)(2,1)S(1)}, bf16[4,2,32,1280]{3,2,1,0:T(8,128)(2,1)S(1)}, u32[]{:S(2)}, u32[]{:S(2)}) collective-permute-start(bf16[4,2,32,1280]{3,2,1,0:T(8,128)(2,1)S(1)} %pad_maximum_fusion.10), channel_id=1, source_target_pairs={{0,4},{4,0},{8,12},{12,8},{16,20},{20,16},{24,28},{28,24},{1,5},{5... | collective-permute-start | bytes 1966088 | tf_op jit(solution)/shard_map/ppermute | solution.py:260
  37.9 18.5 %collective-permute-start.13 = (bf16[2,128,640]{2,1,0:T(8,128)(2,1)S(1)}, bf16[2,128,640]{2,1,0:T(8,128)(2,1)}, u32[]{:S(2)}, u32[]{:S(2)}) collective-permute-start(bf16[2,128,640]{2,1,0:T(8,128)(2,1)S(1)} %slice.170), channel_id=1, source_target_pairs={{0,16},{4,20},{8,24},{12,28},{16,0},{20,4},{24,8},{28,12},{1,17},{... | collective-permute-start | bytes 983048 | tf_op jit(solution)/shard_map/ppermute | solution.py:260
  40.3 16.1 %collective-permute-start.10 = (bf16[128,640]{1,0:T(8,128)(2,1)S(1)}, bf16[128,640]{1,0:T(8,128)(2,1)S(1)}, u32[]{:S(2)}, u32[]{:S(2)}) collective-permute-start(bf16[128,640]{1,0:T(8,128)(2,1)S(1)} %slice_bitcast_fusion.16), channel_id=1, source_target_pairs={{0,4},{4,0},{8,12},{12,8},{16,20},{20,16},{24,28},{28,24},{1,5},{5... | collective-permute-start | bytes 491528 | tf_op jit(solution)/shard_map/ppermute | solution.py:260
  57.0 11.5 %collective-permute-start.14 = (bf16[512,1280]{1,0:T(8,128)(2,1)S(1)}, bf16[512,1280]{1,0:T(8,128)(2,1)}, u32[]{:S(2)}, u32[]{:S(2)}) collective-permute-start(bf16[512,1280]{1,0:T(8,128)(2,1)S(1)} %bitcast.193), channel_id=1, source_target_pairs={{0,1},{1,0},{2,3},{3,2},{4,5},{5,4},{6,7},{7,6},{8,9},{9,8},{10,11... | collective-permute-start | bytes 3932168 | tf_op jit(solution)/shard_map/ppermute | solution.py:260
  58.1 10.4 %collective-permute-start.15 = (bf16[512,1280]{1,0:T(8,128)(2,1)S(1)}, bf16[512,1280]{1,0:T(8,128)(2,1)}, u32[]{:S(2)}, u32[]{:S(2)}) collective-permute-start(bf16[512,1280]{1,0:T(8,128)(2,1)S(1)} %bitcast.195), channel_id=1, source_target_pairs={{0,1},{1,0},{2,3},{3,2},{4,5},{5,4},{6,7},{7,6},{8,9},{9,8},{10,11... | collective-permute-start | bytes 3932168 | tf_op jit(solution)/shard_map/ppermute | solution.py:260
  58.1 10.4 %collective-permute-start.16 = (bf16[2,128,640]{2,1,0:T(8,128)(2,1)}, bf16[2,128,640]{2,1,0:T(8,128)(2,1)}, u32[]{:S(2)}, u32[]{:S(2)}) collective-permute-start(bf16[2,128,640]{2,1,0:T(8,128)(2,1)} %collective-permute-done.13), channel_id=1, source_target_pairs={{0,8},{4,12},{8,0},{12,4},{16,24},{20,28},{24,16},{28,20},{1,9},{5... | collective-permute-start | bytes 983048 | tf_op jit(solution)/shard_map/ppermute | solution.py:260
  70.0 30.5 %collective-permute-start.22 = (bf16[4,2,128,640]{3,2,0,1:T(8,128)(2,1)S(1)}, bf16[4,2,128,640]{3,2,0,1:T(8,128)(2,1)S(1)}, u32[]{:S(2)}, u32[]{:S(2)}) collective-permute-start(bf16[4,2,128,640]{3,2,0,1:T(8,128)(2,1)S(1)} %copy.66), channel_id=1, source_target_pairs={{0,4},{4,0},{8,12},{12,8},{16,20},{20,16},{24,28},{28,24},{1,5},{5... | collective-permute-start | bytes 3932168 | tf_op jit(solution)/shard_map/ppermute | solution.py:260
  70.6 22.4 %collective-permute-start.19 = (bf16[2,128,640]{2,1,0:T(8,128)(2,1)S(1)}, bf16[2,128,640]{2,1,0:T(8,128)(2,1)S(1)}, u32[]{:S(2)}, u32[]{:S(2)}) collective-permute-start(bf16[2,128,640]{2,1,0:T(8,128)(2,1)S(1)} %pad_maximum_fusion.15), channel_id=1, source_target_pairs={{0,8},{4,12},{8,0},{12,4},{16,24},{20,28},{24,16},{28,20},{1,9},{5... | collective-permute-start | bytes 983048 | tf_op jit(solution)/shard_map/ppermute | solution.py:260
  71.9 21.1 %collective-permute-start.20 = (bf16[2,128,640]{2,1,0:T(8,128)(2,1)S(1)}, bf16[2,128,640]{2,1,0:T(8,128)(2,1)S(1)}, u32[]{:S(2)}, u32[]{:S(2)}) collective-permute-start(bf16[2,128,640]{2,1,0:T(8,128)(2,1)S(1)} %pad_maximum_fusion.15), channel_id=1, source_target_pairs={{0,16},{4,20},{8,24},{12,28},{16,0},{20,4},{24,8},{28,12},{1,17},{... | collective-permute-start | bytes 983048 | tf_op jit(solution)/shard_map/ppermute | solution.py:260
  97.0 21.6 %collective-permute-start.27 = (bf16[128,1024]{1,0:T(8,128)(2,1)S(1)}, bf16[128,1024]{1,0:T(8,128)(2,1)S(1)}, u32[]{:S(2)}, u32[]{:S(2)}) collective-permute-start(bf16[128,1024]{1,0:T(8,128)(2,1)S(1)} %copy-done.11), channel_id=1, source_target_pairs={{0,1},{1,0},{2,3},{3,2},{4,5},{5,4},{6,7},{7,6},{8,9},{9,8},{10,11... | collective-permute-start | bytes 786440 | tf_op jit(solution)/shard_map/ppermute | solution.py:260
  98.1 10.2 %collective-permute-start.25 = (bf16[2,128,640]{2,1,0:T(8,128)(2,1)S(1)}, bf16[2,128,640]{2,1,0:T(8,128)(2,1)S(1)}, u32[]{:S(2)}, u32[]{:S(2)}) collective-permute-start(bf16[2,128,640]{2,1,0:T(8,128)(2,1)S(1)} %collective-permute-done.20), channel_id=1, source_target_pairs={{0,8},{4,12},{8,0},{12,4},{16,24},{20,28},{24,16},{28,20},{1,9},{5... | collective-permute-start | bytes 983048 | tf_op jit(solution)/shard_map/ppermute | solution.py:260
  114.7 16.9 %collective-permute-start.30 = (bf16[2,2,128,640]{3,2,1,0:T(8,128)(2,1)S(1)}, bf16[2,2,128,640]{3,2,1,0:T(8,128)(2,1)}, u32[]{:S(2)}, u32[]{:S(2)}) collective-permute-start(bf16[2,2,128,640]{3,2,1,0:T(8,128)(2,1)S(1)} %slice_bitcast_fusion.1), channel_id=1, source_target_pairs={{0,8},{4,12},{8,0},{12,4},{16,24},{20,28},{24,16},{28,20},{1,9},{5... | collective-permute-start | bytes 1966088 | tf_op jit(solution)/shard_map/ppermute | solution.py:260
  116.0 28.4 %collective-permute-start.32 = (bf16[4,128,640]{2,1,0:T(8,128)(2,1)S(1)}, bf16[4,128,640]{2,1,0:T(8,128)(2,1)S(1)}, u32[]{:S(2)}, u32[]{:S(2)}) collective-permute-start(bf16[4,128,640]{2,1,0:T(8,128)(2,1)S(1)} %bitcast.222), channel_id=1, source_target_pairs={{0,4},{4,0},{8,12},{12,8},{16,20},{20,16},{24,28},{28,24},{1,5},{5... | collective-permute-start | bytes 1966088 | tf_op jit(solution)/shard_map/ppermute | solution.py:260
  120.2 26.4 %collective-permute-start.33 = (bf16[4,128,640]{2,1,0:T(8,128)(2,1)S(1)}, bf16[4,128,640]{2,1,0:T(8,128)(2,1)}, u32[]{:S(2)}, u32[]{:S(2)}) collective-permute-start(bf16[4,128,640]{2,1,0:T(8,128)(2,1)S(1)} %bitcast.223), channel_id=1, source_target_pairs={{0,4},{4,0},{8,12},{12,8},{16,20},{20,16},{24,28},{28,24},{1,5},{5... | collective-permute-start | bytes 1966088 | tf_op jit(solution)/shard_map/ppermute | solution.py:260
  132.9 16.8 %collective-permute-start.34 = (bf16[2,128,640]{2,1,0:T(8,128)(2,1)S(1)}, bf16[2,128,640]{2,1,0:T(8,128)(2,1)S(1)}, u32[]{:S(2)}, u32[]{:S(2)}) collective-permute-start(bf16[2,128,640]{2,1,0:T(8,128)(2,1)S(1)} %slice_bitcast_fusion.11), channel_id=1, source_target_pairs={{0,16},{4,20},{8,24},{12,28},{16,0},{20,4},{24,8},{28,12},{1,17},{... | collective-permute-start | bytes 983048 | tf_op jit(solution)/shard_map/ppermute | solution.py:260
  133.3 13.4 %collective-permute-start.31 = (bf16[128,1024]{1,0:T(8,128)(2,1)}, bf16[128,1024]{1,0:T(8,128)(2,1)S(1)}, u32[]{:S(2)}, u32[]{:S(2)}) collective-permute-start(bf16[128,1024]{1,0:T(8,128)(2,1)} %get-tuple-element.178.grad_h1b_ref.refs_4_), channel_id=1, source_target_pairs={{0,2},{1,3},{2,0},{3,1},{4,6},{5,7},{6,4},{7,5},{8,10},{9,11},{10,... | collective-permute-start | bytes 786440 | tf_op jit(solution)/shard_map/ppermute | solution.py:260
  143.0 11.9 %collective-permute-start.35 = (bf16[144,1664]{1,0:T(8,128)(2,1)}, bf16[144,1664]{1,0:T(8,128)(2,1)}, u32[]{:S(2)}, u32[]{:S(2)}) collective-permute-start(bf16[144,1664]{1,0:T(8,128)(2,1)} %get-tuple-element.194.refs_8_), channel_id=1, source_target_pairs={{0,2},{1,3},{2,0},{3,1},{4,6},{5,7},{6,4},{7,5},{8,10},{9,11},{10,... | collective-permute-start | bytes 1437704 | tf_op jit(solution)/shard_map/ppermute | solution.py:260
  144.4 10.6 %collective-permute-start.36 = (bf16[144,1664]{1,0:T(8,128)(2,1)}, bf16[144,1664]{1,0:T(8,128)(2,1)}, u32[]{:S(2)}, u32[]{:S(2)}) collective-permute-start(bf16[144,1664]{1,0:T(8,128)(2,1)} %get-tuple-element.194.refs_8_), channel_id=1, source_target_pairs={{0,1},{1,0},{2,3},{3,2},{4,5},{5,4},{6,7},{7,6},{8,9},{9,8},{10,11... | collective-permute-start | bytes 1437704 | tf_op jit(solution)/shard_map/ppermute | solution.py:260
  149.8 10.2 %collective-permute-start.38 = (bf16[128,1024]{1,0:T(8,128)(2,1)S(1)}, bf16[128,1024]{1,0:T(8,128)(2,1)S(1)}, u32[]{:S(2)}, u32[]{:S(2)}) collective-permute-start(bf16[128,1024]{1,0:T(8,128)(2,1)S(1)} %collective-permute-done.31.refs_5_), channel_id=1, source_target_pairs={{0,1},{1,0},{2,3},{3,2},{4,5},{5,4},{6,7},{7,6},{8,9},{9,8},{10,11... | collective-permute-start | bytes 786440 | tf_op jit(solution)/shard_map/ppermute | solution.py:260
  153.3 19.1 %collective-permute-start.42 = (bf16[2,2,128,640]{3,2,1,0:T(8,128)(2,1)}, bf16[2,2,128,640]{3,2,1,0:T(8,128)(2,1)}, u32[]{:S(2)}, u32[]{:S(2)}) collective-permute-start(bf16[2,2,128,640]{3,2,1,0:T(8,128)(2,1)} %fusion.21), channel_id=1, source_target_pairs={{0,8},{4,12},{8,0},{12,4},{16,24},{20,28},{24,16},{28,20},{1,9},{5... | collective-permute-start | bytes 1966088 | tf_op jit(solution)/shard_map/ppermute | solution.py:260
  163.6 11.3 %collective-permute-start.44 = (bf16[256,1024]{1,0:T(8,128)(2,1)S(1)}, bf16[256,1024]{1,0:T(8,128)(2,1)S(1)}, u32[]{:S(2)}, u32[]{:S(2)}) collective-permute-start(bf16[256,1024]{1,0:T(8,128)(2,1)S(1)} %slice.229), channel_id=1, source_target_pairs={{0,1},{1,0},{2,3},{3,2},{4,5},{5,4},{6,7},{7,6},{8,9},{9,8},{10,11... | collective-permute-start | bytes 1572872 | tf_op jit(solution)/shard_map/ppermute | solution.py:260
  170.9 20.6 %collective-permute-start.41 = (bf16[128,2560]{1,0:T(8,128)(2,1)}, bf16[128,2560]{1,0:T(8,128)(2,1)S(1)}, u32[]{:S(2)}, u32[]{:S(2)}) collective-permute-start(bf16[128,2560]{1,0:T(8,128)(2,1)} %get-tuple-element.198), channel_id=1, source_target_pairs={{0,4},{4,0},{8,12},{12,8},{16,20},{20,16},{24,28},{28,24},{1,5},{5... | collective-permute-start | bytes 1966088 | tf_op jit(solution)/shard_map/ppermute | solution.py:260
  173.7 17.8 %collective-permute-start.43 = (bf16[2,128,640]{2,1,0:T(8,128)(2,1)S(1)}, bf16[2,128,640]{2,1,0:T(8,128)(2,1)S(1)}, u32[]{:S(2)}, u32[]{:S(2)}) collective-permute-start(bf16[2,128,640]{2,1,0:T(8,128)(2,1)S(1)} %slice_bitcast_fusion.9), channel_id=1, source_target_pairs={{0,16},{4,20},{8,24},{12,28},{16,0},{20,4},{24,8},{28,12},{1,17},{... | collective-permute-start | bytes 983048 | tf_op jit(solution)/shard_map/ppermute | solution.py:260
  191.7 9.1 %collective-permute-start.46 = (bf16[2,32,2560]{2,1,0:T(8,128)(2,1)S(1)}, bf16[2,32,2560]{2,1,0:T(8,128)(2,1)S(1)}, u32[]{:S(2)}, u32[]{:S(2)}) collective-permute-start(bf16[2,32,2560]{2,1,0:T(8,128)(2,1)S(1)} %slice_bitcast_fusion.7), channel_id=1, source_target_pairs={{0,8},{4,12},{8,0},{12,4},{16,24},{20,28},{24,16},{28,20},{1,9},{5... | collective-permute-start | bytes 983048 | tf_op jit(solution)/shard_map/ppermute | solution.py:260
  (46 other events, 256.3 us)

commit v5 on v4

--- a/solution.py
+++ b/solution.py
@@ -413,7 +413,7 @@
     grad_in2 = grad_a_ref[...].astype(F32) + grad_b_ref[...].astype(F32)
     normed2, scale2 = norm_rows(hidden1_ref[...])
     back2, gain2_term = norm_rows_back(grad_in2, normed2, scale2, gains_ref[1:2, :])
-    grad_h1 = grad_out_ref[...].astype(F32) + back2
+    grad_h1 = grad_out_ref[: hidden1_ref.shape[0], :].astype(F32) + back2
     grad_h1_ref[...] = grad_h1
     grad_h1b_ref[...] = grad_h1.astype(BF)
     gain2_ref[...] = gain2_term
@@ -479,7 +479,7 @@
 
 
 def make_terms(n_far, n_sub, own, padded, count):
-    def kernel(place_ref, rows_ref, gains_ref, *refs):
+    def kernel(place_ref, rows_a_ref, rows_b_ref, gains_ref, *refs):
         att_refs = refs[:n_sub]
         grad_h1_refs = refs[n_sub : 2 * n_sub]
         grads_refs = refs[2 * n_sub : 3 * n_sub]
@@ -499,10 +499,11 @@
         owner = ((block % n_far * 2 + block // n_far) ^ place_ref[0]) * n_sub + place_ref[2]
         source = jnp.where(spot % padded < own, owner * own + spot % padded, -1)
         select_d = (lax.broadcasted_iota(jnp.int32, (D, rows), 0) == source).astype(F32).astype(BF)
-        group = rows_ref[...].astype(F32)
+        rows_b = jnp.concatenate([rows_a_ref[...], rows_b_ref[...]], axis=0)
+        group = rows_b.astype(F32)
         scale = lax.rsqrt(jnp.sum(group * group, axis=1, keepdims=True) * (1.0 / D) + EPS)
         gain = dot_f(gains_ref[...].astype(BF), select)[0:1, :]
-        left1 = (dot_f(rows_ref[...], select_d) * scale * gain).astype(BF)
+        left1 = (dot_f(rows_b, select_d) * scale * gain).astype(BF)
         left2 = dot_f(tokens([ref[...] for ref in grad_h1_refs]), select).astype(BF)
         right = tokens([ref[:count, :] for ref in grads_refs])
         extra = tokens([ref[count:, :256] for ref in grads_refs])
@@ -581,8 +582,6 @@
     sine = jnp.concatenate([sine, sine], axis=1)
     seg = allowed.astype(F32)
     rows32 = mm(rows, spread_mat)
-    cot = (live * cotangent.astype(F32)).astype(BF)
-    cot_y = swap(cot, "sub", 2)
 
     owner = ((rel ^ my_fsdp) * n_sub + place % n_sub)[None, :]
 
@@ -590,7 +589,10 @@
     attn_block = attn_block.at[own, :share].set(gains)
     far = [swap(attn_block, "fsdp", 2 * k) for k in range(1, n_far)]
     mlp_block = jnp.stack([padded_block(w) for w in (gate_weight, up_weight, down_weight)])
-    came = swap(columns(mlp_block, 1 - my_y, half_ff), "sub", 2)
+    sent = columns(mlp_block, 1 - my_y, half_ff)
+    came = swap(sent, "sub", 2)
+    cot = (live * after(cotangent, sent).astype(F32)).astype(BF)
+    cot_y = swap(cot, "sub", 2)
     mlp_block = put2(columns(mlp_block, my_y, half_ff), came, my_y, 1)
     came = swap(columns(mlp_block, 1 - my_c, quarter), "sub", 1)
     mlp_block = put2(columns(mlp_block, my_c, quarter), came, my_c, 2)
@@ -616,10 +618,9 @@
     y0, x1, third = swap(half0, "sub", 2), swap(half1, "fsdp", 1), swap(gate_up, "fsdp", 4)
     down_x = swap(down, "fsdp", 1)
     cot_all = mm(jnp.concatenate([cot, cot_c]), spread_mat).astype(BF)
-    half0, half1, gate_up, down, down_x, near, y0, x1, third, cot_all, rows = meet(
-        half0, half1, gate_up, down, down_x, near, y0, x1, third, cot_all, rows
-    )
-    grad_outb = cot_all[:count]
+    half0, half1, gate_up, down, down_x, near, y0, x1, third, cot_all = meet(
+        half0, half1, gate_up, down, down_x, near, y0, x1, third, cot_all
+    )
 
     half0 = put2(half0, y0, my_y, 2).reshape(wide // 2, half_ff)
     half1 = jnp.stack([half1, x1]).reshape(wide // 2, half_ff)
@@ -662,8 +663,7 @@
     in2_c = swap(in2_all, "sub", 1)
     rows_c = swap(rows_all, "sub", 1)
     in2_c, gate_up_x, rows_c = meet(in2_c, gate_up_x, rows_c)
-    rows_all = jnp.concatenate([rows_all, rows_c])
-    att_y = swap(att, "sub", 2)
+    att_y = swap(after(att, in2_c), "sub", 2)
     in2_all = jnp.stack([in2_all, in2_c]).reshape(4 * count, wide)
     gate_w = jnp.stack([gate_up[:, 0], gate_up_x[:, 0]]).reshape(wide, quarter)
     up_w = jnp.stack([gate_up[:, 1], gate_up_x[:, 1]]).reshape(wide, quarter)
@@ -672,36 +672,37 @@
     sigma = jax.nn.sigmoid(gate)
     active = gate * sigma
     hidden = (active * up).astype(BF)
-    hidden, att_y, down_last = meet(hidden, att_y, down_last)
     down_term = term(cot_all, hidden).reshape(2, n_far, n_sub * padded, quarter)
+    hidden, down_term, down_last = meet(hidden, down_term, down_last)
     down_w = jnp.stack([down, down_near, down_third, down_last])
     down_w = down_w.transpose(1, 0, 2, 3).reshape(wide, quarter)
     down_near_came = swap(far_pair(down_term, 1, 1), "fsdp", 2)
-    grad_hidden = mm(after(cot_all, down_term), down_w)
+    grad_hidden = mm(cot_all, down_w)
     grad_gate = (grad_hidden * up * sigma * (1.0 + gate * (1.0 - sigma))).astype(BF)
     grad_up = (grad_hidden * active).astype(BF)
     grad_in2 = (mm_t(grad_gate, gate_w) + mm_t(grad_up, up_w)).astype(BF).reshape(2, 2 * count, wide)
+    in2_terms = after(in2_all, grad_in2)
     gate_up_term = [
-        term(in2_all, grad).reshape(2, n_far, n_sub * padded, quarter) for grad in (grad_gate, grad_up)
+        term(in2_terms, grad).reshape(2, n_far, n_sub * padded, quarter) for grad in (grad_gate, grad_up)
     ]
     gate_up_x_came = [swap(part[1], "fsdp", 1) for part in gate_up_term]
     result = mm_t(hidden, down_w).astype(BF).reshape(2, 2 * count, wide)
 
     came = swap(grad_in2[1], "sub", 1)
+    came, att_y = meet(came, att_y)
     atts = [att, att_y, swap(att, "sub", 1), swap(att_y, "sub", 1)]
-    came, atts = meet(came, atts)
     grad_in2 = add2(grad_in2[0], came).reshape(2, count, wide)
     grad_in2_y = swap(grad_in2[1], "sub", 2)
+    down_held = add2(far_pair(down_term, 1, 0), down_near_came)
+    grad_in2_y, result, down_held, atts = meet(grad_in2_y, result, down_held, atts)
+    down_far_came = swap(down_held[:, 1], "fsdp", 4)
     grad_h1, grad_h1b, gain2_term = run_kernel(
         norm_kernel,
         [(tall, F32), (tall, BF), ((1, wide), F32)],
-        (my_place, grad_in2[0], grad_in2_y, grad_outb, hidden1, gains_p),
+        (my_place, grad_in2[0], grad_in2_y, cot_all, hidden1, gains_p),
         name="norm_backward",
     )
     grad_h1_y = swap(grad_h1b, "sub", 2)
-    grad_h1, down_near_came = meet(grad_h1, down_near_came)
-    down_held = add2(far_pair(down_term, 1, 0), down_near_came)
-    down_far_came = swap(down_held[:, 1], "fsdp", 4)
     grads, input_grad = run_kernel(
         make_backward(n_fsdp, own),
         [((count + 16, half_ff + 384), BF), (tall, F32)],
@@ -714,26 +715,26 @@
     )
 
     grads_y = swap(grads, "sub", 2)
-    grads_c = swap(grads, "sub", 1)
     grads, grad_h1_y, gate_up_x_came, down_far_came = meet(
         grads, grad_h1_y, gate_up_x_came, down_far_came
     )
+    grads_c = swap(grads, "sub", 1)
     grad_h1_c, grad_h1_yc = swap(grad_h1b, "sub", 1), swap(grad_h1_y, "sub", 1)
+    down_held = add2(down_held[:, 0], down_far_came)
+    down_x_came = swap(down_held[1], "fsdp", 1)
+    gate_up_x_came, down_held = meet(gate_up_x_came, down_held)
     gate_up_held = jnp.stack([add2(part[0], came) for part, came in zip(gate_up_term, gate_up_x_came)])
     gate_up_near = swap(far_pair(gate_up_held, 1, 1), "fsdp", 2)
-    down_held = add2(down_held[:, 0], down_far_came)
-    down_x_came = swap(down_held[1], "fsdp", 1)
     grads_y, grads_c, grad_h1_c, grad_h1_yc, down_x_came = meet(
         grads_y, grads_c, grad_h1_c, grad_h1_yc, down_x_came
     )
 
     grads_yc = swap(grads_y, "sub", 1)
-    res_c = swap(after(result[1], grads_y), "sub", 1)
     attn_keep, attn_send = run_kernel(
         make_terms(n_far, n_sub, own, padded, count),
         [((n_far * padded, FF), BF)] * 2,
         (
-            my_place, rows_all, gains_p, *atts, grad_h1b, grad_h1_y, grad_h1_c, grad_h1_yc, grads, grads_y, grads_c, grads_yc,
+            my_place, rows_all, rows_c, gains_p, *atts, grad_h1b, grad_h1_y, grad_h1_c, grad_h1_yc, grads, grads_y, grads_c, grads_yc,
         ),
         name="attn_terms",
     )
@@ -741,6 +742,7 @@
     attn_x = swap(attn_send, "fsdp", 1)
     gate_up_held = add2(far_pair(gate_up_held, 1, 0), after(gate_up_near, attn_send))
     gate_up_far = swap(gate_up_held[:, 1], "fsdp", 4)
+    res_c = swap(after(result[1], attn_send), "sub", 1)
     result = add2(result[0], res_c).reshape(2, count, wide)
     res_y = swap(result[1], "sub", 2)
     input_grad = after(input_grad, attn_send)
@@ -763,9 +765,10 @@
     mlp_own = mlp_own.reshape(3, 2, 2, padded, quarter)
     mlp_c = swap(pick(mlp_own, 1 - my_c, 2), "sub", 1)
     attn_near, mlp_c = meet(attn_near, mlp_c)
+    attn_held = add2(far_pair(attn_held, 0, 0), attn_near)
+    mlp_c = after(mlp_c, attn_held)
     mlp_own = side_by_side(pick(mlp_own, my_c, 2), mlp_c, my_c)
     mlp_y = swap(pick(mlp_own, 1 - my_y, 1), "sub", 2)
-    attn_held = add2(far_pair(attn_held, 0, 0), attn_near)
     attn_far = swap(attn_held[1], "fsdp", 4)
     result = hidden1 + result[0].astype(F32) + res_y.astype(F32)
     output = mm_t((live * result).astype(BF), spread_mat).astype(BF)

time: 213 us -> 202 us (0.948)
  waiting for transfers between devices: 85.6 us -> 79.3 us
  other arithmetic: 19.3 us -> 14.7 us
  starting transfers between devices: 41.8 us -> 45.1 us
  local copies, waits for them, and re-layouts: 16.4 us -> 14 us
    ppermute x50, waiting for transfers between devices: 85.6 us -> 79.3 us  [swap(): lax.ppermute(value, axis, [(i, i ^ bit) for i in range(lax.axis_size(axis...]
    convert_element_type x12, other arithmetic: 5.84 us -> 2.53 us  [add2(): return (kept.astype(F32) + came.astype(F32)).astype(BF)]
    ppermute x50, starting transfers between devices: 41.8 us -> 45.1 us  [swap(): lax.ppermute(value, axis, [(i, i ^ bit) for i in range(lax.axis_size(axis...]
    unnamed x57 -> x56, local copies, waits for them, and re-layouts: 4.57 us -> 4.01 us
  transfers between devices with their start and end apart: 50 -> 50, of which waited for: 23 -> 22; matrix products, arithmetic and copies ran while one was open for 21% -> 19% of each run, Pallas kernels for 13% -> 14%
where the time goes in v5:
time: 202 us; the launch traced here: 201 us
  waiting for transfers between devices  79.3 us (39%)
  starting transfers between devices  45.1 us (22%)
  Pallas kernels  27.4 us (14%)
  matrix products  17.7 us (9%)
  other arithmetic  14.7 us (7%)
  local copies, waits for them, and re-layouts  14 us (7%)
  between operations  2.89 us (1%)
    ppermute x50, waiting for transfers between devices, swap(): lax.ppermute(value, axis, [(i, i ^ bit) for i in range(lax.axis_size(axis...  79.3 us
    ppermute x50, starting transfers between devices, swap(): lax.ppermute(value, axis, [(i, i ^ bit) for i in range(lax.axis_size(axis...  45.1 us
    pallas_call x4, Pallas kernels, run_kernel(): pl.pallas_call(kernel, out_shape=[jax.ShapeDtypeStruct(shape, kind) for s...  27.4 us
    dot_general x5, matrix products, mm(): return jnp.dot(a, b, preferred_element_type=F32)  7.36 us
    dot_general x4, matrix products, mm_t(): lax.dot_general(a, b, (((1,), (1,)), ((), ())), preferred_element_type=F32)  4.55 us
  transfers between devices with their start and end apart: 50, of which 22 were waited for; matrix products, arithmetic and copies ran while one was open for 19% of the time, Pallas kernels for 14%

profile of v5, /device:TPU:0, one launch (start us, length us, event | category | flops | bytes accessed | tf_op | source)
XLA Modules:
  0.0 201.1 jit_solution(16744330823160291659)
XLA Ops:
  2.7 5.1 %collective-permute-start.2 = (bf16[32,2560]{1,0:T(8,128)(2,1)S(1)}, bf16[32,2560]{1,0:T(8,128)(2,1)S(1)}, u32[]{:S(2)}, u32[]{:S(2)}) collective-permute-start(bf16[32,2560]{1,0:T(8,128)(2,1)S(1)} %scatter.4), channel_id=1, source_target_pairs={{0,24},{4,28},{8,16},{12,20},{16,8},{20,12},{24,0},{28,4},{1,25},{... | collective-permute-start | bytes 491528 | tf_op jit(solution)/shard_map/ppermute | solution.py:260
  10.2 1.7 collective-permute-start.3
  18.3 1.6 fusion.14.rows_ref
  20.2 1.6 collective-permute-done.1
  24.5 1.5 collective-permute-start.7
  28.2 5.1 %collective-permute-done.8 = bf16[2,128,640]{2,1,0:T(8,128)(2,1)S(1)} collective-permute-done((bf16[2,128,640]{2,1,0:T(8,128)(2,1)S(1)}, bf16[2,128,640]{2,1,0:T(8,128)(2,1)S(1)}, u32[]{:S(2)}, u32[]{:S(2)}) %collective-permute-start.8) | collective-permute-done | bytes 327712 | tf_op jit(solution)/shard_map/ppermute | solution.py:260
  35.7 1.6 collective-permute-start.12
  37.9 2.6 %collective-permute-start.13 = (bf16[2,128,640]{2,1,0:T(8,128)(2,1)S(1)}, bf16[2,128,640]{2,1,0:T(8,128)(2,1)}, u32[]{:S(2)}, u32[]{:S(2)}) collective-permute-start(bf16[2,128,640]{2,1,0:T(8,128)(2,1)S(1)} %slice.165), channel_id=1, source_target_pairs={{0,16},{4,20},{8,24},{12,28},{16,0},{20,4},{24,8},{28,12},{1,17},{... | collective-permute-start | bytes 983048 | tf_op jit(solution)/shard_map/ppermute | solution.py:260
  41.1 2.3 %fusion.8.grad_out_ref = bf16[512,1024]{1,0:T(8,128)(2,1)} fusion(s32[1024]{0:T(1024)S(1)} %fusion.60, bf16[256,960]{0,1:T(8,128)(2,1)S(1)} %collective-permute-done.9, bf16[256,960]{0,1:T(8,128)(2,1)S(1)} %constant_dynamic-update-slice_fusion), kind=kOutput, calls=%fused_computation.13 | convolution fusion | flops 1010106368 | bytes 2035712 | tf_op jit(solution)/shard_map/dot_general | solution.py:291
  43.4 11.6 %collective-permute-done.10 = bf16[128,640]{1,0:T(8,128)(2,1)S(1)} collective-permute-done((bf16[128,640]{1,0:T(8,128)(2,1)S(1)}, bf16[128,640]{1,0:T(8,128)(2,1)S(1)}, u32[]{:S(2)}, u32[]{:S(2)}) %collective-permute-start.10) | collective-permute-done | bytes 163872 | tf_op jit(solution)/shard_map/ppermute | solution.py:260
  60.1 6.8 %collective-permute-done.17 = bf16[128,960]{1,0:T(8,128)(2,1)S(1)} collective-permute-done((bf16[128,960]{1,0:T(8,128)(2,1)S(1)}, bf16[128,960]{1,0:T(8,128)(2,1)S(1)}, u32[]{:S(2)}, u32[]{:S(2)}) %collective-permute-start.17) | collective-permute-done | bytes 245792 | tf_op jit(solution)/shard_map/ppermute | solution.py:260
  68.6 1.6 collective-permute-start.22
  70.1 2.6 %collective-permute-start.20 = (bf16[2,128,640]{2,1,0:T(8,128)(2,1)S(1)}, bf16[2,128,640]{2,1,0:T(8,128)(2,1)S(1)}, u32[]{:S(2)}, u32[]{:S(2)}) collective-permute-start(bf16[2,128,640]{2,1,0:T(8,128)(2,1)S(1)} %pad_maximum_fusion.14), channel_id=1, source_target_pairs={{0,16},{4,20},{8,24},{12,28},{16,0},{20,4},{24,8},{28,12},{1,17},{... | collective-permute-start | bytes 983048 | tf_op jit(solution)/shard_map/ppermute | solution.py:260
  74.6 10.3 %attn_forward.1 = (bf16[128,1024]{1,0:T(8,128)(2,1)}, bf16[128,1280]{1,0:T(8,128)(2,1)}, bf16[128,384]{1,0:T(8,128)(2,1)}, f32[128,15]{1,0:T(8,128)}, f32[128,10...) custom-call(s32[3]{0:T(128)} %pad_add_fusion.place_ref, ...), custom_call_target="tpu_custom_call" | custom-call | flops 1000 | bytes 1000 | tf_op jit(solution)/shard_map/attn_forward/pallas_call | solution.py:535
  85.6 6.4 %collective-permute-done.18 = bf16[128,1024]{1,0:T(8,128)(2,1)S(1)} collective-permute-done((bf16[128,1024]{1,0:T(8,128)(2,1)}, bf16[128,1024]{1,0:T(8,128)(2,1)S(1)}, u32[]{:S(2)}, u32[]{:S(2)}) %collective-permute-start.18) | collective-permute-done | bytes 262176 | tf_op jit(solution)/shard_map/ppermute | solution.py:260
  96.1 2.9 %collective-permute-done.22 = bf16[4,2,128,640]{3,2,0,1:T(8,128)(2,1)S(1)} collective-permute-done((bf16[4,2,128,640]{3,2,0,1:T(8,128)(2,1)S(1)}, bf16[4,2,128,640]{3,2,0,1:T(8,128)(2,1)S(1)}, u32[]{:S(2)}, u32[]{:S(2)}) %collective-permute-start.22) | collective-permute-done | bytes 1310752 | tf_op jit(solution)/shard_map/ppermute | solution.py:260
  114.0 1.6 collective-permute-start.32
  117.1 4.7 %collective-permute-done.28 = bf16[2,2,128,640]{3,2,1,0:T(8,128)(2,1)S(1)} collective-permute-done((bf16[2,2,128,640]{3,2,1,0:T(8,128)(2,1)S(1)}, bf16[2,2,128,640]{3,2,1,0:T(8,128)(2,1)S(1)}, u32[]{:S(2)}, u32[]{:S(2)}) %collective-permute-start.28) | collective-permute-done | bytes 655392 | tf_op jit(solution)/shard_map/ppermute | solution.py:260
  122.1 2.6 %collective-permute-done.27.grad_b_ref = bf16[128,1024]{1,0:T(8,128)(2,1)S(1)} collective-permute-done((bf16[128,1024]{1,0:T(8,128)(2,1)S(1)}, bf16[128,1024]{1,0:T(8,128)(2,1)S(1)}, u32[]{:S(2)}, u32[]{:S(2)}) %collective-permute-start.27) | collective-permute-done | bytes 262176 | tf_op jit(solution)/shard_map/ppermute | solution.py:260
  126.0 2.7 %norm_backward.1 = (f32[128,1024]{1,0:T(8,128)}, bf16[128,1024]{1,0:T(8,128)(2,1)}, f32[1,1024]{1,0:T(1,128)}) custom-call(s32[3]{0:T(128)} %pad_add_fusion.place_ref, bf16[128,1024]{1,0:T(8,128)(2,1)} %get-tuple-element.255.grad_a_ref, bf16[128,1024]{1,0:T(8,128)(2,1)} %copy-done.12, bf16[512,1024]{1,0:T(8,128)(2,1)} %fusion.8.grad_out_ref, ...), custom_call_target="tpu_custom_call" | custom-call | flops 1000 | bytes 1000 | tf_op jit(solution)/shard_map/norm_backward/pallas_call | solution.py:535
  130.0 9.1 %attn_backward.1 = (bf16[144,1664]{1,0:T(8,128)(2,1)}, f32[128,1024]{1,0:T(8,128)}) custom-call(s32[3]{0:T(128)} %pad_add_fusion.place_ref, f32[128,1024]{1,0:T(8,128)} %get-tuple-element.190.grad_h1_ref, bf16[128,1024]{1,0:T(8,128)(2,1)} %get-tuple-element.189.grad_h1b_ref.refs_4_, f32[1,1024]{1,0:T(1,128)} %get-tuple-element.191.gain2_ref, ...), custom_call_target="tpu_custom_call" | custom-call | flops 1000 | bytes 1000 | tf_op jit(solution)/shard_map/attn_backward/pallas_call | solution.py:535
  139.9 3.6 %collective-permute-done.32 = bf16[4,128,640]{2,1,0:T(8,128)(2,1)S(1)} collective-permute-done((bf16[4,128,640]{2,1,0:T(8,128)(2,1)S(1)}, bf16[4,128,640]{2,1,0:T(8,128)(2,1)S(1)}, u32[]{:S(2)}, u32[]{:S(2)}) %collective-permute-start.32) | collective-permute-done | bytes 655392 | tf_op jit(solution)/shard_map/ppermute | solution.py:260
  146.9 5.8 %collective-permute-done.35.refs_9_ = bf16[144,1664]{1,0:T(8,128)(2,1)S(1)} collective-permute-done((bf16[144,1664]{1,0:T(8,128)(2,1)}, bf16[144,1664]{1,0:T(8,128)(2,1)S(1)}, u32[]{:S(2)}, u32[]{:S(2)}) %collective-permute-start.35) | collective-permute-done | bytes 479264 | tf_op jit(solution)/shard_map/ppermute | solution.py:260
  155.5 5.2 %attn_terms.1 = (bf16[128,2560]{1,0:T(8,128)(2,1)}, bf16[128,2560]{1,0:T(8,128)(2,1)}) custom-call(s32[3]{0:T(128)} %pad_add_fusion.place_ref, bf16[256,960]{1,0:T(8,128)(2,1)} %copy-done.2, bf16[256,960]{1,0:T(8,128)(2,1)} %copy-done.7, f32[2,1024]{1,0:T(2,128)} %get-tuple-element.170.gains_ref, bf16[128,1024]{1,0:T(8,128)(2,1)} %get-tuple-element.183.refs_0_, ...), custom_call_target="tpu_custom_call" | custom-call | flops 1000 | bytes 1000 | tf_op jit(solution)/shard_map/attn_terms/pallas_call | solution.py:535
  160.9 1.5 collective-permute-start.41
  163.0 2.2 %collective-permute-start.43 = (bf16[2,128,640]{2,1,0:T(8,128)(2,1)S(1)}, bf16[2,128,640]{2,1,0:T(8,128)(2,1)S(1)}, u32[]{:S(2)}, u32[]{:S(2)}) collective-permute-start(bf16[2,128,640]{2,1,0:T(8,128)(2,1)S(1)} %slice_bitcast_fusion.10), channel_id=1, source_target_pairs={{0,16},{4,20},{8,24},{12,28},{16,0},{20,4},{24,8},{28,12},{1,17},{... | collective-permute-start | bytes 983048 | tf_op jit(solution)/shard_map/ppermute | solution.py:260
  168.0 2.7 %fusion.1 = f32[128,960]{0,1:T(8,128)} fusion(f32[128,1024]{1,0:T(8,128)S(1)} %copy-done.26, s32[1024]{0:T(1024)S(1)} %fusion.60), kind=kOutput, calls=%fused_computation.2 | convolution fusion | flops 1510932480 | bytes 1019904 | tf_op jit(solution)/shard_map/dot_general | solution.py:749
  170.6 9.7 %collective-permute-done.43 = bf16[2,128,640]{2,1,0:T(8,128)(2,1)S(1)} collective-permute-done((bf16[2,128,640]{2,1,0:T(8,128)(2,1)S(1)}, bf16[2,128,640]{2,1,0:T(8,128)(2,1)S(1)}, u32[]{:S(2)}, u32[]{:S(2)}) %collective-permute-start.43) | collective-permute-done | bytes 327712 | tf_op jit(solution)/shard_map/ppermute | solution.py:260
  181.4 1.5 fusion.15
  182.9 6.8 %collective-permute-done.46 = bf16[2,32,2560]{2,1,0:T(8,128)(2,1)S(1)} collective-permute-done((bf16[2,32,2560]{2,1,0:T(8,128)(2,1)S(1)}, bf16[2,32,2560]{2,1,0:T(8,128)(2,1)S(1)}, u32[]{:S(2)}, u32[]{:S(2)}) %collective-permute-start.46) | collective-permute-done | bytes 327712 | tf_op jit(solution)/shard_map/ppermute | solution.py:260
  190.8 1.6 collective-permute-start.48
  192.4 4.0 %collective-permute-done.49 = bf16[3,32,1280]{2,1,0:T(8,128)(2,1)S(1)} collective-permute-done((bf16[3,32,1280]{2,1,0:T(8,128)(2,1)S(1)}, bf16[3,32,1280]{2,1,0:T(8,128)(2,1)S(1)}, u32[]{:S(2)}, u32[]{:S(2)}) %collective-permute-start.49) | collective-permute-done | bytes 245792 | tf_op jit(solution)/shard_map/ppermute | solution.py:260
  (228 shorter events, 67.6 us)
Async XLA Ops:
  2.7 17.4 %collective-permute-start.2 = (bf16[32,2560]{1,0:T(8,128)(2,1)S(1)}, bf16[32,2560]{1,0:T(8,128)(2,1)S(1)}, u32[]{:S(2)}, u32[]{:S(2)}) collective-permute-start(bf16[32,2560]{1,0:T(8,128)(2,1)S(1)} %scatter.4), channel_id=1, source_target_pairs={{0,24},{4,28},{8,16},{12,20},{16,8},{20,12},{24,0},{28,4},{1,25},{... | collective-permute-start | bytes 491528 | tf_op jit(solution)/shard_map/ppermute | solution.py:260
  7.8 13.9 %collective-permute-start.1 = (bf16[32,2560]{1,0:T(8,128)(2,1)S(1)}, bf16[32,2560]{1,0:T(8,128)(2,1)S(1)}, u32[]{:S(2)}, u32[]{:S(2)}) collective-permute-start(bf16[32,2560]{1,0:T(8,128)(2,1)S(1)} %scatter.4), channel_id=1, source_target_pairs={{0,16},{4,20},{8,24},{12,28},{16,0},{20,4},{24,8},{28,12},{1,17},{... | collective-permute-start | bytes 491528 | tf_op jit(solution)/shard_map/ppermute | solution.py:260
  7.9 13.9 %collective-permute-start = (bf16[32,2560]{1,0:T(8,128)(2,1)S(1)}, bf16[32,2560]{1,0:T(8,128)(2,1)S(1)}, u32[]{:S(2)}, u32[]{:S(2)}) collective-permute-start(bf16[32,2560]{1,0:T(8,128)(2,1)S(1)} %scatter.4), channel_id=1, source_target_pairs={{0,8},{4,12},{8,0},{12,4},{16,24},{20,28},{24,16},{28,20},{1,9},{5... | collective-permute-start | bytes 491528 | tf_op jit(solution)/shard_map/ppermute | solution.py:260
  22.8 12.8 %collective-permute-start.9 = (bf16[256,960]{0,1:T(8,128)(2,1)S(1)}, bf16[256,960]{0,1:T(8,128)(2,1)S(1)}, u32[]{:S(2)}, u32[]{:S(2)}) collective-permute-start(bf16[256,960]{0,1:T(8,128)(2,1)S(1)} %constant_dynamic-update-slice_fusion), channel_id=1, source_target_pairs={{0,1},{1,0},{2,3},{3,2},{4,5},{5,4},{6,7},{7,6},{8,9},{9,8},{10,11... | collective-permute-start | bytes 1474568 | tf_op jit(solution)/shard_map/ppermute | solution.py:260
  23.1 10.2 %collective-permute-start.8 = (bf16[2,128,640]{2,1,0:T(8,128)(2,1)S(1)}, bf16[2,128,640]{2,1,0:T(8,128)(2,1)S(1)}, u32[]{:S(2)}, u32[]{:S(2)}) collective-permute-start(bf16[2,128,640]{2,1,0:T(8,128)(2,1)S(1)} %slice.165), channel_id=1, source_target_pairs={{0,8},{4,12},{8,0},{12,4},{16,24},{20,28},{24,16},{28,20},{1,9},{5... | collective-permute-start | bytes 983048 | tf_op jit(solution)/shard_map/ppermute | solution.py:260
  24.5 9.8 %collective-permute-start.7 = (bf16[4,32,1280]{2,1,0:T(8,128)(2,1)S(1)}, bf16[4,32,1280]{2,1,0:T(8,128)(2,1)S(1)}, u32[]{:S(2)}, u32[]{:S(2)}) collective-permute-start(bf16[4,32,1280]{2,1,0:T(8,128)(2,1)S(1)} %get-tuple-element.134), channel_id=1, source_target_pairs={{0,2},{1,3},{2,0},{3,1},{4,6},{5,7},{6,4},{7,5},{8,10},{9,11},{10,... | collective-permute-start | bytes 983048 | tf_op jit(solution)/shard_map/ppermute | solution.py:260
  26.0 9.5 %collective-permute-start.6 = (bf16[4,32,1280]{2,1,0:T(8,128)(2,1)S(1)}, bf16[4,32,1280]{2,1,0:T(8,128)(2,1)S(1)}, u32[]{:S(2)}, u32[]{:S(2)}) collective-permute-start(bf16[4,32,1280]{2,1,0:T(8,128)(2,1)S(1)} %get-tuple-element.132), channel_id=1, source_target_pairs={{0,4},{4,0},{8,12},{12,8},{16,20},{20,16},{24,28},{28,24},{1,5},{5... | collective-permute-start | bytes 983048 | tf_op jit(solution)/shard_map/ppermute | solution.py:260
  35.7 19.3 %collective-permute-start.12 = (bf16[4,2,32,1280]{3,2,1,0:T(8,128)(2,1)S(1)}, bf16[4,2,32,1280]{3,2,1,0:T(8,128)(2,1)S(1)}, u32[]{:S(2)}, u32[]{:S(2)}) collective-permute-start(bf16[4,2,32,1280]{3,2,1,0:T(8,128)(2,1)S(1)} %pad_maximum_fusion.9), channel_id=1, source_target_pairs={{0,4},{4,0},{8,12},{12,8},{16,20},{20,16},{24,28},{28,24},{1,5},{5... | collective-permute-start | bytes 1966088 | tf_op jit(solution)/shard_map/ppermute | solution.py:260
  37.3 17.7 %collective-permute-start.11 = (bf16[2,4,32,1280]{3,2,1,0:T(8,128)(2,1)S(1)}, bf16[2,4,32,1280]{3,2,1,0:T(8,128)(2,1)S(1)}, u32[]{:S(2)}, u32[]{:S(2)}) collective-permute-start(bf16[2,4,32,1280]{3,2,1,0:T(8,128)(2,1)S(1)} %pad_maximum_fusion.8), channel_id=1, source_target_pairs={{0,2},{1,3},{2,0},{3,1},{4,6},{5,7},{6,4},{7,5},{8,10},{9,11},{10,... | collective-permute-start | bytes 1966088 | tf_op jit(solution)/shard_map/ppermute | solution.py:260
  37.9 17.1 %collective-permute-start.13 = (bf16[2,128,640]{2,1,0:T(8,128)(2,1)S(1)}, bf16[2,128,640]{2,1,0:T(8,128)(2,1)}, u32[]{:S(2)}, u32[]{:S(2)}) collective-permute-start(bf16[2,128,640]{2,1,0:T(8,128)(2,1)S(1)} %slice.165), channel_id=1, source_target_pairs={{0,16},{4,20},{8,24},{12,28},{16,0},{20,4},{24,8},{28,12},{1,17},{... | collective-permute-start | bytes 983048 | tf_op jit(solution)/shard_map/ppermute | solution.py:260
  40.5 14.4 %collective-permute-start.10 = (bf16[128,640]{1,0:T(8,128)(2,1)S(1)}, bf16[128,640]{1,0:T(8,128)(2,1)S(1)}, u32[]{:S(2)}, u32[]{:S(2)}) collective-permute-start(bf16[128,640]{1,0:T(8,128)(2,1)S(1)} %slice_bitcast_fusion.15), channel_id=1, source_target_pairs={{0,4},{4,0},{8,12},{12,8},{16,20},{20,16},{24,28},{28,24},{1,5},{5... | collective-permute-start | bytes 491528 | tf_op jit(solution)/shard_map/ppermute | solution.py:260
  55.8 11.4 %collective-permute-start.15 = (bf16[512,1280]{1,0:T(8,128)(2,1)S(1)}, bf16[512,1280]{1,0:T(8,128)(2,1)}, u32[]{:S(2)}, u32[]{:S(2)}) collective-permute-start(bf16[512,1280]{1,0:T(8,128)(2,1)S(1)} %bitcast.196), channel_id=1, source_target_pairs={{0,1},{1,0},{2,3},{3,2},{4,5},{5,4},{6,7},{7,6},{8,9},{9,8},{10,11... | collective-permute-start | bytes 3932168 | tf_op jit(solution)/shard_map/ppermute | solution.py:260
  56.7 10.4 %collective-permute-start.14 = (bf16[512,1280]{1,0:T(8,128)(2,1)S(1)}, bf16[512,1280]{1,0:T(8,128)(2,1)}, u32[]{:S(2)}, u32[]{:S(2)}) collective-permute-start(bf16[512,1280]{1,0:T(8,128)(2,1)S(1)} %bitcast.194), channel_id=1, source_target_pairs={{0,1},{1,0},{2,3},{3,2},{4,5},{5,4},{6,7},{7,6},{8,9},{9,8},{10,11... | collective-permute-start | bytes 3932168 | tf_op jit(solution)/shard_map/ppermute | solution.py:260
  56.7 10.4 %collective-permute-start.16 = (bf16[2,128,640]{2,1,0:T(8,128)(2,1)}, bf16[2,128,640]{2,1,0:T(8,128)(2,1)}, u32[]{:S(2)}, u32[]{:S(2)}) collective-permute-start(bf16[2,128,640]{2,1,0:T(8,128)(2,1)} %collective-permute-done.13), channel_id=1, source_target_pairs={{0,8},{4,12},{8,0},{12,4},{16,24},{20,28},{24,16},{28,20},{1,9},{5... | collective-permute-start | bytes 983048 | tf_op jit(solution)/shard_map/ppermute | solution.py:260
  68.6 30.5 %collective-permute-start.22 = (bf16[4,2,128,640]{3,2,0,1:T(8,128)(2,1)S(1)}, bf16[4,2,128,640]{3,2,0,1:T(8,128)(2,1)S(1)}, u32[]{:S(2)}, u32[]{:S(2)}) collective-permute-start(bf16[4,2,128,640]{3,2,0,1:T(8,128)(2,1)S(1)} %copy.61), channel_id=1, source_target_pairs={{0,4},{4,0},{8,12},{12,8},{16,20},{20,16},{24,28},{28,24},{1,5},{5... | collective-permute-start | bytes 3932168 | tf_op jit(solution)/shard_map/ppermute | solution.py:260
  70.1 21.9 %collective-permute-start.20 = (bf16[2,128,640]{2,1,0:T(8,128)(2,1)S(1)}, bf16[2,128,640]{2,1,0:T(8,128)(2,1)S(1)}, u32[]{:S(2)}, u32[]{:S(2)}) collective-permute-start(bf16[2,128,640]{2,1,0:T(8,128)(2,1)S(1)} %pad_maximum_fusion.14), channel_id=1, source_target_pairs={{0,16},{4,20},{8,24},{12,28},{16,0},{20,4},{24,8},{28,12},{1,17},{... | collective-permute-start | bytes 983048 | tf_op jit(solution)/shard_map/ppermute | solution.py:260
  72.8 19.2 %collective-permute-start.19 = (bf16[2,128,640]{2,1,0:T(8,128)(2,1)S(1)}, bf16[2,128,640]{2,1,0:T(8,128)(2,1)S(1)}, u32[]{:S(2)}, u32[]{:S(2)}) collective-permute-start(bf16[2,128,640]{2,1,0:T(8,128)(2,1)S(1)} %pad_maximum_fusion.14), channel_id=1, source_target_pairs={{0,8},{4,12},{8,0},{12,4},{16,24},{20,28},{24,16},{28,20},{1,9},{5... | collective-permute-start | bytes 983048 | tf_op jit(solution)/shard_map/ppermute | solution.py:260
  93.8 28.2 %collective-permute-start.29 = (bf16[128,1024]{1,0:T(8,128)(2,1)S(1)}, bf16[128,1024]{1,0:T(8,128)(2,1)S(1)}, u32[]{:S(2)}, u32[]{:S(2)}) collective-permute-start(bf16[128,1024]{1,0:T(8,128)(2,1)S(1)} %copy-done.15), channel_id=1, source_target_pairs={{0,1},{1,0},{2,3},{3,2},{4,5},{5,4},{6,7},{7,6},{8,9},{9,8},{10,11... | collective-permute-start | bytes 786440 | tf_op jit(solution)/shard_map/ppermute | solution.py:260
  95.0 10.1 %collective-permute-start.24 = (bf16[2,128,640]{2,1,0:T(8,128)(2,1)S(1)}, bf16[2,128,640]{2,1,0:T(8,128)(2,1)S(1)}, u32[]{:S(2)}, u32[]{:S(2)}) collective-permute-start(bf16[2,128,640]{2,1,0:T(8,128)(2,1)S(1)} %collective-permute-done.20), channel_id=1, source_target_pairs={{0,8},{4,12},{8,0},{12,4},{16,24},{20,28},{24,16},{28,20},{1,9},{5... | collective-permute-start | bytes 983048 | tf_op jit(solution)/shard_map/ppermute | solution.py:260
  99.1 14.9 %collective-permute-start.26 = (bf16[128,1024]{1,0:T(8,128)(2,1)S(1)}, bf16[128,1024]{1,0:T(8,128)(2,1)S(1)}, u32[]{:S(2)}, u32[]{:S(2)}) collective-permute-start(bf16[128,1024]{1,0:T(8,128)(2,1)S(1)} %copy-done.15), channel_id=1, source_target_pairs={{0,2},{1,3},{2,0},{3,1},{4,6},{5,7},{6,4},{7,5},{8,10},{9,11},{10,... | collective-permute-start | bytes 786440 | tf_op jit(solution)/shard_map/ppermute | solution.py:260
  105.5 16.4 %collective-permute-start.28 = (bf16[2,2,128,640]{3,2,1,0:T(8,128)(2,1)S(1)}, bf16[2,2,128,640]{3,2,1,0:T(8,128)(2,1)S(1)}, u32[]{:S(2)}, u32[]{:S(2)}) collective-permute-start(bf16[2,2,128,640]{3,2,1,0:T(8,128)(2,1)S(1)} %slice_bitcast_fusion), channel_id=1, source_target_pairs={{0,8},{4,12},{8,0},{12,4},{16,24},{20,28},{24,16},{28,20},{1,9},{5... | collective-permute-start | bytes 1966088 | tf_op jit(solution)/shard_map/ppermute | solution.py:260
  112.3 26.9 %collective-permute-start.33 = (bf16[4,128,640]{2,1,0:T(8,128)(2,1)S(1)}, bf16[4,128,640]{2,1,0:T(8,128)(2,1)S(1)}, u32[]{:S(2)}, u32[]{:S(2)}) collective-permute-start(bf16[4,128,640]{2,1,0:T(8,128)(2,1)S(1)} %bitcast.225), channel_id=1, source_target_pairs={{0,4},{4,0},{8,12},{12,8},{16,20},{20,16},{24,28},{28,24},{1,5},{5... | collective-permute-start | bytes 1966088 | tf_op jit(solution)/shard_map/ppermute | solution.py:260
  114.0 29.5 %collective-permute-start.32 = (bf16[4,128,640]{2,1,0:T(8,128)(2,1)S(1)}, bf16[4,128,640]{2,1,0:T(8,128)(2,1)S(1)}, u32[]{:S(2)}, u32[]{:S(2)}) collective-permute-start(bf16[4,128,640]{2,1,0:T(8,128)(2,1)S(1)} %bitcast.226), channel_id=1, source_target_pairs={{0,4},{4,0},{8,12},{12,8},{16,20},{20,16},{24,28},{28,24},{1,5},{5... | collective-permute-start | bytes 1966088 | tf_op jit(solution)/shard_map/ppermute | solution.py:260
  124.7 18.8 %collective-permute-start.34 = (bf16[2,128,640]{2,1,0:T(8,128)(2,1)S(1)}, bf16[2,128,640]{2,1,0:T(8,128)(2,1)S(1)}, u32[]{:S(2)}, u32[]{:S(2)}) collective-permute-start(bf16[2,128,640]{2,1,0:T(8,128)(2,1)S(1)} %slice_bitcast_fusion.11), channel_id=1, source_target_pairs={{0,16},{4,20},{8,24},{12,28},{16,0},{20,4},{24,8},{28,12},{1,17},{... | collective-permute-start | bytes 983048 | tf_op jit(solution)/shard_map/ppermute | solution.py:260
  128.7 14.8 %collective-permute-start.31 = (bf16[128,1024]{1,0:T(8,128)(2,1)}, bf16[128,1024]{1,0:T(8,128)(2,1)}, u32[]{:S(2)}, u32[]{:S(2)}) collective-permute-start(bf16[128,1024]{1,0:T(8,128)(2,1)} %get-tuple-element.189.grad_h1b_ref.refs_4_), channel_id=1, source_target_pairs={{0,2},{1,3},{2,0},{3,1},{4,6},{5,7},{6,4},{7,5},{8,10},{9,11},{10,... | collective-permute-start | bytes 786440 | tf_op jit(solution)/shard_map/ppermute | solution.py:260
  130.0 16.0 %collective-permute-start.37 = (bf16[128,1024]{1,0:T(8,128)(2,1)}, bf16[128,1024]{1,0:T(8,128)(2,1)}, u32[]{:S(2)}, u32[]{:S(2)}) collective-permute-start(bf16[128,1024]{1,0:T(8,128)(2,1)} %get-tuple-element.189.grad_h1b_ref.refs_4_), channel_id=1, source_target_pairs={{0,1},{1,0},{2,3},{3,2},{4,5},{5,4},{6,7},{7,6},{8,9},{9,8},{10,11... | collective-permute-start | bytes 786440 | tf_op jit(solution)/shard_map/ppermute | solution.py:260
  139.1 13.6 %collective-permute-start.35 = (bf16[144,1664]{1,0:T(8,128)(2,1)}, bf16[144,1664]{1,0:T(8,128)(2,1)S(1)}, u32[]{:S(2)}, u32[]{:S(2)}) collective-permute-start(bf16[144,1664]{1,0:T(8,128)(2,1)} %get-tuple-element.200.refs_8_), channel_id=1, source_target_pairs={{0,2},{1,3},{2,0},{3,1},{4,6},{5,7},{6,4},{7,5},{8,10},{9,11},{10,... | collective-permute-start | bytes 1437704 | tf_op jit(solution)/shard_map/ppermute | solution.py:260
  143.6 9.2 %collective-permute-start.39 = (bf16[128,640]{1,0:T(8,128)(2,1)S(1)}, bf16[128,640]{1,0:T(8,128)(2,1)S(1)}, u32[]{:S(2)}, u32[]{:S(2)}) collective-permute-start(bf16[128,640]{1,0:T(8,128)(2,1)S(1)} %slice_bitcast_fusion.14), channel_id=1, source_target_pairs={{0,4},{4,0},{8,12},{12,8},{16,20},{20,16},{24,28},{28,24},{1,5},{5... | collective-permute-start | bytes 491528 | tf_op jit(solution)/shard_map/ppermute | solution.py:260
  146.0 16.9 %collective-permute-start.42 = (bf16[2,2,128,640]{3,2,1,0:T(8,128)(2,1)}, bf16[2,2,128,640]{3,2,1,0:T(8,128)(2,1)S(1)}, u32[]{:S(2)}, u32[]{:S(2)}) collective-permute-start(bf16[2,2,128,640]{3,2,1,0:T(8,128)(2,1)} %fusion.22), channel_id=1, source_target_pairs={{0,8},{4,12},{8,0},{12,4},{16,24},{20,28},{24,16},{28,20},{1,9},{5... | collective-permute-start | bytes 1966088 | tf_op jit(solution)/shard_map/ppermute | solution.py:260
  160.9 19.4 %collective-permute-start.41 = (bf16[128,2560]{1,0:T(8,128)(2,1)}, bf16[128,2560]{1,0:T(8,128)(2,1)S(1)}, u32[]{:S(2)}, u32[]{:S(2)}) collective-permute-start(bf16[128,2560]{1,0:T(8,128)(2,1)} %get-tuple-element.207), channel_id=1, source_target_pairs={{0,4},{4,0},{8,12},{12,8},{16,20},{20,16},{24,28},{28,24},{1,5},{5... | collective-permute-start | bytes 1966088 | tf_op jit(solution)/shard_map/ppermute | solution.py:260
  163.0 17.2 %collective-permute-start.43 = (bf16[2,128,640]{2,1,0:T(8,128)(2,1)S(1)}, bf16[2,128,640]{2,1,0:T(8,128)(2,1)S(1)}, u32[]{:S(2)}, u32[]{:S(2)}) collective-permute-start(bf16[2,128,640]{2,1,0:T(8,128)(2,1)S(1)} %slice_bitcast_fusion.10), channel_id=1, source_target_pairs={{0,16},{4,20},{8,24},{12,28},{16,0},{20,4},{24,8},{28,12},{1,17},{... | collective-permute-start | bytes 983048 | tf_op jit(solution)/shard_map/ppermute | solution.py:260
  166.5 13.8 %collective-permute-start.45 = (bf16[128,1024]{1,0:T(8,128)(2,1)S(1)}, bf16[128,1024]{1,0:T(8,128)(2,1)S(1)}, u32[]{:S(2)}, u32[]{:S(2)}) collective-permute-start(bf16[128,1024]{1,0:T(8,128)(2,1)S(1)} %slice.221), channel_id=1, source_target_pairs={{0,2},{1,3},{2,0},{3,1},{4,6},{5,7},{6,4},{7,5},{8,10},{9,11},{10,... | collective-permute-start | bytes 786440 | tf_op jit(solution)/shard_map/ppermute | solution.py:260
  (45 other events, 221.7 us)

commit v6 on v5

--- a/solution.py
+++ b/solution.py
@@ -309,6 +309,10 @@
 
 def dot_0(a, b):
     return lax.dot_general(a, b, (((0,), (0,)), ((), ())), preferred_element_type=F32)
+
+
+def stacked(parts):
+    return jnp.concatenate(parts, axis=0)
 
 
 def norm_rows(values):
@@ -382,22 +386,24 @@
             qk_ref[:, 128 * i : 128 * (i + 1)] = (part * cosine + turned * sine).astype(BF)
         values = dot_f(input1, attn_o_ref[:, :384]).astype(BF)
         v_ref[...] = values
-        allowed = seg_ref[...] > 0.0
-        att_ref[:, :128] = jnp.zeros((rows.shape[0], 128), BF)
+        count = rows.shape[0]
+        allowed = stacked([seg_ref[...]] * GROUP) > 0.0
+        att_ref[:, :128] = jnp.zeros((count, 128), BF)
         shift = kv_width - 256
         for k in range(KV):
             keys = qk_ref[:, D + HD * k : D + HD * (k + 1)]
             value = values[:, HD * k : HD * (k + 1)]
-            for g in range(GROUP):
-                h = GROUP * k + g
-                queries = qk_ref[:, HD * h : HD * (h + 1)]
-                scores = jnp.where(allowed, dot_t(queries, keys) * HD ** (-0.5), NEG)
-                top = jnp.max(scores, axis=1, keepdims=True)
-                expo = jnp.exp(scores - top)
-                total = jnp.sum(expo, axis=1, keepdims=True)
-                logsum_ref[:, h : h + 1] = top + jnp.log(total)
-                weights = (expo / total).astype(BF)
-                att_ref[:, shift + HD * h : shift + HD * (h + 1)] = dot_f(weights, value).astype(BF)
+            heads = [HD * (GROUP * k + g) for g in range(GROUP)]
+            queries = stacked([qk_ref[:, h : h + HD] for h in heads])
+            scores = jnp.where(allowed, dot_t(queries, keys) * HD ** (-0.5), NEG)
+            top = jnp.max(scores, axis=1, keepdims=True)
+            expo = jnp.exp(scores - top)
+            total = jnp.sum(expo, axis=1, keepdims=True)
+            logsum_ref[:, k : k + 1] = top + jnp.log(total)
+            weights = (expo / total).astype(BF)
+            attended = dot_f(weights, value).astype(BF)
+            for g, h in enumerate(heads):
+                att_ref[:, shift + h : shift + h + HD] = attended[count * g : count * (g + 1), :]
         hidden1 = rows + dot_t(att_ref[...], attn_o_ref[:, 256:])
         hidden1_ref[...] = hidden1
         normed2, _ = norm_rows(hidden1)
@@ -431,26 +437,24 @@
         count = rows_ref.shape[0]
         qk_width = turn_ref.shape[1]
         grad_att = dot_f(grad_h1b_ref[...], attn_o_ref[...]).astype(BF)
-        allowed = seg_ref[...] > 0.0
+        allowed = stacked([seg_ref[...]] * GROUP) > 0.0
         grads_ref[:count, qk_width:] = jnp.zeros((count, 384), BF)
         for k in range(KV):
             keys = qk_ref[:, D + HD * k : D + HD * (k + 1)]
             value = v_ref[:, HD * k : HD * (k + 1)]
-            value_grad = jnp.zeros((count, HD), F32)
-            key_grad = jnp.zeros((count, HD), F32)
-            for g in range(GROUP):
-                h = GROUP * k + g
-                queries = qk_ref[:, HD * h : HD * (h + 1)]
-                grad = grad_att[:, kv_width + HD * h : kv_width + HD * (h + 1)]
-                scores = jnp.where(allowed, dot_t(queries, keys) * HD ** (-0.5), NEG)
-                probs = jnp.exp(scores - logsum_ref[:, h : h + 1])
-                value_grad = value_grad + dot_0(probs.astype(BF), grad)
-                prob_grad = dot_t(grad, value)
-                delta = jnp.sum(probs * prob_grad, axis=1, keepdims=True)
-                score_grad = (probs * (prob_grad - delta) * HD ** (-0.5)).astype(BF)
-                turn_ref[:, HD * h : HD * (h + 1)] = dot_f(score_grad, keys)
-                key_grad = key_grad + dot_0(score_grad, queries)
-            turn_ref[:, D + HD * k : D + HD * (k + 1)] = key_grad
+            heads = [HD * (GROUP * k + g) for g in range(GROUP)]
+            queries = stacked([qk_ref[:, h : h + HD] for h in heads])
+            grad = stacked([grad_att[:, kv_width + h : kv_width + h + HD] for h in heads])
+            scores = jnp.where(allowed, dot_t(queries, keys) * HD ** (-0.5), NEG)
+            probs = jnp.exp(scores - logsum_ref[:, k : k + 1])
+            value_grad = dot_0(probs.astype(BF), grad)
+            prob_grad = dot_t(grad, value)
+            delta = jnp.sum(probs * prob_grad, axis=1, keepdims=True)
+            score_grad = (probs * (prob_grad - delta) * HD ** (-0.5)).astype(BF)
+            query_grad = dot_f(score_grad, keys)
+            for g, h in enumerate(heads):
+                turn_ref[:, h : h + HD] = query_grad[count * g : count * (g + 1), :]
+            turn_ref[:, D + HD * k : D + HD * (k + 1)] = dot_0(score_grad, queries)
             grads_ref[:count, qk_width + HD * k : qk_width + HD * (k + 1)] = value_grad.astype(BF)
         cosine = cos_ref[...]
         sine = sin_ref[...]
@@ -626,14 +630,14 @@
     half1 = jnp.stack([half1, x1]).reshape(wide // 2, half_ff)
     c0, c1, last = swap(half0, "sub", 1), swap(half1, "sub", 1), swap(third, "fsdp", 2)
     down = jnp.stack([down, down_x])
+    gate_up_a = jnp.stack([gate_up, near])
+    gate_up_xa = swap(gate_up_a, "fsdp", 1)
     rows_y = swap(rows, "sub", 2)
-    half0, half1, c0, c1, gate_up, near, third, last, down, rows_y = meet(
-        half0, half1, c0, c1, gate_up, near, third, last, down, rows_y
-    )
+    half0, half1, c0, c1, third, last, down, rows_y = meet(half0, half1, c0, c1, third, last, down, rows_y)
     rows_all = jnp.concatenate([rows, rows_y])
 
-    gate_up = jnp.stack([gate_up, near, third, last])
-    gate_up_x = swap(gate_up, "fsdp", 1)
+    gate_up_b = jnp.stack([third, last])
+    gate_up_xb = swap(gate_up_b, "fsdp", 1)
     down_near, down_third = swap(down, "fsdp", 2), swap(down, "fsdp", 4)
     by_fsdp = [(f % 2) * n_far * n_sub + (f // 2) * n_sub for f in range(n_fsdp)]
     my_place = jnp.stack([my_fsdp, my_c, my_sub])
@@ -644,7 +648,7 @@
             ((count, half_ff - 256), BF),
             ((count, half_ff), BF),
             ((count, 384), BF),
-            ((count, KV * GROUP), F32),
+            ((count * GROUP, KV), F32),
             (tall, F32),
             (tall, BF),
             ((2, wide), F32),
@@ -657,16 +661,19 @@
     att, qk, values, logsum, hidden1, input2, gains_p, attn_q, attn_o = forward
 
     in2_y = swap(input2, "sub", 2)
-    input2, in2_y, down_near, down_third = meet(input2, in2_y, down_near, down_third)
+    input2, in2_y, down_near, down_third, gate_up_xa, gate_up_xb = meet(
+        input2, in2_y, down_near, down_third, gate_up_xa, gate_up_xb
+    )
     down_last = swap(down_third, "fsdp", 2)
     in2_all = jnp.stack([input2, in2_y])
     in2_c = swap(in2_all, "sub", 1)
     rows_c = swap(rows_all, "sub", 1)
-    in2_c, gate_up_x, rows_c = meet(in2_c, gate_up_x, rows_c)
+    in2_c, rows_c = meet(in2_c, rows_c)
     att_y = swap(after(att, in2_c), "sub", 2)
     in2_all = jnp.stack([in2_all, in2_c]).reshape(4 * count, wide)
-    gate_w = jnp.stack([gate_up[:, 0], gate_up_x[:, 0]]).reshape(wide, quarter)
-    up_w = jnp.stack([gate_up[:, 1], gate_up_x[:, 1]]).reshape(wide, quarter)
+    gate_up_all = jnp.concatenate([gate_up_a, gate_up_b, gate_up_xa, gate_up_xb])
+    gate_w = gate_up_all[:, 0].reshape(wide, quarter)
+    up_w = gate_up_all[:, 1].reshape(wide, quarter)
     gate = mm(in2_all, gate_w)
     up = mm(in2_all, up_w)
     sigma = jax.nn.sigmoid(gate)
@@ -766,7 +773,7 @@
     mlp_c = swap(pick(mlp_own, 1 - my_c, 2), "sub", 1)
     attn_near, mlp_c = meet(attn_near, mlp_c)
     attn_held = add2(far_pair(attn_held, 0, 0), attn_near)
-    mlp_c = after(mlp_c, attn_held)
+    attn_held, mlp_c = meet(attn_held, mlp_c)
     mlp_own = side_by_side(pick(mlp_own, my_c, 2), mlp_c, my_c)
     mlp_y = swap(pick(mlp_own, 1 - my_y, 1), "sub", 2)
     attn_far = swap(attn_held[1], "fsdp", 4)

time: 202 us -> 199 us (0.985)
  starting transfers between devices: 45.1 us -> 49.9 us
  Pallas kernels: 27.4 us -> 23.4 us
  other arithmetic: 14.7 us -> 11.2 us
    ppermute x50 -> x51, starting transfers between devices: 45.1 us -> 49.9 us  [swap(): lax.ppermute(value, axis, [(i, i ^ bit) for i in range(lax.axis_size(axis...]
    pallas_call x4, Pallas kernels: 27.4 us -> 23.4 us  [run_kernel(): pl.pallas_call(kernel, out_shape=[jax.ShapeDtypeStruct(shape, kind) for s...]
    unnamed x56 -> x67, local copies, waits for them, and re-layouts: 4.01 us -> 4.41 us
    ppermute x50 -> x51, waiting for transfers between devices: 79.3 us -> 79.3 us  [swap(): lax.ppermute(value, axis, [(i, i ^ bit) for i in range(lax.axis_size(axis...]
  transfers between devices with their start and end apart: 50 -> 51, of which waited for: 22 -> 24; matrix products, arithmetic and copies ran while one was open for 19% -> 18% of each run, Pallas kernels for 14% -> 12%
where the time goes in v6:
time: 199 us
  waiting for transfers between devices  79.3 us (40%)
  starting transfers between devices  49.9 us (25%)
  Pallas kernels  23.4 us (12%)
  matrix products  17.7 us (9%)
  local copies, waits for them, and re-layouts  14.5 us (7%)
  other arithmetic  11.2 us (6%)
  between operations  2.94 us (1%)
    ppermute x51, waiting for transfers between devices, swap(): lax.ppermute(value, axis, [(i, i ^ bit) for i in range(lax.axis_size(axis...  79.3 us
    ppermute x51, starting transfers between devices, swap(): lax.ppermute(value, axis, [(i, i ^ bit) for i in range(lax.axis_size(axis...  49.9 us
    pallas_call x4, Pallas kernels, run_kernel(): pl.pallas_call(kernel, out_shape=[jax.ShapeDtypeStruct(shape, kind) for s...  23.4 us
    dot_general x5, matrix products, mm(): return jnp.dot(a, b, preferred_element_type=F32)  7.41 us
    dot_general x4, matrix products, mm_t(): lax.dot_general(a, b, (((1,), (1,)), ((), ())), preferred_element_type=F32)  4.55 us
    unnamed x67, local copies, waits for them, and re-layouts  4.41 us
  transfers between devices with their start and end apart: 51, of which 24 were waited for; matrix products, arithmetic and copies ran while one was open for 18% of the time, Pallas kernels for 12%

profile of v6, /device:TPU:0, one launch (start us, length us, event | category | flops | bytes accessed | tf_op | source)
XLA Modules:
  0.0 198.9 jit_solution(14870459087533834297)
XLA Ops:
  2.7 5.1 %collective-permute-start.2 = (bf16[32,2560]{1,0:T(8,128)(2,1)S(1)}, bf16[32,2560]{1,0:T(8,128)(2,1)S(1)}, u32[]{:S(2)}, u32[]{:S(2)}) collective-permute-start(bf16[32,2560]{1,0:T(8,128)(2,1)S(1)} %scatter.4), channel_id=1, source_target_pairs={{0,24},{4,28},{8,16},{12,20},{16,8},{20,12},{24,0},{28,4},{1,25},{... | collective-permute-start | bytes 491528 | tf_op jit(solution)/shard_map/ppermute | solution.py:260
  10.2 1.7 collective-permute-start.3
  18.3 1.6 fusion.14.rows_ref
  20.2 1.6 collective-permute-done.1
  24.5 1.5 collective-permute-start.7
  28.2 5.1 %collective-permute-done.8 = bf16[2,128,640]{2,1,0:T(8,128)(2,1)S(1)} collective-permute-done((bf16[2,128,640]{2,1,0:T(8,128)(2,1)S(1)}, bf16[2,128,640]{2,1,0:T(8,128)(2,1)S(1)}, u32[]{:S(2)}, u32[]{:S(2)}) %collective-permute-start.8) | collective-permute-done | bytes 327712 | tf_op jit(solution)/shard_map/ppermute | solution.py:260
  35.7 1.6 collective-permute-start.12
  37.9 2.6 %collective-permute-start.13 = (bf16[2,128,640]{2,1,0:T(8,128)(2,1)S(1)}, bf16[2,128,640]{2,1,0:T(8,128)(2,1)S(1)}, u32[]{:S(2)}, u32[]{:S(2)}) collective-permute-start(bf16[2,128,640]{2,1,0:T(8,128)(2,1)S(1)} %slice.159), channel_id=1, source_target_pairs={{0,16},{4,20},{8,24},{12,28},{16,0},{20,4},{24,8},{28,12},{1,17},{... | collective-permute-start | bytes 983048 | tf_op jit(solution)/shard_map/ppermute | solution.py:260
  41.1 2.3 %fusion.8.grad_out_ref = bf16[512,1024]{1,0:T(8,128)(2,1)} fusion(s32[1024]{0:T(1024)S(1)} %fusion.60, bf16[256,960]{0,1:T(8,128)(2,1)S(1)} %collective-permute-done.9, bf16[256,960]{0,1:T(8,128)(2,1)S(1)} %constant_dynamic-update-slice_fusion), kind=kOutput, calls=%fused_computation.13 | convolution fusion | flops 1010106368 | bytes 2035712 | tf_op jit(solution)/shard_map/dot_general | solution.py:291
  43.4 11.6 %collective-permute-done.10 = bf16[128,640]{1,0:T(8,128)(2,1)S(1)} collective-permute-done((bf16[128,640]{1,0:T(8,128)(2,1)S(1)}, bf16[128,640]{1,0:T(8,128)(2,1)S(1)}, u32[]{:S(2)}, u32[]{:S(2)}) %collective-permute-start.10) | collective-permute-done | bytes 163872 | tf_op jit(solution)/shard_map/ppermute | solution.py:260
  62.6 4.4 %collective-permute-done.17 = bf16[128,960]{1,0:T(8,128)(2,1)S(1)} collective-permute-done((bf16[128,960]{1,0:T(8,128)(2,1)S(1)}, bf16[128,960]{1,0:T(8,128)(2,1)S(1)}, u32[]{:S(2)}, u32[]{:S(2)}) %collective-permute-start.17) | collective-permute-done | bytes 245792 | tf_op jit(solution)/shard_map/ppermute | solution.py:260
  66.9 2.5 %collective-permute-done.16 = bf16[2,128,640]{2,1,0:T(8,128)(2,1)S(1)} collective-permute-done((bf16[2,128,640]{2,1,0:T(8,128)(2,1)}, bf16[2,128,640]{2,1,0:T(8,128)(2,1)S(1)}, u32[]{:S(2)}, u32[]{:S(2)}) %collective-permute-start.16) | collective-permute-done | bytes 327712 | tf_op jit(solution)/shard_map/ppermute | solution.py:260
  69.6 1.6 collective-permute-start.22
  71.2 2.7 %collective-permute-start.20 = (bf16[2,128,640]{2,1,0:T(8,128)(2,1)S(1)}, bf16[2,128,640]{2,1,0:T(8,128)(2,1)S(1)}, u32[]{:S(2)}, u32[]{:S(2)}) collective-permute-start(bf16[2,128,640]{2,1,0:T(8,128)(2,1)S(1)} %pad_maximum_fusion.13), channel_id=1, source_target_pairs={{0,16},{4,20},{8,24},{12,28},{16,0},{20,4},{24,8},{28,12},{1,17},{... | collective-permute-start | bytes 983048 | tf_op jit(solution)/shard_map/ppermute | solution.py:260
  74.5 6.9 %attn_forward.1 = (bf16[128,1024]{1,0:T(8,128)(2,1)}, bf16[128,1280]{1,0:T(8,128)(2,1)}, bf16[128,384]{1,0:T(8,128)(2,1)}, f32[384,5]{1,0:T(8,128)}, f32[128,102...) custom-call(s32[3]{0:T(128)} %pad_add_fusion.place_ref, ...), custom_call_target="tpu_custom_call" | custom-call | flops 1000 | bytes 1000 | tf_op jit(solution)/shard_map/attn_forward/pallas_call | solution.py:539
  82.9 5.5 %collective-permute-done.18 = bf16[128,1024]{1,0:T(8,128)(2,1)S(1)} collective-permute-done((bf16[128,1024]{1,0:T(8,128)(2,1)}, bf16[128,1024]{1,0:T(8,128)(2,1)S(1)}, u32[]{:S(2)}, u32[]{:S(2)}) %collective-permute-start.18) | collective-permute-done | bytes 262176 | tf_op jit(solution)/shard_map/ppermute | solution.py:260
  89.2 2.6 %collective-permute-done.22 = bf16[2,2,128,640]{3,2,1,0:T(8,128)(2,1)S(1)} collective-permute-done((bf16[2,2,128,640]{3,2,1,0:T(8,128)(2,1)S(1)}, bf16[2,2,128,640]{3,2,1,0:T(8,128)(2,1)S(1)}, u32[]{:S(2)}, u32[]{:S(2)}) %collective-permute-start.22) | collective-permute-done | bytes 655392 | tf_op jit(solution)/shard_map/ppermute | solution.py:260
  108.0 1.5 collective-permute-start.34
  113.7 3.3 %collective-permute-done.29 = bf16[2,2,128,640]{3,2,1,0:T(8,128)(2,1)S(1)} collective-permute-done((bf16[2,2,128,640]{3,2,1,0:T(8,128)(2,1)S(1)}, bf16[2,2,128,640]{3,2,1,0:T(8,128)(2,1)S(1)}, u32[]{:S(2)}, u32[]{:S(2)}) %collective-permute-start.29) | collective-permute-done | bytes 655392 | tf_op jit(solution)/shard_map/ppermute | solution.py:260
  117.2 3.2 %collective-permute-done.28.grad_b_ref = bf16[128,1024]{1,0:T(8,128)(2,1)S(1)} collective-permute-done((bf16[128,1024]{1,0:T(8,128)(2,1)S(1)}, bf16[128,1024]{1,0:T(8,128)(2,1)S(1)}, u32[]{:S(2)}, u32[]{:S(2)}) %collective-permute-start.28) | collective-permute-done | bytes 262176 | tf_op jit(solution)/shard_map/ppermute | solution.py:260
  120.4 2.7 %collective-permute-start.35 = (bf16[2,128,640]{2,1,0:T(8,128)(2,1)S(1)}, bf16[2,128,640]{2,1,0:T(8,128)(2,1)S(1)}, u32[]{:S(2)}, u32[]{:S(2)}) collective-permute-start(bf16[2,128,640]{2,1,0:T(8,128)(2,1)S(1)} %slice_bitcast_fusion.7), channel_id=1, source_target_pairs={{0,16},{4,20},{8,24},{12,28},{16,0},{20,4},{24,8},{28,12},{1,17},{... | collective-permute-start | bytes 983048 | tf_op jit(solution)/shard_map/ppermute | solution.py:260
  123.2 2.7 %norm_backward.1 = (f32[128,1024]{1,0:T(8,128)}, bf16[128,1024]{1,0:T(8,128)(2,1)}, f32[1,1024]{1,0:T(1,128)}) custom-call(s32[3]{0:T(128)} %pad_add_fusion.place_ref, bf16[128,1024]{1,0:T(8,128)(2,1)} %get-tuple-element.255.grad_a_ref, bf16[128,1024]{1,0:T(8,128)(2,1)} %copy-done.15, bf16[512,1024]{1,0:T(8,128)(2,1)} %fusion.8.grad_out_ref, ...), custom_call_target="tpu_custom_call" | custom-call | flops 1000 | bytes 1000 | tf_op jit(solution)/shard_map/norm_backward/pallas_call | solution.py:539
  127.3 8.5 %attn_backward.1 = (bf16[144,1664]{1,0:T(8,128)(2,1)}, f32[128,1024]{1,0:T(8,128)}) custom-call(s32[3]{0:T(128)} %pad_add_fusion.place_ref, f32[128,1024]{1,0:T(8,128)} %get-tuple-element.189.grad_h1_ref, bf16[128,1024]{1,0:T(8,128)(2,1)} %get-tuple-element.188.grad_h1b_ref.refs_4_, f32[1,1024]{1,0:T(1,128)} %get-tuple-element.190.gain2_ref, ...), custom_call_target="tpu_custom_call" | custom-call | flops 1000 | bytes 1000 | tf_op jit(solution)/shard_map/attn_backward/pallas_call | solution.py:539
  136.6 2.7 %collective-permute-done.33 = bf16[4,128,640]{2,1,0:T(8,128)(2,1)S(1)} collective-permute-done((bf16[4,128,640]{2,1,0:T(8,128)(2,1)S(1)}, bf16[4,128,640]{2,1,0:T(8,128)(2,1)S(1)}, u32[]{:S(2)}, u32[]{:S(2)}) %collective-permute-start.33) | collective-permute-done | bytes 655392 | tf_op jit(solution)/shard_map/ppermute | solution.py:260
  139.3 1.5 collective-permute-start.40
  143.3 6.2 %collective-permute-done.36.refs_9_ = bf16[144,1664]{1,0:T(8,128)(2,1)S(1)} collective-permute-done((bf16[144,1664]{1,0:T(8,128)(2,1)}, bf16[144,1664]{1,0:T(8,128)(2,1)S(1)}, u32[]{:S(2)}, u32[]{:S(2)}) %collective-permute-start.36) | collective-permute-done | bytes 479264 | tf_op jit(solution)/shard_map/ppermute | solution.py:260
  152.3 5.2 %attn_terms.1 = (bf16[128,2560]{1,0:T(8,128)(2,1)}, bf16[128,2560]{1,0:T(8,128)(2,1)}) custom-call(s32[3]{0:T(128)} %pad_add_fusion.place_ref, bf16[256,960]{1,0:T(8,128)(2,1)} %copy-done.2, bf16[256,960]{1,0:T(8,128)(2,1)} %copy-done.10, f32[2,1024]{1,0:T(2,128)} %get-tuple-element.168.gains_ref, bf16[128,1024]{1,0:T(8,128)(2,1)} %get-tuple-element.182.refs_0_, ...), custom_call_target="tpu_custom_call" | custom-call | flops 1000 | bytes 1000 | tf_op jit(solution)/shard_map/attn_terms/pallas_call | solution.py:539
  159.7 2.7 %collective-permute-start.44 = (bf16[2,128,640]{2,1,0:T(8,128)(2,1)S(1)}, bf16[2,128,640]{2,1,0:T(8,128)(2,1)S(1)}, u32[]{:S(2)}, u32[]{:S(2)}) collective-permute-start(bf16[2,128,640]{2,1,0:T(8,128)(2,1)S(1)} %slice_bitcast_fusion.6), channel_id=1, source_target_pairs={{0,16},{4,20},{8,24},{12,28},{16,0},{20,4},{24,8},{28,12},{1,17},{... | collective-permute-start | bytes 983048 | tf_op jit(solution)/shard_map/ppermute | solution.py:260
  165.3 2.7 %fusion.1 = f32[128,960]{0,1:T(8,128)} fusion(f32[128,1024]{1,0:T(8,128)S(1)} %copy-done.29, s32[1024]{0:T(1024)S(1)} %fusion.60), kind=kOutput, calls=%fused_computation.2 | convolution fusion | flops 1510932480 | bytes 1019904 | tf_op jit(solution)/shard_map/dot_general | solution.py:756
  167.9 9.0 %collective-permute-done.44 = bf16[2,128,640]{2,1,0:T(8,128)(2,1)S(1)} collective-permute-done((bf16[2,128,640]{2,1,0:T(8,128)(2,1)S(1)}, bf16[2,128,640]{2,1,0:T(8,128)(2,1)S(1)}, u32[]{:S(2)}, u32[]{:S(2)}) %collective-permute-start.44) | collective-permute-done | bytes 327712 | tf_op jit(solution)/shard_map/ppermute | solution.py:260
  179.6 7.3 %collective-permute-done.47 = bf16[2,32,2560]{2,1,0:T(8,128)(2,1)S(1)} collective-permute-done((bf16[2,32,2560]{2,1,0:T(8,128)(2,1)S(1)}, bf16[2,32,2560]{2,1,0:T(8,128)(2,1)S(1)}, u32[]{:S(2)}, u32[]{:S(2)}) %collective-permute-start.47) | collective-permute-done | bytes 327712 | tf_op jit(solution)/shard_map/ppermute | solution.py:260
  188.5 5.7 %collective-permute-done.50 = bf16[3,32,1280]{2,1,0:T(8,128)(2,1)S(1)} collective-permute-done((bf16[3,32,1280]{2,1,0:T(8,128)(2,1)S(1)}, bf16[3,32,1280]{2,1,0:T(8,128)(2,1)S(1)}, u32[]{:S(2)}, u32[]{:S(2)}) %collective-permute-start.50) | collective-permute-done | bytes 245792 | tf_op jit(solution)/shard_map/ppermute | solution.py:260
  (238 shorter events, 70.0 us)
Async XLA Ops:
  2.7 17.4 %collective-permute-start.2 = (bf16[32,2560]{1,0:T(8,128)(2,1)S(1)}, bf16[32,2560]{1,0:T(8,128)(2,1)S(1)}, u32[]{:S(2)}, u32[]{:S(2)}) collective-permute-start(bf16[32,2560]{1,0:T(8,128)(2,1)S(1)} %scatter.4), channel_id=1, source_target_pairs={{0,24},{4,28},{8,16},{12,20},{16,8},{20,12},{24,0},{28,4},{1,25},{... | collective-permute-start | bytes 491528 | tf_op jit(solution)/shard_map/ppermute | solution.py:260
  7.8 13.9 %collective-permute-start.1 = (bf16[32,2560]{1,0:T(8,128)(2,1)S(1)}, bf16[32,2560]{1,0:T(8,128)(2,1)S(1)}, u32[]{:S(2)}, u32[]{:S(2)}) collective-permute-start(bf16[32,2560]{1,0:T(8,128)(2,1)S(1)} %scatter.4), channel_id=1, source_target_pairs={{0,16},{4,20},{8,24},{12,28},{16,0},{20,4},{24,8},{28,12},{1,17},{... | collective-permute-start | bytes 491528 | tf_op jit(solution)/shard_map/ppermute | solution.py:260
  7.9 13.9 %collective-permute-start = (bf16[32,2560]{1,0:T(8,128)(2,1)S(1)}, bf16[32,2560]{1,0:T(8,128)(2,1)S(1)}, u32[]{:S(2)}, u32[]{:S(2)}) collective-permute-start(bf16[32,2560]{1,0:T(8,128)(2,1)S(1)} %scatter.4), channel_id=1, source_target_pairs={{0,8},{4,12},{8,0},{12,4},{16,24},{20,28},{24,16},{28,20},{1,9},{5... | collective-permute-start | bytes 491528 | tf_op jit(solution)/shard_map/ppermute | solution.py:260
  22.8 12.8 %collective-permute-start.9 = (bf16[256,960]{0,1:T(8,128)(2,1)S(1)}, bf16[256,960]{0,1:T(8,128)(2,1)S(1)}, u32[]{:S(2)}, u32[]{:S(2)}) collective-permute-start(bf16[256,960]{0,1:T(8,128)(2,1)S(1)} %constant_dynamic-update-slice_fusion), channel_id=1, source_target_pairs={{0,1},{1,0},{2,3},{3,2},{4,5},{5,4},{6,7},{7,6},{8,9},{9,8},{10,11... | collective-permute-start | bytes 1474568 | tf_op jit(solution)/shard_map/ppermute | solution.py:260
  23.1 10.2 %collective-permute-start.8 = (bf16[2,128,640]{2,1,0:T(8,128)(2,1)S(1)}, bf16[2,128,640]{2,1,0:T(8,128)(2,1)S(1)}, u32[]{:S(2)}, u32[]{:S(2)}) collective-permute-start(bf16[2,128,640]{2,1,0:T(8,128)(2,1)S(1)} %slice.159), channel_id=1, source_target_pairs={{0,8},{4,12},{8,0},{12,4},{16,24},{20,28},{24,16},{28,20},{1,9},{5... | collective-permute-start | bytes 983048 | tf_op jit(solution)/shard_map/ppermute | solution.py:260
  24.5 9.8 %collective-permute-start.7 = (bf16[4,32,1280]{2,1,0:T(8,128)(2,1)S(1)}, bf16[4,32,1280]{2,1,0:T(8,128)(2,1)S(1)}, u32[]{:S(2)}, u32[]{:S(2)}) collective-permute-start(bf16[4,32,1280]{2,1,0:T(8,128)(2,1)S(1)} %get-tuple-element.134), channel_id=1, source_target_pairs={{0,2},{1,3},{2,0},{3,1},{4,6},{5,7},{6,4},{7,5},{8,10},{9,11},{10,... | collective-permute-start | bytes 983048 | tf_op jit(solution)/shard_map/ppermute | solution.py:260
  35.7 19.3 %collective-permute-start.12 = (bf16[4,2,32,1280]{3,2,1,0:T(8,128)(2,1)S(1)}, bf16[4,2,32,1280]{3,2,1,0:T(8,128)(2,1)S(1)}, u32[]{:S(2)}, u32[]{:S(2)}) collective-permute-start(bf16[4,2,32,1280]{3,2,1,0:T(8,128)(2,1)S(1)} %pad_maximum_fusion.6), channel_id=1, source_target_pairs={{0,4},{4,0},{8,12},{12,8},{16,20},{20,16},{24,28},{28,24},{1,5},{5... | collective-permute-start | bytes 1966088 | tf_op jit(solution)/shard_map/ppermute | solution.py:260
  37.3 17.7 %collective-permute-start.11 = (bf16[2,4,32,1280]{3,2,1,0:T(8,128)(2,1)S(1)}, bf16[2,4,32,1280]{3,2,1,0:T(8,128)(2,1)S(1)}, u32[]{:S(2)}, u32[]{:S(2)}) collective-permute-start(bf16[2,4,32,1280]{3,2,1,0:T(8,128)(2,1)S(1)} %pad_maximum_fusion.5), channel_id=1, source_target_pairs={{0,2},{1,3},{2,0},{3,1},{4,6},{5,7},{6,4},{7,5},{8,10},{9,11},{10,... | collective-permute-start | bytes 1966088 | tf_op jit(solution)/shard_map/ppermute | solution.py:260
  37.9 17.1 %collective-permute-start.13 = (bf16[2,128,640]{2,1,0:T(8,128)(2,1)S(1)}, bf16[2,128,640]{2,1,0:T(8,128)(2,1)S(1)}, u32[]{:S(2)}, u32[]{:S(2)}) collective-permute-start(bf16[2,128,640]{2,1,0:T(8,128)(2,1)S(1)} %slice.159), channel_id=1, source_target_pairs={{0,16},{4,20},{8,24},{12,28},{16,0},{20,4},{24,8},{28,12},{1,17},{... | collective-permute-start | bytes 983048 | tf_op jit(solution)/shard_map/ppermute | solution.py:260
  40.5 14.4 %collective-permute-start.10 = (bf16[128,640]{1,0:T(8,128)(2,1)S(1)}, bf16[128,640]{1,0:T(8,128)(2,1)S(1)}, u32[]{:S(2)}, u32[]{:S(2)}) collective-permute-start(bf16[128,640]{1,0:T(8,128)(2,1)S(1)} %slice_bitcast_fusion.10), channel_id=1, source_target_pairs={{0,4},{4,0},{8,12},{12,8},{16,20},{20,16},{24,28},{28,24},{1,5},{5... | collective-permute-start | bytes 491528 | tf_op jit(solution)/shard_map/ppermute | solution.py:260
  56.1 13.3 %collective-permute-start.15 = (bf16[512,1280]{1,0:T(8,128)(2,1)S(1)}, bf16[512,1280]{1,0:T(8,128)(2,1)}, u32[]{:S(2)}, u32[]{:S(2)}) collective-permute-start(bf16[512,1280]{1,0:T(8,128)(2,1)S(1)} %bitcast.190), channel_id=1, source_target_pairs={{0,1},{1,0},{2,3},{3,2},{4,5},{5,4},{6,7},{7,6},{8,9},{9,8},{10,11... | collective-permute-start | bytes 3932168 | tf_op jit(solution)/shard_map/ppermute | solution.py:260
  57.0 12.4 %collective-permute-start.14 = (bf16[512,1280]{1,0:T(8,128)(2,1)S(1)}, bf16[512,1280]{1,0:T(8,128)(2,1)}, u32[]{:S(2)}, u32[]{:S(2)}) collective-permute-start(bf16[512,1280]{1,0:T(8,128)(2,1)S(1)} %bitcast.188), channel_id=1, source_target_pairs={{0,1},{1,0},{2,3},{3,2},{4,5},{5,4},{6,7},{7,6},{8,9},{9,8},{10,11... | collective-permute-start | bytes 3932168 | tf_op jit(solution)/shard_map/ppermute | solution.py:260
  59.4 10.1 %collective-permute-start.16 = (bf16[2,128,640]{2,1,0:T(8,128)(2,1)}, bf16[2,128,640]{2,1,0:T(8,128)(2,1)S(1)}, u32[]{:S(2)}, u32[]{:S(2)}) collective-permute-start(bf16[2,128,640]{2,1,0:T(8,128)(2,1)} %copy-done.3), channel_id=1, source_target_pairs={{0,8},{4,12},{8,0},{12,4},{16,24},{20,28},{24,16},{28,20},{1,9},{5... | collective-permute-start | bytes 983048 | tf_op jit(solution)/shard_map/ppermute | solution.py:260
  61.0 21.9 %collective-permute-start.21 = (bf16[2,2,128,640]{3,2,1,0:T(8,128)(2,1)}, bf16[2,2,128,640]{3,2,1,0:T(8,128)(2,1)S(1)}, u32[]{:S(2)}, u32[]{:S(2)}) collective-permute-start(bf16[2,2,128,640]{3,2,1,0:T(8,128)(2,1)} %pad_maximum_fusion.7), channel_id=1, source_target_pairs={{0,4},{4,0},{8,12},{12,8},{16,20},{20,16},{24,28},{28,24},{1,5},{5... | collective-permute-start | bytes 1966088 | tf_op jit(solution)/shard_map/ppermute | solution.py:260
  69.6 22.3 %collective-permute-start.22 = (bf16[2,2,128,640]{3,2,1,0:T(8,128)(2,1)S(1)}, bf16[2,2,128,640]{3,2,1,0:T(8,128)(2,1)S(1)}, u32[]{:S(2)}, u32[]{:S(2)}) collective-permute-start(bf16[2,2,128,640]{3,2,1,0:T(8,128)(2,1)S(1)} %pad_maximum_fusion.8), channel_id=1, source_target_pairs={{0,4},{4,0},{8,12},{12,8},{16,20},{20,16},{24,28},{28,24},{1,5},{5... | collective-permute-start | bytes 1966088 | tf_op jit(solution)/shard_map/ppermute | solution.py:260
  71.2 17.2 %collective-permute-start.20 = (bf16[2,128,640]{2,1,0:T(8,128)(2,1)S(1)}, bf16[2,128,640]{2,1,0:T(8,128)(2,1)S(1)}, u32[]{:S(2)}, u32[]{:S(2)}) collective-permute-start(bf16[2,128,640]{2,1,0:T(8,128)(2,1)S(1)} %pad_maximum_fusion.13), channel_id=1, source_target_pairs={{0,16},{4,20},{8,24},{12,28},{16,0},{20,4},{24,8},{28,12},{1,17},{... | collective-permute-start | bytes 983048 | tf_op jit(solution)/shard_map/ppermute | solution.py:260
  73.9 15.3 %collective-permute-start.19 = (bf16[2,128,640]{2,1,0:T(8,128)(2,1)S(1)}, bf16[2,128,640]{2,1,0:T(8,128)(2,1)S(1)}, u32[]{:S(2)}, u32[]{:S(2)}) collective-permute-start(bf16[2,128,640]{2,1,0:T(8,128)(2,1)S(1)} %pad_maximum_fusion.13), channel_id=1, source_target_pairs={{0,8},{4,12},{8,0},{12,4},{16,24},{20,28},{24,16},{28,20},{1,9},{5... | collective-permute-start | bytes 983048 | tf_op jit(solution)/shard_map/ppermute | solution.py:260
  82.8 11.0 %collective-permute-start.24 = (bf16[256,960]{1,0:T(8,128)(2,1)S(1)}, bf16[256,960]{1,0:T(8,128)(2,1)S(1)}, u32[]{:S(2)}, u32[]{:S(2)}) collective-permute-start(bf16[256,960]{1,0:T(8,128)(2,1)S(1)} %pad_maximum_fusion.9.rows_a_ref), channel_id=1, source_target_pairs={{0,1},{1,0},{2,3},{3,2},{4,5},{5,4},{6,7},{7,6},{8,9},{9,8},{10,11... | collective-permute-start | bytes 1474568 | tf_op jit(solution)/shard_map/ppermute | solution.py:260
  88.4 28.8 %collective-permute-start.30 = (bf16[128,1024]{1,0:T(8,128)(2,1)S(1)}, bf16[128,1024]{1,0:T(8,128)(2,1)S(1)}, u32[]{:S(2)}, u32[]{:S(2)}) collective-permute-start(bf16[128,1024]{1,0:T(8,128)(2,1)S(1)} %copy-done.17), channel_id=1, source_target_pairs={{0,1},{1,0},{2,3},{3,2},{4,5},{5,4},{6,7},{7,6},{8,9},{9,8},{10,11... | collective-permute-start | bytes 786440 | tf_op jit(solution)/shard_map/ppermute | solution.py:260
  95.2 15.4 %collective-permute-start.27 = (bf16[128,1024]{1,0:T(8,128)(2,1)S(1)}, bf16[128,1024]{1,0:T(8,128)(2,1)S(1)}, u32[]{:S(2)}, u32[]{:S(2)}) collective-permute-start(bf16[128,1024]{1,0:T(8,128)(2,1)S(1)} %copy-done.17), channel_id=1, source_target_pairs={{0,2},{1,3},{2,0},{3,1},{4,6},{5,7},{6,4},{7,5},{8,10},{9,11},{10,... | collective-permute-start | bytes 786440 | tf_op jit(solution)/shard_map/ppermute | solution.py:260
  100.9 16.1 %collective-permute-start.29 = (bf16[2,2,128,640]{3,2,1,0:T(8,128)(2,1)S(1)}, bf16[2,2,128,640]{3,2,1,0:T(8,128)(2,1)S(1)}, u32[]{:S(2)}, u32[]{:S(2)}) collective-permute-start(bf16[2,2,128,640]{3,2,1,0:T(8,128)(2,1)S(1)} %slice_bitcast_fusion), channel_id=1, source_target_pairs={{0,8},{4,12},{8,0},{12,4},{16,24},{20,28},{24,16},{28,20},{1,9},{5... | collective-permute-start | bytes 1966088 | tf_op jit(solution)/shard_map/ppermute | solution.py:260
  108.0 27.9 %collective-permute-start.34 = (bf16[4,128,640]{2,1,0:T(8,128)(2,1)S(1)}, bf16[4,128,640]{2,1,0:T(8,128)(2,1)S(1)}, u32[]{:S(2)}, u32[]{:S(2)}) collective-permute-start(bf16[4,128,640]{2,1,0:T(8,128)(2,1)S(1)} %bitcast.219), channel_id=1, source_target_pairs={{0,4},{4,0},{8,12},{12,8},{16,20},{20,16},{24,28},{28,24},{1,5},{5... | collective-permute-start | bytes 1966088 | tf_op jit(solution)/shard_map/ppermute | solution.py:260
  110.7 28.5 %collective-permute-start.33 = (bf16[4,128,640]{2,1,0:T(8,128)(2,1)S(1)}, bf16[4,128,640]{2,1,0:T(8,128)(2,1)S(1)}, u32[]{:S(2)}, u32[]{:S(2)}) collective-permute-start(bf16[4,128,640]{2,1,0:T(8,128)(2,1)S(1)} %bitcast.220), channel_id=1, source_target_pairs={{0,4},{4,0},{8,12},{12,8},{16,20},{20,16},{24,28},{28,24},{1,5},{5... | collective-permute-start | bytes 1966088 | tf_op jit(solution)/shard_map/ppermute | solution.py:260
  120.4 18.8 %collective-permute-start.35 = (bf16[2,128,640]{2,1,0:T(8,128)(2,1)S(1)}, bf16[2,128,640]{2,1,0:T(8,128)(2,1)S(1)}, u32[]{:S(2)}, u32[]{:S(2)}) collective-permute-start(bf16[2,128,640]{2,1,0:T(8,128)(2,1)S(1)} %slice_bitcast_fusion.7), channel_id=1, source_target_pairs={{0,16},{4,20},{8,24},{12,28},{16,0},{20,4},{24,8},{28,12},{1,17},{... | collective-permute-start | bytes 983048 | tf_op jit(solution)/shard_map/ppermute | solution.py:260
  125.9 13.3 %collective-permute-start.32 = (bf16[128,1024]{1,0:T(8,128)(2,1)}, bf16[128,1024]{1,0:T(8,128)(2,1)}, u32[]{:S(2)}, u32[]{:S(2)}) collective-permute-start(bf16[128,1024]{1,0:T(8,128)(2,1)} %get-tuple-element.188.grad_h1b_ref.refs_4_), channel_id=1, source_target_pairs={{0,2},{1,3},{2,0},{3,1},{4,6},{5,7},{6,4},{7,5},{8,10},{9,11},{10,... | collective-permute-start | bytes 786440 | tf_op jit(solution)/shard_map/ppermute | solution.py:260
  127.3 15.4 %collective-permute-start.38 = (bf16[128,1024]{1,0:T(8,128)(2,1)}, bf16[128,1024]{1,0:T(8,128)(2,1)}, u32[]{:S(2)}, u32[]{:S(2)}) collective-permute-start(bf16[128,1024]{1,0:T(8,128)(2,1)} %get-tuple-element.188.grad_h1b_ref.refs_4_), channel_id=1, source_target_pairs={{0,1},{1,0},{2,3},{3,2},{4,5},{5,4},{6,7},{7,6},{8,9},{9,8},{10,11... | collective-permute-start | bytes 786440 | tf_op jit(solution)/shard_map/ppermute | solution.py:260
  135.9 13.7 %collective-permute-start.36 = (bf16[144,1664]{1,0:T(8,128)(2,1)}, bf16[144,1664]{1,0:T(8,128)(2,1)S(1)}, u32[]{:S(2)}, u32[]{:S(2)}) collective-permute-start(bf16[144,1664]{1,0:T(8,128)(2,1)} %get-tuple-element.199.refs_8_), channel_id=1, source_target_pairs={{0,2},{1,3},{2,0},{3,1},{4,6},{5,7},{6,4},{7,5},{8,10},{9,11},{10,... | collective-permute-start | bytes 1437704 | tf_op jit(solution)/shard_map/ppermute | solution.py:260
  139.3 10.2 %collective-permute-start.40 = (bf16[128,640]{1,0:T(8,128)(2,1)S(1)}, bf16[128,640]{1,0:T(8,128)(2,1)S(1)}, u32[]{:S(2)}, u32[]{:S(2)}) collective-permute-start(bf16[128,640]{1,0:T(8,128)(2,1)S(1)} %slice_bitcast_fusion.8), channel_id=1, source_target_pairs={{0,4},{4,0},{8,12},{12,8},{16,20},{20,16},{24,28},{28,24},{1,5},{5... | collective-permute-start | bytes 491528 | tf_op jit(solution)/shard_map/ppermute | solution.py:260
  142.7 16.9 %collective-permute-start.43 = (bf16[2,2,128,640]{3,2,1,0:T(8,128)(2,1)}, bf16[2,2,128,640]{3,2,1,0:T(8,128)(2,1)S(1)}, u32[]{:S(2)}, u32[]{:S(2)}) collective-permute-start(bf16[2,2,128,640]{3,2,1,0:T(8,128)(2,1)} %fusion.22), channel_id=1, source_target_pairs={{0,8},{4,12},{8,0},{12,4},{16,24},{20,28},{24,16},{28,20},{1,9},{5... | collective-permute-start | bytes 1966088 | tf_op jit(solution)/shard_map/ppermute | solution.py:260
  157.6 19.3 %collective-permute-start.42 = (bf16[128,2560]{1,0:T(8,128)(2,1)}, bf16[128,2560]{1,0:T(8,128)(2,1)S(1)}, u32[]{:S(2)}, u32[]{:S(2)}) collective-permute-start(bf16[128,2560]{1,0:T(8,128)(2,1)} %get-tuple-element.206), channel_id=1, source_target_pairs={{0,4},{4,0},{8,12},{12,8},{16,20},{20,16},{24,28},{28,24},{1,5},{5... | collective-permute-start | bytes 1966088 | tf_op jit(solution)/shard_map/ppermute | solution.py:260
  159.7 17.2 %collective-permute-start.44 = (bf16[2,128,640]{2,1,0:T(8,128)(2,1)S(1)}, bf16[2,128,640]{2,1,0:T(8,128)(2,1)S(1)}, u32[]{:S(2)}, u32[]{:S(2)}) collective-permute-start(bf16[2,128,640]{2,1,0:T(8,128)(2,1)S(1)} %slice_bitcast_fusion.6), channel_id=1, source_target_pairs={{0,16},{4,20},{8,24},{12,28},{16,0},{20,4},{24,8},{28,12},{1,17},{... | collective-permute-start | bytes 983048 | tf_op jit(solution)/shard_map/ppermute | solution.py:260
  163.7 13.2 %collective-permute-start.46 = (bf16[128,1024]{1,0:T(8,128)(2,1)S(1)}, bf16[128,1024]{1,0:T(8,128)(2,1)S(1)}, u32[]{:S(2)}, u32[]{:S(2)}) collective-permute-start(bf16[128,1024]{1,0:T(8,128)(2,1)S(1)} %slice.213), channel_id=1, source_target_pairs={{0,2},{1,3},{2,0},{3,1},{4,6},{5,7},{6,4},{7,5},{8,10},{9,11},{10,... | collective-permute-start | bytes 786440 | tf_op jit(solution)/shard_map/ppermute | solution.py:260
  (49 other events, 271.6 us)

commit v7 on v6

--- a/solution.py
+++ b/solution.py
@@ -483,7 +483,7 @@
 
 
 def make_terms(n_far, n_sub, own, padded, count):
-    def kernel(place_ref, rows_a_ref, rows_b_ref, gains_ref, *refs):
+    def kernel(place_ref, rows_a_ref, rows_b_ref, gains_ref, select_d_ref, *refs):
         att_refs = refs[:n_sub]
         grad_h1_refs = refs[n_sub : 2 * n_sub]
         grads_refs = refs[2 * n_sub : 3 * n_sub]
@@ -498,16 +498,11 @@
         spot = lax.broadcasted_iota(jnp.int32, (wide, rows), 1)
         source = (spot // padded * n_sub + place_ref[2]) * padded + spot % padded
         select = (lax.broadcasted_iota(jnp.int32, (wide, rows), 0) == source).astype(F32).astype(BF)
-        spot = lax.broadcasted_iota(jnp.int32, (D, rows), 1)
-        block = spot // padded
-        owner = ((block % n_far * 2 + block // n_far) ^ place_ref[0]) * n_sub + place_ref[2]
-        source = jnp.where(spot % padded < own, owner * own + spot % padded, -1)
-        select_d = (lax.broadcasted_iota(jnp.int32, (D, rows), 0) == source).astype(F32).astype(BF)
         rows_b = jnp.concatenate([rows_a_ref[...], rows_b_ref[...]], axis=0)
         group = rows_b.astype(F32)
         scale = lax.rsqrt(jnp.sum(group * group, axis=1, keepdims=True) * (1.0 / D) + EPS)
         gain = dot_f(gains_ref[...].astype(BF), select)[0:1, :]
-        left1 = (dot_f(rows_b, select_d) * scale * gain).astype(BF)
+        left1 = (dot_f(rows_b, select_d_ref[...]) * scale * gain).astype(BF)
         left2 = dot_f(tokens([ref[...] for ref in grad_h1_refs]), select).astype(BF)
         right = tokens([ref[:count, :] for ref in grads_refs])
         extra = tokens([ref[count:, :256] for ref in grads_refs])
@@ -588,6 +583,11 @@
     rows32 = mm(rows, spread_mat)
 
     owner = ((rel ^ my_fsdp) * n_sub + place % n_sub)[None, :]
+    spot = jnp.arange(wide // n_sub, dtype=jnp.int32)
+    block = spot // padded
+    target = ((block % n_far * 2 + block // n_far) ^ my_fsdp) * n_sub + my_sub
+    target = jnp.where(spot % padded < own, target * own + spot % padded, -1)
+    own_select = (jnp.arange(D, dtype=jnp.int32)[:, None] == target[None, :]).astype(BF)
 
     attn_block = padded_block(attn_weight)
     attn_block = attn_block.at[own, :share].set(gains)
@@ -613,8 +613,8 @@
     cot_c = swap(cot, "sub", 1)
     tables = (owner, inner[None, :])
     angles = (cosine, sine, seg)
-    half0, half1, gate_up, down, x0, y1, near, rows32, cot, cot_c, tables, angles = meet(
-        half0, half1, gate_up, down, x0, y1, near, rows32, cot, cot_c, tables, angles
+    half0, half1, gate_up, down, x0, y1, near, rows32, cot, cot_c, tables, angles, own_select = meet(
+        half0, half1, gate_up, down, x0, y1, near, rows32, cot, cot_c, tables, angles, own_select
     )
 
     half0 = jnp.stack([half0, x0])
@@ -741,7 +741,7 @@
         make_terms(n_far, n_sub, own, padded, count),
         [((n_far * padded, FF), BF)] * 2,
         (
-            my_place, rows_all, rows_c, gains_p, *atts, grad_h1b, grad_h1_y, grad_h1_c, grad_h1_yc, grads, grads_y, grads_c, grads_yc,
+            my_place, rows_all, rows_c, gains_p, own_select, *atts, grad_h1b, grad_h1_y, grad_h1_c, grad_h1_yc, grads, grads_y, grads_c, grads_yc,
         ),
         name="attn_terms",
     )

time: 199 us -> 199 us (level)
  transfers between devices with their start and end apart: 51 -> 51, of which waited for: 24 -> 23; matrix products, arithmetic and copies ran while one was open for 18% -> 19% of each run, Pallas kernels for 12% -> 12%
where the time goes in v7:
time: 199 us
  waiting for transfers between devices  78.1 us (39%)
  starting transfers between devices  49.8 us (25%)
  Pallas kernels  23.4 us (12%)
  matrix products  17.7 us (9%)
  local copies, waits for them, and re-layouts  14.7 us (7%)
  other arithmetic  12.1 us (6%)
  between operations  2.97 us (1%)
    ppermute x51, waiting for transfers between devices, swap(): lax.ppermute(value, axis, [(i, i ^ bit) for i in range(lax.axis_size(axis...  78.1 us
    ppermute x51, starting transfers between devices, swap(): lax.ppermute(value, axis, [(i, i ^ bit) for i in range(lax.axis_size(axis...  49.8 us
    pallas_call x4, Pallas kernels, run_kernel(): pl.pallas_call(kernel, out_shape=[jax.ShapeDtypeStruct(shape, kind) for s...  23.4 us
    dot_general x5, matrix products, mm(): return jnp.dot(a, b, preferred_element_type=F32)  7.39 us
    unnamed x67, local copies, waits for them, and re-layouts  4.6 us
    dot_general x4, matrix products, mm_t(): lax.dot_general(a, b, (((1,), (1,)), ((), ())), preferred_element_type=F32)  4.56 us
  transfers between devices with their start and end apart: 51, of which 23 were waited for; matrix products, arithmetic and copies ran while one was open for 19% of the time, Pallas kernels for 12%

profile of v7, /device:TPU:0, one launch (start us, length us, event | category | flops | bytes accessed | tf_op | source)
XLA Modules:
  0.0 198.9 jit_solution(10085599748081818832)
XLA Ops:
  2.7 5.1 %collective-permute-start.2 = (bf16[32,2560]{1,0:T(8,128)(2,1)S(1)}, bf16[32,2560]{1,0:T(8,128)(2,1)S(1)}, u32[]{:S(2)}, u32[]{:S(2)}) collective-permute-start(bf16[32,2560]{1,0:T(8,128)(2,1)S(1)} %scatter.4), channel_id=1, source_target_pairs={{0,24},{4,28},{8,16},{12,20},{16,8},{20,12},{24,0},{28,4},{1,25},{... | collective-permute-start | bytes 491528 | tf_op jit(solution)/shard_map/ppermute | solution.py:260
  10.2 1.7 collective-permute-start.3
  18.7 1.6 fusion.14.rows_ref
  24.5 1.5 collective-permute-start.7
  28.2 5.1 %collective-permute-done.8 = bf16[2,128,640]{2,1,0:T(8,128)(2,1)S(1)} collective-permute-done((bf16[2,128,640]{2,1,0:T(8,128)(2,1)S(1)}, bf16[2,128,640]{2,1,0:T(8,128)(2,1)S(1)}, u32[]{:S(2)}, u32[]{:S(2)}) %collective-permute-start.8) | collective-permute-done | bytes 327712 | tf_op jit(solution)/shard_map/ppermute | solution.py:260
  35.7 1.6 collective-permute-start.12
  37.9 2.6 %collective-permute-start.13 = (bf16[2,128,640]{2,1,0:T(8,128)(2,1)S(1)}, bf16[2,128,640]{2,1,0:T(8,128)(2,1)S(1)}, u32[]{:S(2)}, u32[]{:S(2)}) collective-permute-start(bf16[2,128,640]{2,1,0:T(8,128)(2,1)S(1)} %slice.159), channel_id=1, source_target_pairs={{0,16},{4,20},{8,24},{12,28},{16,0},{20,4},{24,8},{28,12},{1,17},{... | collective-permute-start | bytes 983048 | tf_op jit(solution)/shard_map/ppermute | solution.py:260
  41.1 2.3 %fusion.8.grad_out_ref = bf16[512,1024]{1,0:T(8,128)(2,1)} fusion(s32[1024]{0:T(1024)S(1)} %fusion.61, bf16[256,960]{0,1:T(8,128)(2,1)S(1)} %collective-permute-done.9, bf16[256,960]{0,1:T(8,128)(2,1)S(1)} %constant_dynamic-update-slice_fusion), kind=kOutput, calls=%fused_computation.13 | convolution fusion | flops 1010106368 | bytes 2035712 | tf_op jit(solution)/shard_map/dot_general | solution.py:291
  43.4 11.6 %collective-permute-done.10 = bf16[128,640]{1,0:T(8,128)(2,1)S(1)} collective-permute-done((bf16[128,640]{1,0:T(8,128)(2,1)S(1)}, bf16[128,640]{1,0:T(8,128)(2,1)S(1)}, u32[]{:S(2)}, u32[]{:S(2)}) %collective-permute-start.10) | collective-permute-done | bytes 163872 | tf_op jit(solution)/shard_map/ppermute | solution.py:260
  62.6 4.4 %collective-permute-done.17 = bf16[128,960]{1,0:T(8,128)(2,1)S(1)} collective-permute-done((bf16[128,960]{1,0:T(8,128)(2,1)S(1)}, bf16[128,960]{1,0:T(8,128)(2,1)S(1)}, u32[]{:S(2)}, u32[]{:S(2)}) %collective-permute-start.17) | collective-permute-done | bytes 245792 | tf_op jit(solution)/shard_map/ppermute | solution.py:260
  66.9 2.5 %collective-permute-done.16 = bf16[2,128,640]{2,1,0:T(8,128)(2,1)S(1)} collective-permute-done((bf16[2,128,640]{2,1,0:T(8,128)(2,1)}, bf16[2,128,640]{2,1,0:T(8,128)(2,1)S(1)}, u32[]{:S(2)}, u32[]{:S(2)}) %collective-permute-start.16) | collective-permute-done | bytes 327712 | tf_op jit(solution)/shard_map/ppermute | solution.py:260
  69.6 1.6 collective-permute-start.22
  71.2 2.7 %collective-permute-start.20 = (bf16[2,128,640]{2,1,0:T(8,128)(2,1)S(1)}, bf16[2,128,640]{2,1,0:T(8,128)(2,1)S(1)}, u32[]{:S(2)}, u32[]{:S(2)}) collective-permute-start(bf16[2,128,640]{2,1,0:T(8,128)(2,1)S(1)} %pad_maximum_fusion.13), channel_id=1, source_target_pairs={{0,16},{4,20},{8,24},{12,28},{16,0},{20,4},{24,8},{28,12},{1,17},{... | collective-permute-start | bytes 983048 | tf_op jit(solution)/shard_map/ppermute | solution.py:260
  74.5 6.9 %attn_forward.1 = (bf16[128,1024]{1,0:T(8,128)(2,1)}, bf16[128,1280]{1,0:T(8,128)(2,1)}, bf16[128,384]{1,0:T(8,128)(2,1)}, f32[384,5]{1,0:T(8,128)}, f32[128,102...) custom-call(s32[3]{0:T(128)} %pad_add_fusion.place_ref, ...), custom_call_target="tpu_custom_call" | custom-call | flops 1000 | bytes 1000 | tf_op jit(solution)/shard_map/attn_forward/pallas_call | solution.py:534
  82.9 5.5 %collective-permute-done.18 = bf16[128,1024]{1,0:T(8,128)(2,1)S(1)} collective-permute-done((bf16[128,1024]{1,0:T(8,128)(2,1)}, bf16[128,1024]{1,0:T(8,128)(2,1)S(1)}, u32[]{:S(2)}, u32[]{:S(2)}) %collective-permute-start.18) | collective-permute-done | bytes 262176 | tf_op jit(solution)/shard_map/ppermute | solution.py:260
  89.2 2.6 %collective-permute-done.22 = bf16[2,2,128,640]{3,2,1,0:T(8,128)(2,1)S(1)} collective-permute-done((bf16[2,2,128,640]{3,2,1,0:T(8,128)(2,1)S(1)}, bf16[2,2,128,640]{3,2,1,0:T(8,128)(2,1)S(1)}, u32[]{:S(2)}, u32[]{:S(2)}) %collective-permute-start.22) | collective-permute-done | bytes 655392 | tf_op jit(solution)/shard_map/ppermute | solution.py:260
  108.0 1.6 collective-permute-start.34
  113.7 3.5 %collective-permute-done.29 = bf16[2,2,128,640]{3,2,1,0:T(8,128)(2,1)S(1)} collective-permute-done((bf16[2,2,128,640]{3,2,1,0:T(8,128)(2,1)S(1)}, bf16[2,2,128,640]{3,2,1,0:T(8,128)(2,1)S(1)}, u32[]{:S(2)}, u32[]{:S(2)}) %collective-permute-start.29) | collective-permute-done | bytes 655392 | tf_op jit(solution)/shard_map/ppermute | solution.py:260
  117.4 3.0 %collective-permute-done.28.grad_b_ref = bf16[128,1024]{1,0:T(8,128)(2,1)S(1)} collective-permute-done((bf16[128,1024]{1,0:T(8,128)(2,1)S(1)}, bf16[128,1024]{1,0:T(8,128)(2,1)S(1)}, u32[]{:S(2)}, u32[]{:S(2)}) %collective-permute-start.28) | collective-permute-done | bytes 262176 | tf_op jit(solution)/shard_map/ppermute | solution.py:260
  120.4 2.7 %collective-permute-start.35 = (bf16[2,128,640]{2,1,0:T(8,128)(2,1)S(1)}, bf16[2,128,640]{2,1,0:T(8,128)(2,1)S(1)}, u32[]{:S(2)}, u32[]{:S(2)}) collective-permute-start(bf16[2,128,640]{2,1,0:T(8,128)(2,1)S(1)} %slice_bitcast_fusion.7), channel_id=1, source_target_pairs={{0,16},{4,20},{8,24},{12,28},{16,0},{20,4},{24,8},{28,12},{1,17},{... | collective-permute-start | bytes 983048 | tf_op jit(solution)/shard_map/ppermute | solution.py:260
  123.1 2.7 %norm_backward.1 = (f32[128,1024]{1,0:T(8,128)}, bf16[128,1024]{1,0:T(8,128)(2,1)}, f32[1,1024]{1,0:T(1,128)}) custom-call(s32[3]{0:T(128)} %pad_add_fusion.place_ref, bf16[128,1024]{1,0:T(8,128)(2,1)} %get-tuple-element.257.grad_a_ref, bf16[128,1024]{1,0:T(8,128)(2,1)} %copy-done.20, bf16[512,1024]{1,0:T(8,128)(2,1)} %fusion.8.grad_out_ref, ...), custom_call_target="tpu_custom_call" | custom-call | flops 1000 | bytes 1000 | tf_op jit(solution)/shard_map/norm_backward/pallas_call | solution.py:534
  127.3 8.6 %attn_backward.1 = (bf16[144,1664]{1,0:T(8,128)(2,1)}, f32[128,1024]{1,0:T(8,128)}) custom-call(s32[3]{0:T(128)} %pad_add_fusion.place_ref, f32[128,1024]{1,0:T(8,128)} %get-tuple-element.191.grad_h1_ref, bf16[128,1024]{1,0:T(8,128)(2,1)} %get-tuple-element.190.grad_h1b_ref.refs_4_, f32[1,1024]{1,0:T(1,128)} %get-tuple-element.192.gain2_ref, ...), custom_call_target="tpu_custom_call" | custom-call | flops 1000 | bytes 1000 | tf_op jit(solution)/shard_map/attn_backward/pallas_call | solution.py:534
  136.6 2.6 %collective-permute-done.33 = bf16[4,128,640]{2,1,0:T(8,128)(2,1)S(1)} collective-permute-done((bf16[4,128,640]{2,1,0:T(8,128)(2,1)S(1)}, bf16[4,128,640]{2,1,0:T(8,128)(2,1)S(1)}, u32[]{:S(2)}, u32[]{:S(2)}) %collective-permute-start.33) | collective-permute-done | bytes 655392 | tf_op jit(solution)/shard_map/ppermute | solution.py:260
  139.3 1.6 collective-permute-start.40
  143.3 6.2 %collective-permute-done.36.refs_9_ = bf16[144,1664]{1,0:T(8,128)(2,1)S(1)} collective-permute-done((bf16[144,1664]{1,0:T(8,128)(2,1)}, bf16[144,1664]{1,0:T(8,128)(2,1)S(1)}, u32[]{:S(2)}, u32[]{:S(2)}) %collective-permute-start.36) | collective-permute-done | bytes 479264 | tf_op jit(solution)/shard_map/ppermute | solution.py:260
  152.3 5.3 %attn_terms.1 = (bf16[128,2560]{1,0:T(8,128)(2,1)}, bf16[128,2560]{1,0:T(8,128)(2,1)}) custom-call(s32[3]{0:T(128)} %pad_add_fusion.place_ref, bf16[256,960]{1,0:T(8,128)(2,1)} %copy-done.2, bf16[256,960]{1,0:T(8,128)(2,1)} %copy-done.10, f32[2,1024]{1,0:T(2,128)} %get-tuple-element.169.gains_ref, bf16[960,256]{1,0:T(8,128)(2,1)} %fusion.20.select_d_ref, ...), custom_call_target="tpu_custom_call" | custom-call | flops 1000 | bytes 1000 | tf_op jit(solution)/shard_map/attn_terms/pallas_call | solution.py:534
  159.7 2.7 %collective-permute-start.44 = (bf16[2,128,640]{2,1,0:T(8,128)(2,1)S(1)}, bf16[2,128,640]{2,1,0:T(8,128)(2,1)S(1)}, u32[]{:S(2)}, u32[]{:S(2)}) collective-permute-start(bf16[2,128,640]{2,1,0:T(8,128)(2,1)S(1)} %slice_bitcast_fusion.6), channel_id=1, source_target_pairs={{0,16},{4,20},{8,24},{12,28},{16,0},{20,4},{24,8},{28,12},{1,17},{... | collective-permute-start | bytes 983048 | tf_op jit(solution)/shard_map/ppermute | solution.py:260
  165.3 2.7 %fusion.1 = f32[128,960]{0,1:T(8,128)} fusion(f32[128,1024]{1,0:T(8,128)S(1)} %copy-done.29, s32[1024]{0:T(1024)S(1)} %fusion.61), kind=kOutput, calls=%fused_computation.2 | convolution fusion | flops 1510932480 | bytes 1019904 | tf_op jit(solution)/shard_map/dot_general | solution.py:756
  167.9 9.1 %collective-permute-done.44 = bf16[2,128,640]{2,1,0:T(8,128)(2,1)S(1)} collective-permute-done((bf16[2,128,640]{2,1,0:T(8,128)(2,1)S(1)}, bf16[2,128,640]{2,1,0:T(8,128)(2,1)S(1)}, u32[]{:S(2)}, u32[]{:S(2)}) %collective-permute-start.44) | collective-permute-done | bytes 327712 | tf_op jit(solution)/shard_map/ppermute | solution.py:260
  178.2 1.5 fusion.15
  179.7 7.3 %collective-permute-done.47 = bf16[2,32,2560]{2,1,0:T(8,128)(2,1)S(1)} collective-permute-done((bf16[2,32,2560]{2,1,0:T(8,128)(2,1)S(1)}, bf16[2,32,2560]{2,1,0:T(8,128)(2,1)S(1)}, u32[]{:S(2)}, u32[]{:S(2)}) %collective-permute-start.47) | collective-permute-done | bytes 327712 | tf_op jit(solution)/shard_map/ppermute | solution.py:260
  188.5 5.8 %collective-permute-done.50 = bf16[3,32,1280]{2,1,0:T(8,128)(2,1)S(1)} collective-permute-done((bf16[3,32,1280]{2,1,0:T(8,128)(2,1)S(1)}, bf16[3,32,1280]{2,1,0:T(8,128)(2,1)S(1)}, u32[]{:S(2)}, u32[]{:S(2)}) %collective-permute-start.50) | collective-permute-done | bytes 245792 | tf_op jit(solution)/shard_map/ppermute | solution.py:260
  (240 shorter events, 69.7 us)
Async XLA Ops:
  2.7 17.8 %collective-permute-start.2 = (bf16[32,2560]{1,0:T(8,128)(2,1)S(1)}, bf16[32,2560]{1,0:T(8,128)(2,1)S(1)}, u32[]{:S(2)}, u32[]{:S(2)}) collective-permute-start(bf16[32,2560]{1,0:T(8,128)(2,1)S(1)} %scatter.4), channel_id=1, source_target_pairs={{0,24},{4,28},{8,16},{12,20},{16,8},{20,12},{24,0},{28,4},{1,25},{... | collective-permute-start | bytes 491528 | tf_op jit(solution)/shard_map/ppermute | solution.py:260
  7.8 13.9 %collective-permute-start.1 = (bf16[32,2560]{1,0:T(8,128)(2,1)S(1)}, bf16[32,2560]{1,0:T(8,128)(2,1)S(1)}, u32[]{:S(2)}, u32[]{:S(2)}) collective-permute-start(bf16[32,2560]{1,0:T(8,128)(2,1)S(1)} %scatter.4), channel_id=1, source_target_pairs={{0,16},{4,20},{8,24},{12,28},{16,0},{20,4},{24,8},{28,12},{1,17},{... | collective-permute-start | bytes 491528 | tf_op jit(solution)/shard_map/ppermute | solution.py:260
  7.9 13.9 %collective-permute-start = (bf16[32,2560]{1,0:T(8,128)(2,1)S(1)}, bf16[32,2560]{1,0:T(8,128)(2,1)S(1)}, u32[]{:S(2)}, u32[]{:S(2)}) collective-permute-start(bf16[32,2560]{1,0:T(8,128)(2,1)S(1)} %scatter.4), channel_id=1, source_target_pairs={{0,8},{4,12},{8,0},{12,4},{16,24},{20,28},{24,16},{28,20},{1,9},{5... | collective-permute-start | bytes 491528 | tf_op jit(solution)/shard_map/ppermute | solution.py:260
  22.8 12.8 %collective-permute-start.9 = (bf16[256,960]{0,1:T(8,128)(2,1)S(1)}, bf16[256,960]{0,1:T(8,128)(2,1)S(1)}, u32[]{:S(2)}, u32[]{:S(2)}) collective-permute-start(bf16[256,960]{0,1:T(8,128)(2,1)S(1)} %constant_dynamic-update-slice_fusion), channel_id=1, source_target_pairs={{0,1},{1,0},{2,3},{3,2},{4,5},{5,4},{6,7},{7,6},{8,9},{9,8},{10,11... | collective-permute-start | bytes 1474568 | tf_op jit(solution)/shard_map/ppermute | solution.py:260
  23.1 10.2 %collective-permute-start.8 = (bf16[2,128,640]{2,1,0:T(8,128)(2,1)S(1)}, bf16[2,128,640]{2,1,0:T(8,128)(2,1)S(1)}, u32[]{:S(2)}, u32[]{:S(2)}) collective-permute-start(bf16[2,128,640]{2,1,0:T(8,128)(2,1)S(1)} %slice.159), channel_id=1, source_target_pairs={{0,8},{4,12},{8,0},{12,4},{16,24},{20,28},{24,16},{28,20},{1,9},{5... | collective-permute-start | bytes 983048 | tf_op jit(solution)/shard_map/ppermute | solution.py:260
  24.5 9.8 %collective-permute-start.7 = (bf16[4,32,1280]{2,1,0:T(8,128)(2,1)S(1)}, bf16[4,32,1280]{2,1,0:T(8,128)(2,1)S(1)}, u32[]{:S(2)}, u32[]{:S(2)}) collective-permute-start(bf16[4,32,1280]{2,1,0:T(8,128)(2,1)S(1)} %get-tuple-element.135), channel_id=1, source_target_pairs={{0,2},{1,3},{2,0},{3,1},{4,6},{5,7},{6,4},{7,5},{8,10},{9,11},{10,... | collective-permute-start | bytes 983048 | tf_op jit(solution)/shard_map/ppermute | solution.py:260
  35.7 19.3 %collective-permute-start.12 = (bf16[4,2,32,1280]{3,2,1,0:T(8,128)(2,1)S(1)}, bf16[4,2,32,1280]{3,2,1,0:T(8,128)(2,1)S(1)}, u32[]{:S(2)}, u32[]{:S(2)}) collective-permute-start(bf16[4,2,32,1280]{3,2,1,0:T(8,128)(2,1)S(1)} %pad_maximum_fusion.6), channel_id=1, source_target_pairs={{0,4},{4,0},{8,12},{12,8},{16,20},{20,16},{24,28},{28,24},{1,5},{5... | collective-permute-start | bytes 1966088 | tf_op jit(solution)/shard_map/ppermute | solution.py:260
  37.3 17.7 %collective-permute-start.11 = (bf16[2,4,32,1280]{3,2,1,0:T(8,128)(2,1)S(1)}, bf16[2,4,32,1280]{3,2,1,0:T(8,128)(2,1)S(1)}, u32[]{:S(2)}, u32[]{:S(2)}) collective-permute-start(bf16[2,4,32,1280]{3,2,1,0:T(8,128)(2,1)S(1)} %pad_maximum_fusion.5), channel_id=1, source_target_pairs={{0,2},{1,3},{2,0},{3,1},{4,6},{5,7},{6,4},{7,5},{8,10},{9,11},{10,... | collective-permute-start | bytes 1966088 | tf_op jit(solution)/shard_map/ppermute | solution.py:260
  37.9 17.1 %collective-permute-start.13 = (bf16[2,128,640]{2,1,0:T(8,128)(2,1)S(1)}, bf16[2,128,640]{2,1,0:T(8,128)(2,1)S(1)}, u32[]{:S(2)}, u32[]{:S(2)}) collective-permute-start(bf16[2,128,640]{2,1,0:T(8,128)(2,1)S(1)} %slice.159), channel_id=1, source_target_pairs={{0,16},{4,20},{8,24},{12,28},{16,0},{20,4},{24,8},{28,12},{1,17},{... | collective-permute-start | bytes 983048 | tf_op jit(solution)/shard_map/ppermute | solution.py:260
  40.5 14.4 %collective-permute-start.10 = (bf16[128,640]{1,0:T(8,128)(2,1)S(1)}, bf16[128,640]{1,0:T(8,128)(2,1)S(1)}, u32[]{:S(2)}, u32[]{:S(2)}) collective-permute-start(bf16[128,640]{1,0:T(8,128)(2,1)S(1)} %slice_bitcast_fusion.10), channel_id=1, source_target_pairs={{0,4},{4,0},{8,12},{12,8},{16,20},{20,16},{24,28},{28,24},{1,5},{5... | collective-permute-start | bytes 491528 | tf_op jit(solution)/shard_map/ppermute | solution.py:260
  56.1 13.3 %collective-permute-start.15 = (bf16[512,1280]{1,0:T(8,128)(2,1)S(1)}, bf16[512,1280]{1,0:T(8,128)(2,1)}, u32[]{:S(2)}, u32[]{:S(2)}) collective-permute-start(bf16[512,1280]{1,0:T(8,128)(2,1)S(1)} %bitcast.190), channel_id=1, source_target_pairs={{0,1},{1,0},{2,3},{3,2},{4,5},{5,4},{6,7},{7,6},{8,9},{9,8},{10,11... | collective-permute-start | bytes 3932168 | tf_op jit(solution)/shard_map/ppermute | solution.py:260
  57.0 12.4 %collective-permute-start.14 = (bf16[512,1280]{1,0:T(8,128)(2,1)S(1)}, bf16[512,1280]{1,0:T(8,128)(2,1)}, u32[]{:S(2)}, u32[]{:S(2)}) collective-permute-start(bf16[512,1280]{1,0:T(8,128)(2,1)S(1)} %bitcast.188), channel_id=1, source_target_pairs={{0,1},{1,0},{2,3},{3,2},{4,5},{5,4},{6,7},{7,6},{8,9},{9,8},{10,11... | collective-permute-start | bytes 3932168 | tf_op jit(solution)/shard_map/ppermute | solution.py:260
  59.4 10.1 %collective-permute-start.16 = (bf16[2,128,640]{2,1,0:T(8,128)(2,1)}, bf16[2,128,640]{2,1,0:T(8,128)(2,1)S(1)}, u32[]{:S(2)}, u32[]{:S(2)}) collective-permute-start(bf16[2,128,640]{2,1,0:T(8,128)(2,1)} %copy-done.3), channel_id=1, source_target_pairs={{0,8},{4,12},{8,0},{12,4},{16,24},{20,28},{24,16},{28,20},{1,9},{5... | collective-permute-start | bytes 983048 | tf_op jit(solution)/shard_map/ppermute | solution.py:260
  61.0 21.9 %collective-permute-start.21 = (bf16[2,2,128,640]{3,2,1,0:T(8,128)(2,1)}, bf16[2,2,128,640]{3,2,1,0:T(8,128)(2,1)S(1)}, u32[]{:S(2)}, u32[]{:S(2)}) collective-permute-start(bf16[2,2,128,640]{3,2,1,0:T(8,128)(2,1)} %pad_maximum_fusion.7), channel_id=1, source_target_pairs={{0,4},{4,0},{8,12},{12,8},{16,20},{20,16},{24,28},{28,24},{1,5},{5... | collective-permute-start | bytes 1966088 | tf_op jit(solution)/shard_map/ppermute | solution.py:260
  69.6 22.3 %collective-permute-start.22 = (bf16[2,2,128,640]{3,2,1,0:T(8,128)(2,1)S(1)}, bf16[2,2,128,640]{3,2,1,0:T(8,128)(2,1)S(1)}, u32[]{:S(2)}, u32[]{:S(2)}) collective-permute-start(bf16[2,2,128,640]{3,2,1,0:T(8,128)(2,1)S(1)} %pad_maximum_fusion.8), channel_id=1, source_target_pairs={{0,4},{4,0},{8,12},{12,8},{16,20},{20,16},{24,28},{28,24},{1,5},{5... | collective-permute-start | bytes 1966088 | tf_op jit(solution)/shard_map/ppermute | solution.py:260
  71.2 17.2 %collective-permute-start.20 = (bf16[2,128,640]{2,1,0:T(8,128)(2,1)S(1)}, bf16[2,128,640]{2,1,0:T(8,128)(2,1)S(1)}, u32[]{:S(2)}, u32[]{:S(2)}) collective-permute-start(bf16[2,128,640]{2,1,0:T(8,128)(2,1)S(1)} %pad_maximum_fusion.13), channel_id=1, source_target_pairs={{0,16},{4,20},{8,24},{12,28},{16,0},{20,4},{24,8},{28,12},{1,17},{... | collective-permute-start | bytes 983048 | tf_op jit(solution)/shard_map/ppermute | solution.py:260
  73.9 15.3 %collective-permute-start.19 = (bf16[2,128,640]{2,1,0:T(8,128)(2,1)S(1)}, bf16[2,128,640]{2,1,0:T(8,128)(2,1)S(1)}, u32[]{:S(2)}, u32[]{:S(2)}) collective-permute-start(bf16[2,128,640]{2,1,0:T(8,128)(2,1)S(1)} %pad_maximum_fusion.13), channel_id=1, source_target_pairs={{0,8},{4,12},{8,0},{12,4},{16,24},{20,28},{24,16},{28,20},{1,9},{5... | collective-permute-start | bytes 983048 | tf_op jit(solution)/shard_map/ppermute | solution.py:260
  82.8 11.0 %collective-permute-start.24 = (bf16[256,960]{1,0:T(8,128)(2,1)S(1)}, bf16[256,960]{1,0:T(8,128)(2,1)S(1)}, u32[]{:S(2)}, u32[]{:S(2)}) collective-permute-start(bf16[256,960]{1,0:T(8,128)(2,1)S(1)} %pad_maximum_fusion.9.rows_a_ref), channel_id=1, source_target_pairs={{0,1},{1,0},{2,3},{3,2},{4,5},{5,4},{6,7},{7,6},{8,9},{9,8},{10,11... | collective-permute-start | bytes 1474568 | tf_op jit(solution)/shard_map/ppermute | solution.py:260
  88.4 29.0 %collective-permute-start.30 = (bf16[128,1024]{1,0:T(8,128)(2,1)S(1)}, bf16[128,1024]{1,0:T(8,128)(2,1)S(1)}, u32[]{:S(2)}, u32[]{:S(2)}) collective-permute-start(bf16[128,1024]{1,0:T(8,128)(2,1)S(1)} %copy-done.15), channel_id=1, source_target_pairs={{0,1},{1,0},{2,3},{3,2},{4,5},{5,4},{6,7},{7,6},{8,9},{9,8},{10,11... | collective-permute-start | bytes 786440 | tf_op jit(solution)/shard_map/ppermute | solution.py:260
  95.3 15.4 %collective-permute-start.27 = (bf16[128,1024]{1,0:T(8,128)(2,1)S(1)}, bf16[128,1024]{1,0:T(8,128)(2,1)S(1)}, u32[]{:S(2)}, u32[]{:S(2)}) collective-permute-start(bf16[128,1024]{1,0:T(8,128)(2,1)S(1)} %copy-done.15), channel_id=1, source_target_pairs={{0,2},{1,3},{2,0},{3,1},{4,6},{5,7},{6,4},{7,5},{8,10},{9,11},{10,... | collective-permute-start | bytes 786440 | tf_op jit(solution)/shard_map/ppermute | solution.py:260
  100.9 16.3 %collective-permute-start.29 = (bf16[2,2,128,640]{3,2,1,0:T(8,128)(2,1)S(1)}, bf16[2,2,128,640]{3,2,1,0:T(8,128)(2,1)S(1)}, u32[]{:S(2)}, u32[]{:S(2)}) collective-permute-start(bf16[2,2,128,640]{3,2,1,0:T(8,128)(2,1)S(1)} %slice_bitcast_fusion), channel_id=1, source_target_pairs={{0,8},{4,12},{8,0},{12,4},{16,24},{20,28},{24,16},{28,20},{1,9},{5... | collective-permute-start | bytes 1966088 | tf_op jit(solution)/shard_map/ppermute | solution.py:260
  108.0 27.9 %collective-permute-start.34 = (bf16[4,128,640]{2,1,0:T(8,128)(2,1)S(1)}, bf16[4,128,640]{2,1,0:T(8,128)(2,1)S(1)}, u32[]{:S(2)}, u32[]{:S(2)}) collective-permute-start(bf16[4,128,640]{2,1,0:T(8,128)(2,1)S(1)} %bitcast.219), channel_id=1, source_target_pairs={{0,4},{4,0},{8,12},{12,8},{16,20},{20,16},{24,28},{28,24},{1,5},{5... | collective-permute-start | bytes 1966088 | tf_op jit(solution)/shard_map/ppermute | solution.py:260
  110.7 28.5 %collective-permute-start.33 = (bf16[4,128,640]{2,1,0:T(8,128)(2,1)S(1)}, bf16[4,128,640]{2,1,0:T(8,128)(2,1)S(1)}, u32[]{:S(2)}, u32[]{:S(2)}) collective-permute-start(bf16[4,128,640]{2,1,0:T(8,128)(2,1)S(1)} %bitcast.220), channel_id=1, source_target_pairs={{0,4},{4,0},{8,12},{12,8},{16,20},{20,16},{24,28},{28,24},{1,5},{5... | collective-permute-start | bytes 1966088 | tf_op jit(solution)/shard_map/ppermute | solution.py:260
  120.4 18.8 %collective-permute-start.35 = (bf16[2,128,640]{2,1,0:T(8,128)(2,1)S(1)}, bf16[2,128,640]{2,1,0:T(8,128)(2,1)S(1)}, u32[]{:S(2)}, u32[]{:S(2)}) collective-permute-start(bf16[2,128,640]{2,1,0:T(8,128)(2,1)S(1)} %slice_bitcast_fusion.7), channel_id=1, source_target_pairs={{0,16},{4,20},{8,24},{12,28},{16,0},{20,4},{24,8},{28,12},{1,17},{... | collective-permute-start | bytes 983048 | tf_op jit(solution)/shard_map/ppermute | solution.py:260
  125.9 13.3 %collective-permute-start.32 = (bf16[128,1024]{1,0:T(8,128)(2,1)}, bf16[128,1024]{1,0:T(8,128)(2,1)}, u32[]{:S(2)}, u32[]{:S(2)}) collective-permute-start(bf16[128,1024]{1,0:T(8,128)(2,1)} %get-tuple-element.190.grad_h1b_ref.refs_4_), channel_id=1, source_target_pairs={{0,2},{1,3},{2,0},{3,1},{4,6},{5,7},{6,4},{7,5},{8,10},{9,11},{10,... | collective-permute-start | bytes 786440 | tf_op jit(solution)/shard_map/ppermute | solution.py:260
  127.3 15.4 %collective-permute-start.38 = (bf16[128,1024]{1,0:T(8,128)(2,1)}, bf16[128,1024]{1,0:T(8,128)(2,1)}, u32[]{:S(2)}, u32[]{:S(2)}) collective-permute-start(bf16[128,1024]{1,0:T(8,128)(2,1)} %get-tuple-element.190.grad_h1b_ref.refs_4_), channel_id=1, source_target_pairs={{0,1},{1,0},{2,3},{3,2},{4,5},{5,4},{6,7},{7,6},{8,9},{9,8},{10,11... | collective-permute-start | bytes 786440 | tf_op jit(solution)/shard_map/ppermute | solution.py:260
  135.9 13.7 %collective-permute-start.36 = (bf16[144,1664]{1,0:T(8,128)(2,1)}, bf16[144,1664]{1,0:T(8,128)(2,1)S(1)}, u32[]{:S(2)}, u32[]{:S(2)}) collective-permute-start(bf16[144,1664]{1,0:T(8,128)(2,1)} %get-tuple-element.201.refs_8_), channel_id=1, source_target_pairs={{0,2},{1,3},{2,0},{3,1},{4,6},{5,7},{6,4},{7,5},{8,10},{9,11},{10,... | collective-permute-start | bytes 1437704 | tf_op jit(solution)/shard_map/ppermute | solution.py:260
  139.3 10.2 %collective-permute-start.40 = (bf16[128,640]{1,0:T(8,128)(2,1)S(1)}, bf16[128,640]{1,0:T(8,128)(2,1)S(1)}, u32[]{:S(2)}, u32[]{:S(2)}) collective-permute-start(bf16[128,640]{1,0:T(8,128)(2,1)S(1)} %slice_bitcast_fusion.8), channel_id=1, source_target_pairs={{0,4},{4,0},{8,12},{12,8},{16,20},{20,16},{24,28},{28,24},{1,5},{5... | collective-permute-start | bytes 491528 | tf_op jit(solution)/shard_map/ppermute | solution.py:260
  142.7 16.9 %collective-permute-start.43 = (bf16[2,2,128,640]{3,2,1,0:T(8,128)(2,1)}, bf16[2,2,128,640]{3,2,1,0:T(8,128)(2,1)S(1)}, u32[]{:S(2)}, u32[]{:S(2)}) collective-permute-start(bf16[2,2,128,640]{3,2,1,0:T(8,128)(2,1)} %fusion.23), channel_id=1, source_target_pairs={{0,8},{4,12},{8,0},{12,4},{16,24},{20,28},{24,16},{28,20},{1,9},{5... | collective-permute-start | bytes 1966088 | tf_op jit(solution)/shard_map/ppermute | solution.py:260
  157.8 19.3 %collective-permute-start.42 = (bf16[128,2560]{1,0:T(8,128)(2,1)}, bf16[128,2560]{1,0:T(8,128)(2,1)S(1)}, u32[]{:S(2)}, u32[]{:S(2)}) collective-permute-start(bf16[128,2560]{1,0:T(8,128)(2,1)} %get-tuple-element.208), channel_id=1, source_target_pairs={{0,4},{4,0},{8,12},{12,8},{16,20},{20,16},{24,28},{28,24},{1,5},{5... | collective-permute-start | bytes 1966088 | tf_op jit(solution)/shard_map/ppermute | solution.py:260
  159.7 17.3 %collective-permute-start.44 = (bf16[2,128,640]{2,1,0:T(8,128)(2,1)S(1)}, bf16[2,128,640]{2,1,0:T(8,128)(2,1)S(1)}, u32[]{:S(2)}, u32[]{:S(2)}) collective-permute-start(bf16[2,128,640]{2,1,0:T(8,128)(2,1)S(1)} %slice_bitcast_fusion.6), channel_id=1, source_target_pairs={{0,16},{4,20},{8,24},{12,28},{16,0},{20,4},{24,8},{28,12},{1,17},{... | collective-permute-start | bytes 983048 | tf_op jit(solution)/shard_map/ppermute | solution.py:260
  163.7 13.3 %collective-permute-start.46 = (bf16[128,1024]{1,0:T(8,128)(2,1)S(1)}, bf16[128,1024]{1,0:T(8,128)(2,1)S(1)}, u32[]{:S(2)}, u32[]{:S(2)}) collective-permute-start(bf16[128,1024]{1,0:T(8,128)(2,1)S(1)} %slice.213), channel_id=1, source_target_pairs={{0,2},{1,3},{2,0},{3,1},{4,6},{5,7},{6,4},{7,5},{8,10},{9,11},{10,... | collective-permute-start | bytes 786440 | tf_op jit(solution)/shard_map/ppermute | solution.py:260
  (49 other events, 271.3 us)
